TPU v7x, 768 devices: a whole 4x8x12 slice. The times are simulated.
768 devices in a mesh: occ: 16 (over y, core), vir: 48 (over x, z).
Axes of the slice: x: 4, y: 8, z: 12, core: 2. Of those that a mesh axis runs over, the one named last changes fastest.
Arguments:
- amplitudes: bfloat16 [2, 192, 1152, 1152], P(None, 'occ', 'vir'), may hold values from -6 to 6
- integrals: bfloat16 [2, 1152, 1152], P(None, 'vir'), may hold values from -0.1875 to 0.1875
- block_mask: int32 [2, 6, 6], replicated, may hold values 0 or 1
- residual_in: float32 [192, 1152, 1152], P('occ', 'vir'), may hold values from -6 to 6
Outputs:
- residual_out: float32 [192, 1152, 1152], P('occ', 'vir')
All inputs are finite; a program needn't handle non-finite values.
Results may differ from a plain program's by a relative error of at most 0.0028.
Values may be sent and summed in bfloat16 or wider, within the bound.
No kernel may reach another device: no remote copies, remote signals or barrier semaphores. Data moves between devices by JAX's collectives and lax.ppermute only.
A program may use at most 128 MiB of HBM per device.

v0:
```python
import jax
import jax.numpy as jnp
from jax import lax
from jax.sharding import PartitionSpec as P

TILE = 192


def tile_mask(block_mask, row_count, col_count):
    tiles = block_mask.shape[1]
    tile_ids = jnp.arange(tiles, dtype=jnp.int32)
    row_tiles = jnp.arange(row_count, dtype=jnp.int32) // TILE
    col_tiles = jnp.arange(col_count, dtype=jnp.int32) // TILE
    row_hot = (row_tiles[:, None] == tile_ids[None, :]).astype(jnp.float32)
    col_hot = (col_tiles[:, None] == tile_ids[None, :]).astype(jnp.float32)
    return jnp.einsum("rt,kts,cs->krc", row_hot, block_mask.astype(jnp.float32), col_hot)


def per_device(amplitudes, integrals, block_mask, residual_in):
    swapped = lax.all_to_all(amplitudes, "vir", split_axis=3, concat_axis=2, tiled=True)
    combined = (
        2.0 * amplitudes.astype(jnp.float32) - jnp.swapaxes(swapped, 2, 3).astype(jnp.float32)
    ).astype(jnp.bfloat16)
    full_width = combined.shape[3]
    partial_value = lax.all_gather(integrals, "vir", axis=1, tiled=True)
    count = partial_value.shape[1]
    weights = (partial_value.astype(jnp.float32) * tile_mask(block_mask, count, full_width)).astype(
        jnp.bfloat16
    )
    return residual_in + jnp.einsum(
        "kiac,kcb->iab", combined, weights, preferred_element_type=jnp.float32
    )


def solution(mesh):
    return jax.shard_map(
        per_device,
        mesh=mesh,
        in_specs=(P(None, "occ", "vir", None), P(None, "vir", None), P(), P("occ", "vir", None)),
        out_specs=P("occ", "vir", None),
        check_vma=False,
    )
```

profile of v0, /device:TPU:6, one launch (start us, length us, event | category | flops | bytes accessed | tf_op | source)
XLA Modules:
  0.0 177.3 jit_solution(3489249706334422020)
XLA Ops:
  6.5 0.0 all-gather.2.cloned.1.call-start
  6.5 0.7 all-gather.2.cloned.1.call-update
  7.3 9.8 %copy.13 = bf16[2,12,24,1152]{2,1,0,3:T(8,128)(2,1)} copy(bf16[2,12,24,1152]{3,2,1,0:T(8,128)(2,1)} %param.4) | data formatting | bytes 2654208 | tf_op args[0]
  17.0 12.9 %reshape.22 = bf16[48,2,6912]{2,1,0:T(2,128)(2,1)} reshape(bf16[1152,2,12,24]{3,2,1,0:T(8,128)(2,1)} %bitcast.34) | data formatting | bytes 2654208
  29.9 0.0 copy-start
  29.9 18.7 %all-to-all-start = ((bf16[48,2,6912]{2,1,0:T(2,128)(2,1)}), bf16[48,2,6912]{2,1,0:T(2,128)(2,1)S(1)}, u32[]{:S(2)}, u32[]{:S(2)}) async-start(bf16[48,2,6912]{2,1,0:T(2,128)(2,1)} %reshape.22), calls=%async_computation | async-start | bytes 2654208 | tf_op jit(solution)/shard_map/all_to_all | solution.py:20
  48.6 0.0 copy-done
  48.7 0.2 convolution_bitcast_fusion.1
  48.9 54.1 %all-to-all-done = bf16[48,2,6912]{2,1,0:T(2,128)(2,1)S(1)} async-done(((bf16[48,2,6912]{2,1,0:T(2,128)(2,1)}), bf16[48,2,6912]{2,1,0:T(2,128)(2,1)S(1)}, u32[]{:S(2)}, u32[]{:S(2)}) %all-to-all-start) | async-done | bytes 1327136 | tf_op jit(solution)/shard_map/all_to_all | solution.py:20
  102.9 11.7 %reshape.23 = bf16[1152,2,12,24]{3,2,1,0:T(8,128)(2,1)} reshape(bf16[48,2,6912]{2,1,0:T(2,128)(2,1)S(1)} %all-to-all-done) | data formatting | bytes 2654208
  114.6 10.2 %copy.14 = bf16[2,12,24,1152]{3,2,1,0:T(8,128)(2,1)S(1)} copy(bf16[2,12,24,1152]{2,1,0,3:T(8,128)(2,1)} %bitcast.33) | data formatting | bytes 2654208 | tf_op jit(solution)/shard_map/all_to_all | solution.py:20
  124.8 10.6 %reshape.18 = f32[2,12,24,48,24]{4,3,2,1,0:T(8,128)} reshape(bf16[2,12,24,1152]{3,2,1,0:T(8,128)(2,1)S(1)} %copy.14) | data formatting | bytes 3981312 | tf_op jit(solution)/shard_map/convert_element_type | solution.py:22
  135.4 16.6 %copy.15 = f32[2,12,48,24,24]{3,2,4,1,0:T(8,128)} copy(f32[2,12,48,24,24]{4,2,3,1,0:T(8,128)} %bitcast.32) | data formatting | bytes 5308416 | tf_op jit(solution)/shard_map/convert_element_type | solution.py:22
  152.0 10.6 %reshape.17 = f32[2,12,1152,24]{2,3,1,0:T(8,128)S(1)} reshape(f32[2,12,48,24,24]{3,2,4,1,0:T(8,128)} %copy.15) | data formatting | bytes 5308416 | tf_op jit(solution)/shard_map/convert_element_type | solution.py:22
  162.6 0.0 all-gather.2.cloned.1.call-done
  162.7 7.8 %fusion.2 = f32[12,24,1152]{2,1,0:T(8,128)} fusion(f32[12,24,1152]{2,1,0:T(8,128)} %param.7, bf16[2,6,1152]{2,1,0:T(8,128)(2,1)S(1)} %convolution_bitcast_fusion.1, bf16[2,1152,1152]{2,1,0:T(8,128)(2,1)} %all-gather.2.cloned.1.call-done, f32[2,12,1152,24]{2,3,1,0:T(8,128)S(1)} %reshape.17, bf16[2,12,24,1152]{3,2,1,0:T(8,128)(2,1)} %param.4, ...), kind=kOutput, calls=%fused_computation.4 | convolution fusion | flops 1571629824 | bytes 11976192 | tf_op jit(solution)/shard_map/kiac,kcb->iab/dot_general | solution.py:30
  (2 shorter events, 0.0 us)
Async XLA Ops:
  6.5 156.1 %all-gather.2.cloned.1.call-start = ((), (), s32[]{:S(2)}) async-start(), calls=%async_computation.1 | async-start | bytes 5419008 | tf_op jit(solution)/shard_map/all_gather | solution.py:25
  29.9 18.7 %copy-start = (s32[2,6,6]{2,0,1:T(2,128)S(1)}, s32[2,6,6]{2,0,1:T(2,128)}, u32[]{:S(2)}) copy-start(s32[2,6,6]{2,0,1:T(2,128)} %param.6) | copy-start | bytes 868
  29.9 73.0 %all-to-all-start = ((bf16[48,2,6912]{2,1,0:T(2,128)(2,1)}), bf16[48,2,6912]{2,1,0:T(2,128)(2,1)S(1)}, u32[]{:S(2)}, u32[]{:S(2)}) async-start(bf16[48,2,6912]{2,1,0:T(2,128)(2,1)} %reshape.22), calls=%async_computation | async-start | bytes 2654208 | tf_op jit(solution)/shard_map/all_to_all | solution.py:20
Sparse Core Ops, SparseCore 0:
  11.0 147.0 all-gather.1
where the time goes:
time: 178 us; the launch traced here: 177 us
  local copies, waits for them, and re-layouts  82.4 us (46%)
  waiting for transfers between devices  54.8 us (31%)
  starting transfers between devices  18.7 us (11%)
  between operations  13.4 us (8%)
  matrix products  7.98 us (4%)
    all_to_all x1, waiting for transfers between devices, per_device(): lax.all_to_all(amplitudes, 'vir', split_axis=3, concat_axis=2, tiled=True)  54.1 us
    convert_element_type x3, local copies, waits for them, and re-layouts, per_device(): jnp.swapaxes(swapped, 2, 3).astype(jnp.float32)  37.8 us
    unnamed x5, local copies, waits for them, and re-layouts  34.4 us
    all_to_all x1, starting transfers between devices, per_device(): lax.all_to_all(amplitudes, 'vir', split_axis=3, concat_axis=2, tiled=True)  18.7 us
    all_to_all x1, local copies, waits for them, and re-layouts, per_device(): lax.all_to_all(amplitudes, 'vir', split_axis=3, concat_axis=2, tiled=True)  10.2 us
    dot_general x1, matrix products, per_device(): jnp.einsum('kiac,kcb->iab', combined, weights, preferred_element_type=jnp...  7.78 us
  transfers between devices with their start and end apart: 2, of which 1 were waited for; matrix products, arithmetic and copies ran while one was open for 47% of the time, Pallas kernels for 0%

commit v1 on v0

v1 whole, which is shorter than its diff:
```python
import jax
import jax.numpy as jnp
from jax import lax
from jax.experimental import pallas as pl
from jax.experimental.pallas import tpu as pltpu
from jax.sharding import PartitionSpec as P

TILE = 192
LANES = 128
NX, NZ = 4, 12


def pack_body(source, packed, wide):
    pairs, rows, width = source.shape
    peers, tiles = packed.shape[0], packed.shape[1]
    step = width // peers
    wide[...] = source[...].astype(jnp.float32)
    lane = lax.broadcasted_iota(jnp.int32, (rows, LANES), 1)
    for q in range(peers):
        tile, at = divmod(step * q, LANES)
        made = [None] * (tiles + 1)
        for g in range(pairs):
            piece = wide[g, :, tile * LANES : (tile + 1) * LANES]
            if at + step > LANES:
                piece = jnp.where(lane >= at, piece, wide[g, :, (tile + 1) * LANES : (tile + 2) * LANES])
            put, to = divmod(step * g, LANES)
            if to != at:
                piece = pltpu.roll(piece, (to - at) % LANES, 1)
            made[put] = piece if made[put] is None else jnp.where(lane >= to, piece, made[put])
            if to + step > LANES:
                made[put + 1] = piece
        for d in range(tiles):
            packed[q, d] = made[d].astype(jnp.bfloat16)


def pack(amplitudes, peers):
    pairs, rows, width = amplitudes.shape
    step = width // peers
    tiles = -(-pairs * step // LANES)
    blocks = width // 384
    return pl.pallas_call(
        pack_body,
        grid=(blocks,),
        in_specs=[pl.BlockSpec((pairs, rows, 384), lambda p: (0, 0, p))],
        out_specs=pl.BlockSpec((peers // blocks, tiles, rows, LANES), lambda p: (p, 0, 0, 0)),
        out_shape=jax.ShapeDtypeStruct((peers, tiles, rows, LANES), jnp.bfloat16),
        scratch_shapes=[pltpu.VMEM((pairs, rows, 384), jnp.float32)],
        compiler_params=pltpu.CompilerParams(vmem_limit_bytes=40 << 20),
        name="pack",
    )(amplitudes)


def final_body(where, mask, amplitudes, swapped, residual, *rest):
    pieces, out, combined, weights, mask_rows = rest[:-4], rest[-4], rest[-3], rest[-2], rest[-1]
    kept, rows = weights.shape[0], weights.shape[1]
    tiles = rows // TILE
    lane = lax.broadcasted_iota(jnp.int32, (16, rows), 1)
    for k in range(kept):
        for t in range(tiles):
            row = jnp.zeros((16, rows), jnp.float32)
            for u in range(tiles):
                inside = (lane >= u * TILE) & (lane < (u + 1) * TILE)
                row = jnp.where(inside, mask[(k * tiles + t) * tiles + u].astype(jnp.float32), row)
            mask_rows[k * tiles + t] = row.astype(jnp.bfloat16)
    core, mine = where[0], where[1]
    half = pieces[0].shape[0]
    own = half // 2
    spots = [(0, 0), (NX - 1, 0), (1, 0), (NX - 2, 0), (NX - 2, own)]
    for side in range(2):
        k = core if side == 0 else 1 - core
        for at, (shift, start) in enumerate(spots):
            piece = pieces[side * len(spots) + at]
            base = lax.rem(mine + shift, NX) * half + start
            for part in range(piece.shape[0] // 48):
                row = base + part * 48
                tile_row = mask_rows[k * tiles + row // TILE]
                for sub in range(3):
                    spot = part * 48 + sub * 16
                    weights[k, pl.ds(pl.multiple_of(base + spot, 16), 16), :] = piece[spot : spot + 16, :] * tile_row
    pairs = amplitudes.shape[0]
    for d in range(swapped.shape[1]):
        count = min(LANES, pairs - d * LANES)
        turned = jnp.transpose(swapped[:, d].reshape(rows, LANES).astype(jnp.float32))
        own_rows = amplitudes[d * LANES : d * LANES + count, :].astype(jnp.float32)
        combined[d * LANES : d * LANES + count, :] = (2.0 * own_rows - turned[:count]).astype(jnp.bfloat16)
    half_rows = pairs // kept
    out[...] = (
        residual[...]
        + jnp.dot(combined[:half_rows, :], weights[0], preferred_element_type=jnp.float32)
        + jnp.dot(combined[half_rows:, :], weights[1], preferred_element_type=jnp.float32)
    )


def per_device(amplitudes, integrals, block_mask, residual_in):
    kept, occ, rows, width = amplitudes.shape
    core = lax.rem(lax.axis_index("occ"), 2)
    column = lax.div(lax.axis_index("vir"), NZ)
    flat = amplitudes.reshape(kept * occ, rows, width)
    packed = pack(flat, width // rows)
    swapped = lax.all_to_all(packed, "vir", 0, 0, tiled=True)

    along = NX * NZ
    slab = jnp.where(core == 0, integrals[0], integrals[1])
    groups = [[x * NZ + z for z in range(NZ)] for x in range(NX)]
    here = lax.all_gather(slab, "vir", axis=0, tiled=True, axis_index_groups=groups)
    up = [(v, (v + NZ) % along) for v in range(along)]
    down = [(v, (v - NZ) % along) for v in range(along)]
    left = lax.ppermute(here, "vir", up)
    right = lax.ppermute(here, "vir", down)
    half = here.shape[0] // 2
    far_low = lax.ppermute(left[:half], "vir", up)
    far_high = lax.ppermute(right[half:], "vir", down)
    pieces = [here, left, right, far_low, far_high]
    swap_cores = [(j, j ^ 1) for j in range(16)]
    pieces += [lax.ppermute(piece, "occ", swap_cores) for piece in pieces]

    where = jnp.stack([core, column]).astype(jnp.int32)
    flat_rows = kept * occ * rows
    smem = pl.BlockSpec(memory_space=pltpu.SMEM)
    vmem = pl.BlockSpec(memory_space=pltpu.VMEM)
    out = pl.pallas_call(
        final_body,
        in_specs=[smem, smem] + [vmem] * (3 + len(pieces)),
        out_specs=vmem,
        out_shape=jax.ShapeDtypeStruct((occ * rows, width), jnp.float32),
        scratch_shapes=[
            pltpu.VMEM((flat_rows, width), jnp.bfloat16),
            pltpu.VMEM((kept, width, width), jnp.bfloat16),
            pltpu.VMEM((kept * (width // TILE), 16, width), jnp.bfloat16),
        ],
        compiler_params=pltpu.CompilerParams(vmem_limit_bytes=56 << 20),
        name="final",
    )(
        where,
        block_mask.reshape(-1),
        amplitudes.reshape(flat_rows, width),
        swapped,
        residual_in.reshape(occ * rows, width),
        *pieces,
    )
    return out.reshape(residual_in.shape)


def solution(mesh):
    return jax.shard_map(
        per_device,
        mesh=mesh,
        in_specs=(P(None, "occ", "vir", None), P(None, "vir", None), P(), P("occ", "vir", None)),
        out_specs=P("occ", "vir", None),
        check_vma=False,
    )
```

time: 178 us -> 142 us (0.80)
  local copies, waits for them, and re-layouts: 82.4 us -> 3.15 us
  blocking collectives: 0 us -> 70.3 us
  waiting for transfers between devices: 54.8 us -> 15.2 us
  starting transfers between devices: 18.7 us -> 40.4 us
  between operations: 13.4 us -> 0.21 us
  Pallas kernels: 0 us -> 10.4 us
  matrix products: 7.98 us -> 0 us
    all_gather x0 -> x1, blocking collectives: none -> 70.3 us  [per_device(): lax.all_gather(slab, 'vir', axis=0, tiled=True, axis_index_groups=groups)]
    all_to_all x1, waiting for transfers between devices: 54.1 us -> 0.01 us  [per_device(): swapped = lax.all_to_all(packed, 'vir', 0, 0, tiled=True)]
    convert_element_type x3 -> x0, local copies, waits for them, and re-layouts: 37.8 us -> none  [per_device(): jnp.swapaxes(swapped, 2, 3).astype(jnp.float32)]
    unnamed x5 -> x15, local copies, waits for them, and re-layouts: 34.4 us -> 2.44 us
    ppermute x0 -> x9, starting transfers between devices: none -> 21.8 us  [the longest x5 10.1 us: per_device(): pieces += [lax.ppermute(piece, 'occ', swap_cores) for piece in pieces]]
    ppermute x0 -> x9, waiting for transfers between devices: none -> 15.2 us  [the longest x1 7.86 us: per_device(): far_high = lax.ppermute(right[half:], 'vir', down)]
    pallas_call x0 -> x2, Pallas kernels: none -> 10.4 us  [the longest x1 7.4 us: per_device(): pl.pallas_call(final_body, in_specs=[smem, smem] + [vmem] * (3 + len(piec...]
    all_to_all x1 -> x0, local copies, waits for them, and re-layouts: 10.2 us -> none  [per_device(): lax.all_to_all(amplitudes, 'vir', split_axis=3, concat_axis=2, tiled=True)]
  transfers between devices with their start and end apart: 2 -> 10, of which waited for: 1 -> 3; matrix products, arithmetic and copies ran while one was open for 47% -> 1% of each run, Pallas kernels for 0% -> 0%
where the time goes in v1:
time: 142 us; the launch traced here: 140 us
  blocking collectives  70.3 us (50%)
  starting transfers between devices  40.4 us (28%)
  waiting for transfers between devices  15.2 us (11%)
  Pallas kernels  10.4 us (7%)
  local copies, waits for them, and re-layouts  3.15 us (2%)
    all_gather x1, blocking collectives, per_device(): lax.all_gather(slab, 'vir', axis=0, tiled=True, axis_index_groups=groups)  70.3 us
    all_to_all x1, starting transfers between devices, per_device(): swapped = lax.all_to_all(packed, 'vir', 0, 0, tiled=True)  18.7 us
    ppermute x5, starting transfers between devices, per_device(): pieces += [lax.ppermute(piece, 'occ', swap_cores) for piece in pieces]  10.1 us
    ppermute x1, waiting for transfers between devices, per_device(): far_high = lax.ppermute(right[half:], 'vir', down)  7.86 us
    pallas_call x1, Pallas kernels, per_device(): pl.pallas_call(final_body, in_specs=[smem, smem] + [vmem] * (3 + len(piec...  7.4 us
    ppermute x1, waiting for transfers between devices, per_device(): left = lax.ppermute(here, 'vir', up)  6.67 us
    ppermute x1, starting transfers between devices, per_device(): right = lax.ppermute(here, 'vir', down)  3.71 us
    ppermute x1, starting transfers between devices, per_device(): far_high = lax.ppermute(right[half:], 'vir', down)  3.11 us
  transfers between devices with their start and end apart: 10, of which 3 were waited for; matrix products, arithmetic and copies ran while one was open for 1% of the time, Pallas kernels for 0%

profile of v1, /device:TPU:6, one launch (start us, length us, event | category | flops | bytes accessed | tf_op | source)
XLA Modules:
  0.0 140.3 jit_solution(7117289883863153307)
XLA Ops:
  0.0 0.0 copy-start
  0.0 1.3 copy-done
  1.3 3.0 %pack.1 = bf16[48,5,24,128]{3,2,1,0:T(8,128)(2,1)} custom-call(bf16[24,24,1152]{2,1,0:T(8,128)(2,1)S(1)} %bitcast.8), custom_call_target="tpu_custom_call" | custom-call | tf_op jit(solution)/shard_map/pack/pallas_call | solution.py:41
  4.3 0.0 copy-start.5
  4.3 18.7 %all-to-all-start = ((bf16[48,5,24,128]{3,2,1,0:T(8,128)(2,1)}), bf16[48,5,24,128]{3,2,1,0:T(8,128)(2,1)S(1)}, u32[]{:S(2)}, u32[]{:S(2)}) async-start(bf16[48,5,24,128]{3,2,1,0:T(8,128)(2,1)} %pack.1), calls=%async_computation | async-start | bytes 2949120 | tf_op jit(solution)/shard_map/all_to_all | solution.py:100
  23.0 0.0 copy-start.6
  23.0 0.0 copy-done.5
  23.1 70.3 %all-gather = bf16[1,288,1152]{2,1,0:T(8,128)(2,1)S(1)} all-gather(bf16[1,24,1152]{2,1,0:T(8,128)(2,1)S(1)} %slice_select_fusion), channel_id=2, replica_groups={{0,1,2,3,4,5,6,7,8,9,10,11},{12,13,14,15,16,17,18,19,20,21,22,23},{24,2..., dimensions={1}, use_global_device_ids=true | all-gather | bytes 718848 | tf_op jit(solution)/shard_map/all_gather | solution.py:105
  93.4 0.0 copy-start.2
  93.4 2.1 %collective-permute-start = (bf16[288,1152]{1,0:T(8,128)(2,1)S(1)}, bf16[288,1152]{1,0:T(8,128)(2,1)S(1)}, u32[]{:S(2)}, u32[]{:S(2)}) collective-permute-start(bf16[288,1152]{1,0:T(8,128)(2,1)S(1)} %bitcast.9), channel_id=1, source_target_pairs={{0,12},{1,13},{2,14},{3,15},{4,16},{5,17},{6,18},{7,19},{8,20},{9,... | collective-permute-start | bytes 1990664 | tf_op jit(solution)/shard_map/ppermute | solution.py:108
  95.5 3.7 %collective-permute-start.1 = (bf16[288,1152]{1,0:T(8,128)(2,1)S(1)}, bf16[288,1152]{1,0:T(8,128)(2,1)S(1)}, u32[]{:S(2)}, u32[]{:S(2)}) collective-permute-start(bf16[288,1152]{1,0:T(8,128)(2,1)S(1)} %bitcast.10), channel_id=1, source_target_pairs={{0,36},{1,37},{2,38},{3,39},{4,40},{5,41},{6,42},{7,43},{8,44},{9,... | collective-permute-start | bytes 1990664 | tf_op jit(solution)/shard_map/ppermute | solution.py:109
  99.2 1.9 %collective-permute-start.4 = (bf16[288,1152]{1,0:T(8,128)(2,1)S(1)}, bf16[288,1152]{1,0:T(8,128)(2,1)}, u32[]{:S(2)}, u32[]{:S(2)}) collective-permute-start(bf16[288,1152]{1,0:T(8,128)(2,1)S(1)} %bitcast.11), channel_id=1, source_target_pairs={{0,48},{48,0},{96,144},{144,96},{192,240},{240,192},{288,336},{336... | collective-permute-start | bytes 1990664 | tf_op jit(solution)/shard_map/ppermute | solution.py:115
  101.2 6.7 %collective-permute-done.rest_1_ = bf16[288,1152]{1,0:T(8,128)(2,1)S(1)} collective-permute-done((bf16[288,1152]{1,0:T(8,128)(2,1)S(1)}, bf16[288,1152]{1,0:T(8,128)(2,1)S(1)}, u32[]{:S(2)}, u32[]{:S(2)}) %collective-permute-start) | collective-permute-done | bytes 663584 | tf_op jit(solution)/shard_map/ppermute | solution.py:108
  107.8 0.0 copy-start.3
  107.9 2.7 %collective-permute-start.2 = (bf16[144,1152]{1,0:T(8,128)(2,1)S(1)}, bf16[144,1152]{1,0:T(8,128)(2,1)}, u32[]{:S(2)}, u32[]{:S(2)}) collective-permute-start(bf16[144,1152]{1,0:T(8,128)(2,1)S(1)} %slice.16), channel_id=1, source_target_pairs={{0,12},{1,13},{2,14},{3,15},{4,16},{5,17},{6,18},{7,19},{8,20},{9,... | collective-permute-start | bytes 995336 | tf_op jit(solution)/shard_map/ppermute | solution.py:111
  110.6 1.9 %collective-permute-start.5 = (bf16[288,1152]{1,0:T(8,128)(2,1)S(1)}, bf16[288,1152]{1,0:T(8,128)(2,1)}, u32[]{:S(2)}, u32[]{:S(2)}) collective-permute-start(bf16[288,1152]{1,0:T(8,128)(2,1)S(1)} %collective-permute-done.rest_1_), channel_id=1, source_target_pairs={{0,48},{48,0},{96,144},{144,96},{192,240},{240,192},{288,336},{336... | collective-permute-start | bytes 1990664 | tf_op jit(solution)/shard_map/ppermute | solution.py:115
  112.5 0.0 collective-permute-done.1.rest_2_
  112.6 0.0 copy-start.4
  112.6 2.4 %collective-permute-start.6 = (bf16[288,1152]{1,0:T(8,128)(2,1)S(1)}, bf16[288,1152]{1,0:T(8,128)(2,1)}, u32[]{:S(2)}, u32[]{:S(2)}) collective-permute-start(bf16[288,1152]{1,0:T(8,128)(2,1)S(1)} %collective-permute-done.1.rest_2_), channel_id=1, source_target_pairs={{0,48},{48,0},{96,144},{144,96},{192,240},{240,192},{288,336},{336... | collective-permute-start | bytes 1990664 | tf_op jit(solution)/shard_map/ppermute | solution.py:115
  115.0 3.1 %collective-permute-start.3 = (bf16[144,1152]{1,0:T(8,128)(2,1)S(1)}, bf16[144,1152]{1,0:T(8,128)(2,1)}, u32[]{:S(2)}, u32[]{:S(2)}) collective-permute-start(bf16[144,1152]{1,0:T(8,128)(2,1)S(1)} %slice.17), channel_id=1, source_target_pairs={{0,36},{1,37},{2,38},{3,39},{4,40},{5,41},{6,42},{7,43},{8,44},{9,... | collective-permute-start | bytes 995336 | tf_op jit(solution)/shard_map/ppermute | solution.py:112
  118.1 0.0 collective-permute-done.2.rest_3_
  118.1 1.9 %collective-permute-start.7 = (bf16[144,1152]{1,0:T(8,128)(2,1)}, bf16[144,1152]{1,0:T(8,128)(2,1)}, u32[]{:S(2)}, u32[]{:S(2)}) collective-permute-start(bf16[144,1152]{1,0:T(8,128)(2,1)} %collective-permute-done.2.rest_3_), channel_id=1, source_target_pairs={{0,48},{48,0},{96,144},{144,96},{192,240},{240,192},{288,336},{336... | collective-permute-start | bytes 995336 | tf_op jit(solution)/shard_map/ppermute | solution.py:115
  120.1 7.9 %collective-permute-done.3.rest_4_ = bf16[144,1152]{1,0:T(8,128)(2,1)} collective-permute-done((bf16[144,1152]{1,0:T(8,128)(2,1)S(1)}, bf16[144,1152]{1,0:T(8,128)(2,1)}, u32[]{:S(2)}, u32[]{:S(2)}) %collective-permute-start.3) | collective-permute-done | bytes 331808 | tf_op jit(solution)/shard_map/ppermute | solution.py:112
  127.9 1.9 %collective-permute-start.8 = (bf16[144,1152]{1,0:T(8,128)(2,1)}, bf16[144,1152]{1,0:T(8,128)(2,1)}, u32[]{:S(2)}, u32[]{:S(2)}) collective-permute-start(bf16[144,1152]{1,0:T(8,128)(2,1)} %collective-permute-done.3.rest_4_), channel_id=1, source_target_pairs={{0,48},{48,0},{96,144},{144,96},{192,240},{240,192},{288,336},{336... | collective-permute-start | bytes 995336 | tf_op jit(solution)/shard_map/ppermute | solution.py:115
  129.9 0.0 copy-done.6
  129.9 0.7 reshape.17.mask
  130.5 0.6 pad_add_fusion.where
  131.2 0.0 collective-permute-done.4.rest_5_
  131.2 0.0 collective-permute-done.5.rest_6_
  131.2 0.0 collective-permute-done.6.rest_7_
  131.2 0.0 collective-permute-done.7.rest_8_
  131.2 0.6 collective-permute-done.8.rest_9_
  131.8 0.0 all-to-all-done.swapped
  131.8 0.0 copy-start.1
  131.8 0.0 copy-done.2
  131.8 0.0 copy-done.3
  131.8 0.0 copy-done.4
  131.8 1.1 copy-done.1
  132.9 7.4 %final.1 = f32[288,1152]{1,0:T(8,128)} custom-call(s32[2]{0:T(128)} %pad_add_fusion.where, s32[72]{0:T(128)} %reshape.17.mask, bf16[576,1152]{1,0:T(8,128)(2,1)} %bitcast.7, bf16[48,5,24,128]{3,2,1,0:T(8,128)(2,1)} %copy-done.1, f32[288,1152]{1,0:T(8,128)} %bitcast.13, bf16[288,1152]{1,0:T(8,128)(2,1)} %bitcast.12, bf16[288,1152]{1,0:T(8,128)(2,1)} %copy-done.3, ...), custom_call_target="tpu_custom_call" | custom-call | tf_op jit(solution)/shard_map/final/pallas_call | solution.py:121
  (4 shorter events, 0.1 us)
Async XLA Ops:
  0.0 1.3 copy-start
  4.3 18.7 %copy-start.5 = (bf16[2,24,1152]{2,1,0:T(8,128)(2,1)S(1)}, bf16[2,24,1152]{2,1,0:T(8,128)(2,1)}, u32[]{:S(2)}) copy-start(bf16[2,24,1152]{2,1,0:T(8,128)(2,1)} %param.5) | copy-start | bytes 331780
  4.3 127.5 %all-to-all-start = ((bf16[48,5,24,128]{3,2,1,0:T(8,128)(2,1)}), bf16[48,5,24,128]{3,2,1,0:T(8,128)(2,1)S(1)}, u32[]{:S(2)}, u32[]{:S(2)}) async-start(bf16[48,5,24,128]{3,2,1,0:T(8,128)(2,1)} %pack.1), calls=%async_computation | async-start | bytes 2949120 | tf_op jit(solution)/shard_map/all_to_all | solution.py:100
  23.0 106.9 %copy-start.6 = (s32[2,6,6]{2,0,1:T(2,128)S(1)}, s32[2,6,6]{2,0,1:T(2,128)}, u32[]{:S(2)}) copy-start(s32[2,6,6]{2,0,1:T(2,128)} %param.6) | copy-start | bytes 868
  93.4 38.4 %copy-start.2 = (bf16[1,288,1152]{2,1,0:T(8,128)(2,1)}, bf16[1,288,1152]{2,1,0:T(8,128)(2,1)S(1)}, u32[]{:S(2)}) copy-start(bf16[1,288,1152]{2,1,0:T(8,128)(2,1)S(1)} %all-gather) | copy-start | bytes 1990660
  93.4 14.4 %collective-permute-start = (bf16[288,1152]{1,0:T(8,128)(2,1)S(1)}, bf16[288,1152]{1,0:T(8,128)(2,1)S(1)}, u32[]{:S(2)}, u32[]{:S(2)}) collective-permute-start(bf16[288,1152]{1,0:T(8,128)(2,1)S(1)} %bitcast.9), channel_id=1, source_target_pairs={{0,12},{1,13},{2,14},{3,15},{4,16},{5,17},{6,18},{7,19},{8,20},{9,... | collective-permute-start | bytes 1990664 | tf_op jit(solution)/shard_map/ppermute | solution.py:108
  95.5 17.0 %collective-permute-start.1 = (bf16[288,1152]{1,0:T(8,128)(2,1)S(1)}, bf16[288,1152]{1,0:T(8,128)(2,1)S(1)}, u32[]{:S(2)}, u32[]{:S(2)}) collective-permute-start(bf16[288,1152]{1,0:T(8,128)(2,1)S(1)} %bitcast.10), channel_id=1, source_target_pairs={{0,36},{1,37},{2,38},{3,39},{4,40},{5,41},{6,42},{7,43},{8,44},{9,... | collective-permute-start | bytes 1990664 | tf_op jit(solution)/shard_map/ppermute | solution.py:109
  99.2 31.9 %collective-permute-start.4 = (bf16[288,1152]{1,0:T(8,128)(2,1)S(1)}, bf16[288,1152]{1,0:T(8,128)(2,1)}, u32[]{:S(2)}, u32[]{:S(2)}) collective-permute-start(bf16[288,1152]{1,0:T(8,128)(2,1)S(1)} %bitcast.11), channel_id=1, source_target_pairs={{0,48},{48,0},{96,144},{144,96},{192,240},{240,192},{288,336},{336... | collective-permute-start | bytes 1990664 | tf_op jit(solution)/shard_map/ppermute | solution.py:115
  107.8 24.0 %copy-start.3 = (bf16[288,1152]{1,0:T(8,128)(2,1)}, bf16[288,1152]{1,0:T(8,128)(2,1)S(1)}, u32[]{:S(2)}) copy-start(bf16[288,1152]{1,0:T(8,128)(2,1)S(1)} %collective-permute-done.rest_1_) | copy-start | bytes 1990660
  107.9 10.3 %collective-permute-start.2 = (bf16[144,1152]{1,0:T(8,128)(2,1)S(1)}, bf16[144,1152]{1,0:T(8,128)(2,1)}, u32[]{:S(2)}, u32[]{:S(2)}) collective-permute-start(bf16[144,1152]{1,0:T(8,128)(2,1)S(1)} %slice.16), channel_id=1, source_target_pairs={{0,12},{1,13},{2,14},{3,15},{4,16},{5,17},{6,18},{7,19},{8,20},{9,... | collective-permute-start | bytes 995336 | tf_op jit(solution)/shard_map/ppermute | solution.py:111
  110.6 20.6 %collective-permute-start.5 = (bf16[288,1152]{1,0:T(8,128)(2,1)S(1)}, bf16[288,1152]{1,0:T(8,128)(2,1)}, u32[]{:S(2)}, u32[]{:S(2)}) collective-permute-start(bf16[288,1152]{1,0:T(8,128)(2,1)S(1)} %collective-permute-done.rest_1_), channel_id=1, source_target_pairs={{0,48},{48,0},{96,144},{144,96},{192,240},{240,192},{288,336},{336... | collective-permute-start | bytes 1990664 | tf_op jit(solution)/shard_map/ppermute | solution.py:115
  112.6 19.3 %copy-start.4 = (bf16[288,1152]{1,0:T(8,128)(2,1)}, bf16[288,1152]{1,0:T(8,128)(2,1)S(1)}, u32[]{:S(2)}) copy-start(bf16[288,1152]{1,0:T(8,128)(2,1)S(1)} %collective-permute-done.1.rest_2_) | copy-start | bytes 1990660
  112.6 18.6 %collective-permute-start.6 = (bf16[288,1152]{1,0:T(8,128)(2,1)S(1)}, bf16[288,1152]{1,0:T(8,128)(2,1)}, u32[]{:S(2)}, u32[]{:S(2)}) collective-permute-start(bf16[288,1152]{1,0:T(8,128)(2,1)S(1)} %collective-permute-done.1.rest_2_), channel_id=1, source_target_pairs={{0,48},{48,0},{96,144},{144,96},{192,240},{240,192},{288,336},{336... | collective-permute-start | bytes 1990664 | tf_op jit(solution)/shard_map/ppermute | solution.py:115
  115.0 12.9 %collective-permute-start.3 = (bf16[144,1152]{1,0:T(8,128)(2,1)S(1)}, bf16[144,1152]{1,0:T(8,128)(2,1)}, u32[]{:S(2)}, u32[]{:S(2)}) collective-permute-start(bf16[144,1152]{1,0:T(8,128)(2,1)S(1)} %slice.17), channel_id=1, source_target_pairs={{0,36},{1,37},{2,38},{3,39},{4,40},{5,41},{6,42},{7,43},{8,44},{9,... | collective-permute-start | bytes 995336 | tf_op jit(solution)/shard_map/ppermute | solution.py:112
  118.1 13.0 %collective-permute-start.7 = (bf16[144,1152]{1,0:T(8,128)(2,1)}, bf16[144,1152]{1,0:T(8,128)(2,1)}, u32[]{:S(2)}, u32[]{:S(2)}) collective-permute-start(bf16[144,1152]{1,0:T(8,128)(2,1)} %collective-permute-done.2.rest_3_), channel_id=1, source_target_pairs={{0,48},{48,0},{96,144},{144,96},{192,240},{240,192},{288,336},{336... | collective-permute-start | bytes 995336 | tf_op jit(solution)/shard_map/ppermute | solution.py:115
  127.9 3.9 %collective-permute-start.8 = (bf16[144,1152]{1,0:T(8,128)(2,1)}, bf16[144,1152]{1,0:T(8,128)(2,1)}, u32[]{:S(2)}, u32[]{:S(2)}) collective-permute-start(bf16[144,1152]{1,0:T(8,128)(2,1)} %collective-permute-done.3.rest_4_), channel_id=1, source_target_pairs={{0,48},{48,0},{96,144},{144,96},{192,240},{240,192},{288,336},{336... | collective-permute-start | bytes 995336 | tf_op jit(solution)/shard_map/ppermute | solution.py:115
  131.8 1.1 copy-start.1

commit v2 on v1

v2 whole, which is shorter than its diff:
```python
import jax
import jax.numpy as jnp
from jax import lax
from jax.experimental import pallas as pl
from jax.experimental.pallas import tpu as pltpu
from jax.sharding import PartitionSpec as P

TILE = 192
LANES = 128
NX, NZ = 4, 12


def pack_body(source, packed, wide):
    pairs, rows, width = source.shape
    peers = packed.shape[0]
    step = width // peers
    full = pairs * step // LANES
    wide[...] = source[...].astype(jnp.float32)
    lane = lax.broadcasted_iota(jnp.int32, (rows, LANES), 1)
    for q in range(peers):
        tile, at = divmod(step * q, LANES)
        made = [None] * (full + 2)
        for g in range(pairs):
            piece = wide[g, :, tile * LANES : (tile + 1) * LANES]
            if at + step > LANES:
                piece = jnp.where(lane >= at, piece, wide[g, :, (tile + 1) * LANES : (tile + 2) * LANES])
            put, to = divmod(step * g, LANES)
            if to != at:
                piece = pltpu.roll(piece, (to - at) % LANES, 1)
            made[put] = piece if made[put] is None else jnp.where(lane >= to, piece, made[put])
            if to + step > LANES:
                made[put + 1] = piece
        for d in range(full):
            packed[q, d * rows : (d + 1) * rows] = made[d].astype(jnp.bfloat16)
        low, middle, high = (made[full][8 * j : 8 * j + 8] for j in range(3))
        low = jnp.where(lane[:8] < LANES // 2, low, pltpu.roll(middle, LANES // 2, 1))
        packed[q, full * rows :] = jnp.concatenate([low, high], axis=0).astype(jnp.bfloat16)


def pack(amplitudes, peers):
    pairs, rows, width = amplitudes.shape
    full = pairs * (width // peers) // LANES
    tall = full * rows + 16
    blocks = width // 384
    return pl.pallas_call(
        pack_body,
        grid=(blocks,),
        in_specs=[pl.BlockSpec((pairs, rows, 384), lambda p: (0, 0, p))],
        out_specs=pl.BlockSpec((peers // blocks, tall, LANES), lambda p: (p, 0, 0)),
        out_shape=jax.ShapeDtypeStruct((peers, tall, LANES), jnp.bfloat16),
        scratch_shapes=[pltpu.VMEM((pairs, rows, 384), jnp.float32)],
        compiler_params=pltpu.CompilerParams(vmem_limit_bytes=12 << 20),
        name="pack",
    )(amplitudes)


def final_body(where, mask, amplitudes, residual, swapped, *rest):
    pieces, (out, own, combined, weights, start, made, mask_rows, sems) = rest[:-8], rest[-8:]
    kept, width = weights.shape[0], weights.shape[1]
    tiles = width // TILE
    core, mine = where[0], where[1]
    half = pieces[0].shape[0]
    copies = [pltpu.make_async_copy(amplitudes, own, sems.at[0])]
    spots = [(0, 0), (NX - 1, 0), (1, 0), (NX - 2, 0), (NX - 2, half // 2)]
    for side in range(2):
        k = core if side == 0 else 1 - core
        for at, (shift, first) in enumerate(spots):
            piece = pieces[side * len(spots) + at]
            base = pl.multiple_of(lax.rem(mine + shift, NX) * half + first, 16)
            target = weights.at[k, pl.ds(base, piece.shape[0]), :]
            copies.append(pltpu.make_async_copy(piece, target, sems.at[len(copies)]))
    copies.append(pltpu.make_async_copy(residual, start, sems.at[len(copies)]))
    for copy in copies:
        copy.start()

    lane = lax.broadcasted_iota(jnp.int32, (16, width), 1)
    for k in range(kept):
        for t in range(tiles):
            row = jnp.zeros((16, width), jnp.float32)
            for u in range(tiles):
                inside = (lane >= u * TILE) & (lane < (u + 1) * TILE)
                row = jnp.where(inside, mask[(k * tiles + t) * tiles + u].astype(jnp.float32), row)
            mask_rows[k * tiles + t] = row.astype(jnp.bfloat16)

    copies[0].wait()
    pairs = own.shape[0]
    peers, tall = swapped.shape[0], swapped.shape[1]
    rows = width // peers
    full = tall // rows
    for d in range(full + 1):
        count = min(LANES, pairs - d * LANES)
        if d < full:
            tile = swapped[:, d * rows : (d + 1) * rows, :].astype(jnp.float32)
        else:
            ends = swapped[:, d * rows :, :].astype(jnp.float32)
            low = ends[:, :8].reshape(peers * 8, LANES)
            middle = pltpu.roll(low, LANES // 2, 1).reshape(peers, 8, LANES)
            tile = jnp.concatenate([ends[:, :8], middle, ends[:, 8:]], axis=1)
        turned = jnp.transpose(tile.reshape(width, LANES))
        own_rows = own[d * LANES : d * LANES + count, :].astype(jnp.float32)
        combined[d * LANES : d * LANES + count, :] = (2.0 * own_rows - turned[:count]).astype(jnp.bfloat16)

    for copy in copies[1:]:
        copy.wait()
    half_rows = pairs // kept
    wide = 384
    stores = []
    for n in range(width // wide):
        cols = slice(n * wide, (n + 1) * wide)
        total = start[:, cols]
        for k in range(kept):
            masked = jnp.concatenate(
                [
                    (weights[k, t * TILE : (t + 1) * TILE, cols].reshape(-1, 16, wide) * mask_rows[k * tiles + t, :, cols][None])
                    for t in range(tiles)
                ]
            ).reshape(width, wide)
            total += jnp.dot(
                combined[k * half_rows : (k + 1) * half_rows, :], masked, preferred_element_type=jnp.float32
            )
        made[:, cols] = total
        stores.append(pltpu.make_async_copy(made.at[:, cols], out.at[:, cols], sems.at[len(copies) + n]))
        stores[-1].start()
    for store in stores:
        store.wait()


def final(where, mask, amplitudes, residual, swapped, pieces, kept):
    width = residual.shape[1]
    smem = pl.BlockSpec(memory_space=pltpu.SMEM)
    vmem = pl.BlockSpec(memory_space=pltpu.VMEM)
    hbm = pl.BlockSpec(memory_space=pltpu.HBM)
    return pl.pallas_call(
        final_body,
        in_specs=[smem, smem, hbm, hbm, vmem] + [hbm] * len(pieces),
        out_specs=hbm,
        out_shape=jax.ShapeDtypeStruct(residual.shape, jnp.float32),
        scratch_shapes=[
            pltpu.VMEM(amplitudes.shape, jnp.bfloat16),
            pltpu.VMEM(amplitudes.shape, jnp.bfloat16),
            pltpu.VMEM((kept, width, width), jnp.bfloat16),
            pltpu.VMEM(residual.shape, jnp.float32),
            pltpu.VMEM(residual.shape, jnp.float32),
            pltpu.VMEM((kept * (width // TILE), 16, width), jnp.bfloat16),
            pltpu.SemaphoreType.DMA((len(pieces) + 2 + width // 384,)),
        ],
        compiler_params=pltpu.CompilerParams(vmem_limit_bytes=24 << 20),
        name="final",
    )(where, mask, amplitudes, residual, swapped, *pieces)


def per_device(amplitudes, integrals, block_mask, residual_in):
    kept, occ, rows, width = amplitudes.shape
    core = lax.rem(lax.axis_index("occ"), 2)
    column = lax.div(lax.axis_index("vir"), NZ)
    where = jnp.stack([core, column]).astype(jnp.int32)

    along = NX * NZ
    slab = jnp.where(core == 0, integrals[0], integrals[1])
    groups = [[x * NZ + z for z in range(NZ)] for x in range(NX)]
    here = lax.all_gather(slab, "vir", axis=0, tiled=True, axis_index_groups=groups)

    flat, here = lax.optimization_barrier((amplitudes.reshape(kept * occ, rows, width), here))
    packed = pack(pltpu.with_memory_space_constraint(flat, pltpu.HBM), width // rows)
    swapped = lax.all_to_all(packed, "vir", 0, 0, tiled=True)

    up = [(v, (v + NZ) % along) for v in range(along)]
    down = [(v, (v - NZ) % along) for v in range(along)]
    left = lax.ppermute(here, "vir", up)
    right = lax.ppermute(here, "vir", down)
    half = here.shape[0] // 2
    far_low = lax.ppermute(left[:half], "vir", up)
    far_high = lax.ppermute(right[half:], "vir", down)
    pieces = [here, left, right, far_low, far_high]
    swap_cores = [(j, j ^ 1) for j in range(16)]
    pieces += [lax.ppermute(piece, "occ", swap_cores) for piece in pieces]

    out = final(
        where,
        block_mask.reshape(-1),
        pltpu.with_memory_space_constraint(amplitudes.reshape(kept * occ * rows, width), pltpu.HBM),
        pltpu.with_memory_space_constraint(residual_in.reshape(occ * rows, width), pltpu.HBM),
        swapped,
        pieces,
        kept,
    )
    return out.reshape(residual_in.shape)


def solution(mesh):
    return jax.shard_map(
        per_device,
        mesh=mesh,
        in_specs=(P(None, "occ", "vir", None), P(None, "vir", None), P(), P("occ", "vir", None)),
        out_specs=P("occ", "vir", None),
        check_vma=False,
    )
```

time: 142 us -> 107 us (0.75)
  blocking collectives: 70.3 us -> 36.2 us
  starting transfers between devices: 40.4 us -> 28.3 us
  waiting for transfers between devices: 15.2 us -> 26.6 us
  local copies, waits for them, and re-layouts: 3.15 us -> 0.14 us
  Pallas kernels: 10.4 us -> 13.4 us
    all_gather x1, blocking collectives: 70.3 us -> 36.2 us  [per_device(): lax.all_gather(slab, 'vir', axis=0, tiled=True, axis_index_groups=groups)]
    all_to_all x1, starting transfers between devices: 18.7 us -> 6.49 us  [per_device(): swapped = lax.all_to_all(packed, 'vir', 0, 0, tiled=True)]
    ppermute x1, waiting for transfers between devices: 6.67 us -> 15 us  [per_device(): left = lax.ppermute(here, 'vir', up)]
    pallas_call x1, Pallas kernels: 2.99 us -> 6.55 us  [pack(): pl.pallas_call(pack_body, grid=(blocks,), in_specs=[pl.BlockSpec((pairs,...]
    unnamed x15 -> x3, local copies, waits for them, and re-layouts: 2.44 us -> 0.01 us
    ppermute x1, waiting for transfers between devices: 7.86 us -> 9.83 us  [per_device(): far_high = lax.ppermute(right[half:], 'vir', down)]
  transfers between devices with their start and end apart: 10 -> 10, of which waited for: 3 -> 3; matrix products, arithmetic and copies ran while one was open for 1% -> 0% of each run, Pallas kernels for 0% -> 0%
where the time goes in v2:
time: 107 us; the launch traced here: 106 us
  blocking collectives  36.2 us (34%)
  starting transfers between devices  28.3 us (26%)
  waiting for transfers between devices  26.6 us (25%)
  Pallas kernels  13.4 us (13%)
    all_gather x1, blocking collectives, per_device(): lax.all_gather(slab, 'vir', axis=0, tiled=True, axis_index_groups=groups)  36.2 us
    ppermute x1, waiting for transfers between devices, per_device(): left = lax.ppermute(here, 'vir', up)  15 us
    ppermute x5, starting transfers between devices, per_device(): pieces += [lax.ppermute(piece, 'occ', swap_cores) for piece in pieces]  10.1 us
    ppermute x1, waiting for transfers between devices, per_device(): far_high = lax.ppermute(right[half:], 'vir', down)  9.83 us
    pallas_call x1, Pallas kernels, final(): pl.pallas_call(final_body, in_specs=[smem, smem, hbm, hbm, vmem] + [hbm]...  6.86 us
    pallas_call x1, Pallas kernels, pack(): pl.pallas_call(pack_body, grid=(blocks,), in_specs=[pl.BlockSpec((pairs,...  6.55 us
    all_to_all x1, starting transfers between devices, per_device(): swapped = lax.all_to_all(packed, 'vir', 0, 0, tiled=True)  6.49 us
    ppermute x1, starting transfers between devices, per_device(): right = lax.ppermute(here, 'vir', down)  3.72 us
  transfers between devices with their start and end apart: 10, of which 3 were waited for; matrix products, arithmetic and copies ran while one was open for 0% of the time, Pallas kernels for 0%

profile of v2, /device:TPU:6, one launch (start us, length us, event | category | flops | bytes accessed | tf_op | source)
XLA Modules:
  0.0 105.7 jit_solution(4179041253474173638)
XLA Ops:
  0.0 0.8 slice_select_fusion
  0.9 36.2 %all-gather = bf16[1,288,1152]{2,1,0:T(8,128)(2,1)S(1)} all-gather(bf16[1,24,1152]{2,1,0:T(8,128)(2,1)S(1)} %slice_select_fusion), channel_id=2, replica_groups={{0,1,2,3,4,5,6,7,8,9,10,11},{12,13,14,15,16,17,18,19,20,21,22,23},{24,2..., dimensions={1}, use_global_device_ids=true | all-gather | bytes 718848 | tf_op jit(solution)/shard_map/all_gather | solution.py:161
  37.1 6.5 %pack.1 = bf16[48,112,128]{2,1,0:T(8,128)(2,1)} custom-call(bf16[24,24,1152]{2,1,0:T(8,128)(2,1)} %bitcast.11), custom_call_target="tpu_custom_call" | custom-call | tf_op jit(solution)/shard_map/pack/pallas_call | solution.py:45
  43.6 6.5 %all-to-all-start = ((bf16[48,112,128]{2,1,0:T(8,128)(2,1)}), bf16[48,112,128]{2,1,0:T(8,128)(2,1)S(1)}, u32[]{:S(2)}, u32[]{:S(2)}) async-start(bf16[48,112,128]{2,1,0:T(8,128)(2,1)} %pack.1), calls=%async_computation | async-start | bytes 2752512 | tf_op jit(solution)/shard_map/all_to_all | solution.py:165
  50.1 0.0 copy-start
  50.1 2.1 %collective-permute-start = (bf16[288,1152]{1,0:T(8,128)(2,1)S(1)}, bf16[288,1152]{1,0:T(8,128)(2,1)S(1)}, u32[]{:S(2)}, u32[]{:S(2)}) collective-permute-start(bf16[288,1152]{1,0:T(8,128)(2,1)S(1)} %bitcast.7), channel_id=1, source_target_pairs={{0,12},{1,13},{2,14},{3,15},{4,16},{5,17},{6,18},{7,19},{8,20},{9,... | collective-permute-start | bytes 1990664 | tf_op jit(solution)/shard_map/ppermute | solution.py:169
  52.2 3.7 %collective-permute-start.1 = (bf16[288,1152]{1,0:T(8,128)(2,1)S(1)}, bf16[288,1152]{1,0:T(8,128)(2,1)S(1)}, u32[]{:S(2)}, u32[]{:S(2)}) collective-permute-start(bf16[288,1152]{1,0:T(8,128)(2,1)S(1)} %bitcast.8), channel_id=1, source_target_pairs={{0,36},{1,37},{2,38},{3,39},{4,40},{5,41},{6,42},{7,43},{8,44},{9,... | collective-permute-start | bytes 1990664 | tf_op jit(solution)/shard_map/ppermute | solution.py:170
  56.0 1.9 %collective-permute-start.4 = (bf16[288,1152]{1,0:T(8,128)(2,1)S(1)}, bf16[288,1152]{1,0:T(8,128)(2,1)}, u32[]{:S(2)}, u32[]{:S(2)}) collective-permute-start(bf16[288,1152]{1,0:T(8,128)(2,1)S(1)} %bitcast.9), channel_id=1, source_target_pairs={{0,48},{48,0},{96,144},{144,96},{192,240},{240,192},{288,336},{336... | collective-permute-start | bytes 1990664 | tf_op jit(solution)/shard_map/ppermute | solution.py:176
  57.9 15.0 %collective-permute-done.rest_1_ = bf16[288,1152]{1,0:T(8,128)(2,1)S(1)} collective-permute-done((bf16[288,1152]{1,0:T(8,128)(2,1)S(1)}, bf16[288,1152]{1,0:T(8,128)(2,1)S(1)}, u32[]{:S(2)}, u32[]{:S(2)}) %collective-permute-start) | collective-permute-done | bytes 663584 | tf_op jit(solution)/shard_map/ppermute | solution.py:169
  73.0 3.0 %collective-permute-start.2 = (bf16[144,1152]{1,0:T(8,128)(2,1)S(1)}, bf16[144,1152]{1,0:T(8,128)(2,1)}, u32[]{:S(2)}, u32[]{:S(2)}) collective-permute-start(bf16[144,1152]{1,0:T(8,128)(2,1)S(1)} %slice.16), channel_id=1, source_target_pairs={{0,12},{1,13},{2,14},{3,15},{4,16},{5,17},{6,18},{7,19},{8,20},{9,... | collective-permute-start | bytes 995336 | tf_op jit(solution)/shard_map/ppermute | solution.py:172
  75.9 1.9 %collective-permute-start.5 = (bf16[288,1152]{1,0:T(8,128)(2,1)S(1)}, bf16[288,1152]{1,0:T(8,128)(2,1)}, u32[]{:S(2)}, u32[]{:S(2)}) collective-permute-start(bf16[288,1152]{1,0:T(8,128)(2,1)S(1)} %collective-permute-done.rest_1_), channel_id=1, source_target_pairs={{0,48},{48,0},{96,144},{144,96},{192,240},{240,192},{288,336},{336... | collective-permute-start | bytes 1990664 | tf_op jit(solution)/shard_map/ppermute | solution.py:176
  77.9 0.0 collective-permute-done.1.rest_2_
  77.9 2.4 %collective-permute-start.6 = (bf16[288,1152]{1,0:T(8,128)(2,1)S(1)}, bf16[288,1152]{1,0:T(8,128)(2,1)}, u32[]{:S(2)}, u32[]{:S(2)}) collective-permute-start(bf16[288,1152]{1,0:T(8,128)(2,1)S(1)} %collective-permute-done.1.rest_2_), channel_id=1, source_target_pairs={{0,48},{48,0},{96,144},{144,96},{192,240},{240,192},{288,336},{336... | collective-permute-start | bytes 1990664 | tf_op jit(solution)/shard_map/ppermute | solution.py:176
  80.3 2.9 %collective-permute-start.3 = (bf16[144,1152]{1,0:T(8,128)(2,1)S(1)}, bf16[144,1152]{1,0:T(8,128)(2,1)}, u32[]{:S(2)}, u32[]{:S(2)}) collective-permute-start(bf16[144,1152]{1,0:T(8,128)(2,1)S(1)} %slice.17), channel_id=1, source_target_pairs={{0,36},{1,37},{2,38},{3,39},{4,40},{5,41},{6,42},{7,43},{8,44},{9,... | collective-permute-start | bytes 995336 | tf_op jit(solution)/shard_map/ppermute | solution.py:173
  83.2 0.0 collective-permute-done.2.rest_3_
  83.2 1.9 %collective-permute-start.7 = (bf16[144,1152]{1,0:T(8,128)(2,1)}, bf16[144,1152]{1,0:T(8,128)(2,1)}, u32[]{:S(2)}, u32[]{:S(2)}) collective-permute-start(bf16[144,1152]{1,0:T(8,128)(2,1)} %collective-permute-done.2.rest_3_), channel_id=1, source_target_pairs={{0,48},{48,0},{96,144},{144,96},{192,240},{240,192},{288,336},{336... | collective-permute-start | bytes 995336 | tf_op jit(solution)/shard_map/ppermute | solution.py:176
  85.1 9.8 %collective-permute-done.3.rest_4_ = bf16[144,1152]{1,0:T(8,128)(2,1)} collective-permute-done((bf16[144,1152]{1,0:T(8,128)(2,1)S(1)}, bf16[144,1152]{1,0:T(8,128)(2,1)}, u32[]{:S(2)}, u32[]{:S(2)}) %collective-permute-start.3) | collective-permute-done | bytes 331808 | tf_op jit(solution)/shard_map/ppermute | solution.py:173
  95.0 1.9 %collective-permute-start.8 = (bf16[144,1152]{1,0:T(8,128)(2,1)}, bf16[144,1152]{1,0:T(8,128)(2,1)}, u32[]{:S(2)}, u32[]{:S(2)}) collective-permute-start(bf16[144,1152]{1,0:T(8,128)(2,1)} %collective-permute-done.3.rest_4_), channel_id=1, source_target_pairs={{0,48},{48,0},{96,144},{144,96},{192,240},{240,192},{288,336},{336... | collective-permute-start | bytes 995336 | tf_op jit(solution)/shard_map/ppermute | solution.py:176
  96.9 0.0 copy-done
  96.9 0.1 reshape.17.mask
  97.0 0.1 pad_add_fusion.where
  97.1 0.0 collective-permute-done.4.rest_5_
  97.1 0.0 collective-permute-done.5.rest_6_
  97.1 0.0 collective-permute-done.6.rest_7_
  97.1 0.0 collective-permute-done.7.rest_8_
  97.1 1.7 %collective-permute-done.8.rest_9_ = bf16[144,1152]{1,0:T(8,128)(2,1)} collective-permute-done((bf16[144,1152]{1,0:T(8,128)(2,1)}, bf16[144,1152]{1,0:T(8,128)(2,1)}, u32[]{:S(2)}, u32[]{:S(2)}) %collective-permute-start.8) | collective-permute-done | bytes 331808 | tf_op jit(solution)/shard_map/ppermute | solution.py:176
  98.8 0.0 all-to-all-done.swapped
  98.8 6.9 %final.1 = f32[288,1152]{1,0:T(8,128)} custom-call(s32[2]{0:T(128)S(1)} %pad_add_fusion.where, s32[72]{0:T(128)S(1)} %reshape.17.mask, bf16[576,1152]{1,0:T(8,128)(2,1)} %bitcast.12, f32[288,1152]{1,0:T(8,128)} %bitcast.13, bf16[48,112,128]{2,1,0:T(8,128)(2,1)S(1)} %all-to-all-done.swapped, bf16[288,1152]{1,0:T(8,128)(2,1)S(1)} %bitcast.10, ...), custom_call_target="tpu_custom_call" | custom-call | tf_op jit(solution)/shard_map/final/pallas_call | solution.py:133
  (3 shorter events, 0.1 us)
Async XLA Ops:
  43.6 55.2 %all-to-all-start = ((bf16[48,112,128]{2,1,0:T(8,128)(2,1)}), bf16[48,112,128]{2,1,0:T(8,128)(2,1)S(1)}, u32[]{:S(2)}, u32[]{:S(2)}) async-start(bf16[48,112,128]{2,1,0:T(8,128)(2,1)} %pack.1), calls=%async_computation | async-start | bytes 2752512 | tf_op jit(solution)/shard_map/all_to_all | solution.py:165
  50.1 46.8 %copy-start = (s32[2,6,6]{2,0,1:T(2,128)S(1)}, s32[2,6,6]{2,0,1:T(2,128)}, u32[]{:S(2)}) copy-start(s32[2,6,6]{2,0,1:T(2,128)} %param.6) | copy-start | bytes 868
  50.1 22.8 %collective-permute-start = (bf16[288,1152]{1,0:T(8,128)(2,1)S(1)}, bf16[288,1152]{1,0:T(8,128)(2,1)S(1)}, u32[]{:S(2)}, u32[]{:S(2)}) collective-permute-start(bf16[288,1152]{1,0:T(8,128)(2,1)S(1)} %bitcast.7), channel_id=1, source_target_pairs={{0,12},{1,13},{2,14},{3,15},{4,16},{5,17},{6,18},{7,19},{8,20},{9,... | collective-permute-start | bytes 1990664 | tf_op jit(solution)/shard_map/ppermute | solution.py:169
  52.2 25.6 %collective-permute-start.1 = (bf16[288,1152]{1,0:T(8,128)(2,1)S(1)}, bf16[288,1152]{1,0:T(8,128)(2,1)S(1)}, u32[]{:S(2)}, u32[]{:S(2)}) collective-permute-start(bf16[288,1152]{1,0:T(8,128)(2,1)S(1)} %bitcast.8), channel_id=1, source_target_pairs={{0,36},{1,37},{2,38},{3,39},{4,40},{5,41},{6,42},{7,43},{8,44},{9,... | collective-permute-start | bytes 1990664 | tf_op jit(solution)/shard_map/ppermute | solution.py:170
  56.0 41.1 %collective-permute-start.4 = (bf16[288,1152]{1,0:T(8,128)(2,1)S(1)}, bf16[288,1152]{1,0:T(8,128)(2,1)}, u32[]{:S(2)}, u32[]{:S(2)}) collective-permute-start(bf16[288,1152]{1,0:T(8,128)(2,1)S(1)} %bitcast.9), channel_id=1, source_target_pairs={{0,48},{48,0},{96,144},{144,96},{192,240},{240,192},{288,336},{336... | collective-permute-start | bytes 1990664 | tf_op jit(solution)/shard_map/ppermute | solution.py:176
  73.0 10.3 %collective-permute-start.2 = (bf16[144,1152]{1,0:T(8,128)(2,1)S(1)}, bf16[144,1152]{1,0:T(8,128)(2,1)}, u32[]{:S(2)}, u32[]{:S(2)}) collective-permute-start(bf16[144,1152]{1,0:T(8,128)(2,1)S(1)} %slice.16), channel_id=1, source_target_pairs={{0,12},{1,13},{2,14},{3,15},{4,16},{5,17},{6,18},{7,19},{8,20},{9,... | collective-permute-start | bytes 995336 | tf_op jit(solution)/shard_map/ppermute | solution.py:172
  75.9 21.2 %collective-permute-start.5 = (bf16[288,1152]{1,0:T(8,128)(2,1)S(1)}, bf16[288,1152]{1,0:T(8,128)(2,1)}, u32[]{:S(2)}, u32[]{:S(2)}) collective-permute-start(bf16[288,1152]{1,0:T(8,128)(2,1)S(1)} %collective-permute-done.rest_1_), channel_id=1, source_target_pairs={{0,48},{48,0},{96,144},{144,96},{192,240},{240,192},{288,336},{336... | collective-permute-start | bytes 1990664 | tf_op jit(solution)/shard_map/ppermute | solution.py:176
  77.9 19.2 %collective-permute-start.6 = (bf16[288,1152]{1,0:T(8,128)(2,1)S(1)}, bf16[288,1152]{1,0:T(8,128)(2,1)}, u32[]{:S(2)}, u32[]{:S(2)}) collective-permute-start(bf16[288,1152]{1,0:T(8,128)(2,1)S(1)} %collective-permute-done.1.rest_2_), channel_id=1, source_target_pairs={{0,48},{48,0},{96,144},{144,96},{192,240},{240,192},{288,336},{336... | collective-permute-start | bytes 1990664 | tf_op jit(solution)/shard_map/ppermute | solution.py:176
  80.3 14.6 %collective-permute-start.3 = (bf16[144,1152]{1,0:T(8,128)(2,1)S(1)}, bf16[144,1152]{1,0:T(8,128)(2,1)}, u32[]{:S(2)}, u32[]{:S(2)}) collective-permute-start(bf16[144,1152]{1,0:T(8,128)(2,1)S(1)} %slice.17), channel_id=1, source_target_pairs={{0,36},{1,37},{2,38},{3,39},{4,40},{5,41},{6,42},{7,43},{8,44},{9,... | collective-permute-start | bytes 995336 | tf_op jit(solution)/shard_map/ppermute | solution.py:173
  83.2 13.9 %collective-permute-start.7 = (bf16[144,1152]{1,0:T(8,128)(2,1)}, bf16[144,1152]{1,0:T(8,128)(2,1)}, u32[]{:S(2)}, u32[]{:S(2)}) collective-permute-start(bf16[144,1152]{1,0:T(8,128)(2,1)} %collective-permute-done.2.rest_3_), channel_id=1, source_target_pairs={{0,48},{48,0},{96,144},{144,96},{192,240},{240,192},{288,336},{336... | collective-permute-start | bytes 995336 | tf_op jit(solution)/shard_map/ppermute | solution.py:176
  95.0 3.9 %collective-permute-start.8 = (bf16[144,1152]{1,0:T(8,128)(2,1)}, bf16[144,1152]{1,0:T(8,128)(2,1)}, u32[]{:S(2)}, u32[]{:S(2)}) collective-permute-start(bf16[144,1152]{1,0:T(8,128)(2,1)} %collective-permute-done.3.rest_4_), channel_id=1, source_target_pairs={{0,48},{48,0},{96,144},{144,96},{192,240},{240,192},{288,336},{336... | collective-permute-start | bytes 995336 | tf_op jit(solution)/shard_map/ppermute | solution.py:176

commit v3 on v2

v3 whole, which is shorter than its diff:
```python
import jax
import jax.numpy as jnp
from jax import lax
from jax.experimental import pallas as pl
from jax.experimental.pallas import tpu as pltpu
from jax.sharding import PartitionSpec as P

TILE = 192
LANES = 128
NX, NZ = 4, 12


SPLIT = 6


def in_hbm(array):
    return pltpu.with_memory_space_constraint(array, pltpu.HBM)


def pack_body(source, gathered, packed, narrow, wide, made, sems):
    pairs, rows, width = source.shape
    peers = packed.shape[0]
    step = width // peers
    full = pairs * step // LANES
    part = pairs // SPLIT
    loads = [
        pltpu.make_async_copy(source.at[pl.ds(j * part, part)], narrow.at[pl.ds(j * part, part)], sems.at[j])
        for j in range(SPLIT)
    ]
    for load in loads:
        load.start()
    for j in range(SPLIT):
        loads[j].wait()
        wide[j * part : (j + 1) * part] = narrow[j * part : (j + 1) * part].astype(jnp.float32)
    lane = lax.broadcasted_iota(jnp.int32, (rows, LANES), 1)
    block = 3 * LANES
    many = block // step

    def store(p):
        span = pl.ds(p * many, many)
        return pltpu.make_async_copy(made.at[span], packed.at[span], sems.at[SPLIT + p])

    def fill(p, carry):
        for q in range(many):
            tile, at = divmod(step * q, LANES)
            here = pl.ds(pl.multiple_of(p * block + tile * LANES, LANES), LANES)
            next_tile = pl.ds(pl.multiple_of(p * block + (tile + 1) * LANES, LANES), LANES)
            parts = [None] * (full + 2)
            for g in range(pairs):
                piece = wide[g, :, here]
                if at + step > LANES:
                    piece = jnp.where(lane >= at, piece, wide[g, :, next_tile])
                put, to = divmod(step * g, LANES)
                if to != at:
                    piece = pltpu.roll(piece, (to - at) % LANES, 1)
                parts[put] = piece if parts[put] is None else jnp.where(lane >= to, piece, parts[put])
                if to + step > LANES:
                    parts[put + 1] = piece
            for d in range(full):
                made[p * many + q, d * rows : (d + 1) * rows] = parts[d].astype(jnp.bfloat16)
            low, middle, high = (parts[full][8 * j : 8 * j + 8] for j in range(3))
            low = jnp.where(lane[:8] < LANES // 2, low, pltpu.roll(middle, LANES // 2, 1))
            made[p * many + q, full * rows :] = jnp.concatenate([low, high], axis=0).astype(jnp.bfloat16)
        store(p).start()
        return carry

    blocks = width // block
    lax.fori_loop(0, blocks, fill, 0)
    for p in range(blocks):
        store(p).wait()


def pack(amplitudes, gathered, peers):
    pairs, rows, width = amplitudes.shape
    full = pairs * (width // peers) // LANES
    tall = full * rows + 16
    hbm = pl.BlockSpec(memory_space=pltpu.HBM)
    return pl.pallas_call(
        pack_body,
        in_specs=[hbm, hbm],
        out_specs=hbm,
        out_shape=jax.ShapeDtypeStruct((peers, tall, LANES), jnp.bfloat16),
        scratch_shapes=[
            pltpu.VMEM(amplitudes.shape, jnp.bfloat16),
            pltpu.VMEM(amplitudes.shape, jnp.float32),
            pltpu.VMEM((peers, tall, LANES), jnp.bfloat16),
            pltpu.SemaphoreType.DMA((SPLIT + width // 384,)),
        ],
        compiler_params=pltpu.CompilerParams(vmem_limit_bytes=12 << 20),
        name="pack",
    )(in_hbm(amplitudes), in_hbm(gathered))


def spread_body(mask, piece, mask_rows):
    count, _, width = mask_rows.shape
    tiles = width // TILE
    lane = lax.broadcasted_iota(jnp.int32, (16, width), 1)
    for t in range(count):
        row = jnp.zeros((16, width), jnp.float32)
        for u in range(tiles):
            inside = (lane >= u * TILE) & (lane < (u + 1) * TILE)
            row = jnp.where(inside, mask[t * tiles + u].astype(jnp.float32), row)
        mask_rows[t] = row.astype(jnp.bfloat16)


def spread(block_mask, piece, width):
    tiles = width // TILE
    count = block_mask.size // tiles
    return pl.pallas_call(
        spread_body,
        in_specs=[pl.BlockSpec(memory_space=pltpu.SMEM), pl.BlockSpec(memory_space=pltpu.HBM)],
        out_specs=pl.BlockSpec(memory_space=pltpu.VMEM),
        out_shape=jax.ShapeDtypeStruct((count, 16, width), jnp.bfloat16),
        cost_estimate=pl.CostEstimate(flops=25 * 10**9, transcendentals=0, bytes_accessed=count * 32 * width),
        name="spread",
    )(block_mask.reshape(-1), in_hbm(piece))


def final_body(where, amplitudes, residual, masks, swapped, *rest):
    pieces, (out, own, combined, weights, start, made, mask_rows, sems) = rest[:-8], rest[-8:]
    kept, width = weights.shape[0], weights.shape[1]
    tiles = width // TILE
    core, mine = where[0], where[1]
    half = pieces[0].shape[0]
    copies = [pltpu.make_async_copy(amplitudes, own, sems.at[0])]
    steps = len(pieces) // kept
    for side in range(kept):
        k = core if side == 0 else 1 - core
        for j in range(steps):
            piece = pieces[side * steps + j]
            base = pl.multiple_of(lax.rem(mine + jnp.where(k == 0, NX - j, j), NX) * half, 16)
            target = weights.at[k, pl.ds(base, half), :]
            copies.append(pltpu.make_async_copy(piece, target, sems.at[len(copies)]))
    copies.append(pltpu.make_async_copy(masks, mask_rows, sems.at[len(copies)]))
    copies.append(pltpu.make_async_copy(residual, start, sems.at[len(copies)]))
    for copy in copies:
        copy.start()

    copies[0].wait()
    pairs = own.shape[0]
    peers, tall = swapped.shape[0], swapped.shape[1]
    rows = width // peers
    full = tall // rows
    for d in range(full + 1):
        count = min(LANES, pairs - d * LANES)
        if d < full:
            tile = swapped[:, d * rows : (d + 1) * rows, :].astype(jnp.float32)
        else:
            ends = swapped[:, d * rows :, :].astype(jnp.float32)
            low = ends[:, :8].reshape(peers * 8, LANES)
            middle = pltpu.roll(low, LANES // 2, 1).reshape(peers, 8, LANES)
            tile = jnp.concatenate([ends[:, :8], middle, ends[:, 8:]], axis=1)
        turned = jnp.transpose(tile.reshape(width, LANES))
        own_rows = own[d * LANES : d * LANES + count, :].astype(jnp.float32)
        combined[d * LANES : d * LANES + count, :] = (2.0 * own_rows - turned[:count]).astype(jnp.bfloat16)

    for copy in copies[1:]:
        copy.wait()
    half_rows = pairs // kept
    wide = 384
    stores = []
    for n in range(width // wide):
        cols = slice(n * wide, (n + 1) * wide)
        total = start[:, cols]
        for k in range(kept):
            masked = jnp.concatenate(
                [
                    (weights[k, t * TILE : (t + 1) * TILE, cols].reshape(-1, 16, wide) * mask_rows[k * tiles + t, :, cols][None])
                    for t in range(tiles)
                ]
            ).reshape(width, wide)
            total += jnp.dot(
                combined[k * half_rows : (k + 1) * half_rows, :], masked, preferred_element_type=jnp.float32
            )
        made[:, cols] = total
        stores.append(pltpu.make_async_copy(made.at[:, cols], out.at[:, cols], sems.at[len(copies) + n]))
        stores[-1].start()
    for store in stores:
        store.wait()


def final(where, amplitudes, residual, mask_rows, swapped, pieces, kept):
    width = residual.shape[1]
    smem = pl.BlockSpec(memory_space=pltpu.SMEM)
    vmem = pl.BlockSpec(memory_space=pltpu.VMEM)
    hbm = pl.BlockSpec(memory_space=pltpu.HBM)
    return pl.pallas_call(
        final_body,
        in_specs=[smem, hbm, hbm, hbm, vmem] + [hbm] * len(pieces),
        out_specs=hbm,
        out_shape=jax.ShapeDtypeStruct(residual.shape, jnp.float32),
        scratch_shapes=[
            pltpu.VMEM(amplitudes.shape, jnp.bfloat16),
            pltpu.VMEM(amplitudes.shape, jnp.bfloat16),
            pltpu.VMEM((kept, width, width), jnp.bfloat16),
            pltpu.VMEM(residual.shape, jnp.float32),
            pltpu.VMEM(residual.shape, jnp.float32),
            pltpu.VMEM(mask_rows.shape, jnp.bfloat16),
            pltpu.SemaphoreType.DMA((len(pieces) + 3 + width // 384,)),
        ],
        compiler_params=pltpu.CompilerParams(vmem_limit_bytes=24 << 20),
        name="final",
    )(where, amplitudes, residual, mask_rows, swapped, *pieces)


def per_device(amplitudes, integrals, block_mask, residual_in):
    kept, occ, rows, width = amplitudes.shape
    core = lax.rem(lax.axis_index("occ"), 2)
    column = lax.div(lax.axis_index("vir"), NZ)
    where = jnp.stack([core, column]).astype(jnp.int32)

    along = NX * NZ
    occ_axis = lax.axis_size("occ")
    slab = jnp.where(core == 0, integrals[0], integrals[1])
    groups = [[x * NZ + z for z in range(NZ)] for x in range(NX)]
    here = lax.all_gather(slab, "vir", axis=0, tiled=True, axis_index_groups=groups)

    packed = pack(amplitudes.reshape(kept * occ, rows, width), here, width // rows)
    swapped = lax.all_to_all(packed, "vir", 0, 0, tiled=True)

    ring = [
        (o * along + v, o * along + (v + (NZ if o % 2 == 0 else -NZ)) % along) for o in range(occ_axis) for v in range(along)
    ]
    pieces = [here]
    for _ in range(NX - 1):
        pieces.append(lax.ppermute(pieces[-1], ("occ", "vir"), ring))
    mask_rows = spread(block_mask, pieces[1][:16, :LANES], width)
    swap_cores = [(j, j ^ 1) for j in range(occ_axis)]
    pieces += [lax.ppermute(piece, "occ", swap_cores) for piece in pieces]

    out = final(
        where,
        in_hbm(amplitudes.reshape(kept * occ * rows, width)),
        in_hbm(residual_in.reshape(occ * rows, width)),
        in_hbm(mask_rows),
        swapped,
        pieces,
        kept,
    )
    return out.reshape(residual_in.shape)


def solution(mesh):
    return jax.shard_map(
        per_device,
        mesh=mesh,
        in_specs=(P(None, "occ", "vir", None), P(None, "vir", None), P(), P("occ", "vir", None)),
        out_specs=P("occ", "vir", None),
        check_vma=False,
    )
```

time: 107 us -> 110 us (1.028)
  starting transfers between devices: 28.3 us -> 23.4 us
  waiting for transfers between devices: 26.6 us -> 30.1 us
  Pallas kernels: 13.4 us -> 15.4 us
  blocking collectives: 36.2 us -> 38 us
    all_to_all x1, waiting for transfers between devices: 0.01 us -> 11.8 us  [per_device(): swapped = lax.all_to_all(packed, 'vir', 0, 0, tiled=True)]
    ppermute x4 -> x3, waiting for transfers between devices: 24.9 us -> 17.6 us  [per_device(): pieces.append(lax.ppermute(pieces[-1], ('occ', 'vir'), ring))]
    ppermute x4 -> x3, starting transfers between devices: 11.7 us -> 8.17 us  [per_device(): pieces.append(lax.ppermute(pieces[-1], ('occ', 'vir'), ring))]
    pallas_call x2 -> x3, Pallas kernels: 13.4 us -> 15.4 us  [the longest x1 7.05 us: pack(): pl.pallas_call(pack_body, in_specs=[hbm, hbm], out_specs=hbm, out_shape=j...]
    ppermute x5 -> x4, starting transfers between devices: 10.1 us -> 8.14 us  [per_device(): pieces += [lax.ppermute(piece, 'occ', swap_cores) for piece in pieces]]
    all_gather x1, blocking collectives: 36.2 us -> 38 us  [per_device(): lax.all_gather(slab, 'vir', axis=0, tiled=True, axis_index_groups=groups)]
  transfers between devices with their start and end apart: 10 -> 8, of which waited for: 3 -> 4; matrix products, arithmetic and copies ran while one was open for 0% -> 1% of each run, Pallas kernels for 0% -> 8%
where the time goes in v3:
time: 110 us; the launch traced here: 109 us
  blocking collectives  38 us (35%)
  waiting for transfers between devices  30.1 us (27%)
  starting transfers between devices  23.4 us (21%)
  Pallas kernels  15.4 us (14%)
  local copies, waits for them, and re-layouts  1.2 us (1%)
    all_gather x1, blocking collectives, per_device(): lax.all_gather(slab, 'vir', axis=0, tiled=True, axis_index_groups=groups)  38 us
    ppermute x3, waiting for transfers between devices, per_device(): pieces.append(lax.ppermute(pieces[-1], ('occ', 'vir'), ring))  17.6 us
    all_to_all x1, waiting for transfers between devices, per_device(): swapped = lax.all_to_all(packed, 'vir', 0, 0, tiled=True)  11.8 us
    ppermute x3, starting transfers between devices, per_device(): pieces.append(lax.ppermute(pieces[-1], ('occ', 'vir'), ring))  8.17 us
    ppermute x4, starting transfers between devices, per_device(): pieces += [lax.ppermute(piece, 'occ', swap_cores) for piece in pieces]  8.14 us
    all_to_all x1, starting transfers between devices, per_device(): swapped = lax.all_to_all(packed, 'vir', 0, 0, tiled=True)  7.11 us
    pallas_call x1, Pallas kernels, pack(): pl.pallas_call(pack_body, in_specs=[hbm, hbm], out_specs=hbm, out_shape=j...  7.05 us
    pallas_call x1, Pallas kernels, final(): pl.pallas_call(final_body, in_specs=[smem, hbm, hbm, hbm, vmem] + [hbm] *...  6.84 us
  transfers between devices with their start and end apart: 8, of which 4 were waited for; matrix products, arithmetic and copies ran while one was open for 1% of the time, Pallas kernels for 8%

profile of v3, /device:TPU:6, one launch (start us, length us, event | category | flops | bytes accessed | tf_op | source)
XLA Modules:
  0.0 109.1 jit_solution(16597471662514445830)
XLA Ops:
  0.0 0.8 slice_select_fusion
  0.9 38.0 %all-gather = bf16[1,288,1152]{2,1,0:T(8,128)(2,1)} all-gather(bf16[1,24,1152]{2,1,0:T(8,128)(2,1)S(1)} %slice_select_fusion), channel_id=2, replica_groups={{0,1,2,3,4,5,6,7,8,9,10,11},{12,13,14,15,16,17,18,19,20,21,22,23},{24,2..., dimensions={1}, use_global_device_ids=true | all-gather | bytes 718848 | tf_op jit(solution)/shard_map/all_gather | solution.py:216
  38.8 2.4 %collective-permute-start = (bf16[288,1152]{1,0:T(8,128)(2,1)}, bf16[288,1152]{1,0:T(8,128)(2,1)S(1)}, u32[]{:S(2)}, u32[]{:S(2)}) collective-permute-start(bf16[288,1152]{1,0:T(8,128)(2,1)} %bitcast.4.gathered.rest_0_), channel_id=1, source_target_pairs={{0,12},{1,13},{2,14},{3,15},{4,16},{5,17},{6,18},{7,19},{8,20},{9,... | collective-permute-start | bytes 1990664 | tf_op jit(solution)/shard_map/ppermute | solution.py:226
  41.2 7.1 %pack.1 = bf16[48,112,128]{2,1,0:T(8,128)(2,1)} custom-call(bf16[24,24,1152]{2,1,0:T(8,128)(2,1)} %bitcast.7, bf16[288,1152]{1,0:T(8,128)(2,1)} %bitcast.4.gathered.rest_0_), custom_call_target="tpu_custom_call" | custom-call | tf_op jit(solution)/shard_map/pack/pallas_call | solution.py:78
  48.3 0.0 copy-start
  48.3 7.1 %all-to-all-start = ((bf16[48,112,128]{2,1,0:T(8,128)(2,1)}), bf16[48,112,128]{2,1,0:T(8,128)(2,1)S(1)}, u32[]{:S(2)}, u32[]{:S(2)}) async-start(bf16[48,112,128]{2,1,0:T(8,128)(2,1)} %pack.1), calls=%async_computation | async-start | bytes 2752512 | tf_op jit(solution)/shard_map/all_to_all | solution.py:219
  55.4 0.0 collective-permute-done.rest_1_
  55.4 2.1 %collective-permute-start.1 = (bf16[288,1152]{1,0:T(8,128)(2,1)S(1)}, bf16[288,1152]{1,0:T(8,128)(2,1)S(1)}, u32[]{:S(2)}, u32[]{:S(2)}) collective-permute-start(bf16[288,1152]{1,0:T(8,128)(2,1)S(1)} %collective-permute-done.rest_1_), channel_id=1, source_target_pairs={{0,12},{1,13},{2,14},{3,15},{4,16},{5,17},{6,18},{7,19},{8,20},{9,... | collective-permute-start | bytes 1990664 | tf_op jit(solution)/shard_map/ppermute | solution.py:226
  57.5 13.7 %collective-permute-done.1.rest_2_ = bf16[288,1152]{1,0:T(8,128)(2,1)S(1)} collective-permute-done((bf16[288,1152]{1,0:T(8,128)(2,1)S(1)}, bf16[288,1152]{1,0:T(8,128)(2,1)S(1)}, u32[]{:S(2)}, u32[]{:S(2)}) %collective-permute-start.1) | collective-permute-done | bytes 663584 | tf_op jit(solution)/shard_map/ppermute | solution.py:226
  71.2 3.7 %collective-permute-start.2 = (bf16[288,1152]{1,0:T(8,128)(2,1)S(1)}, bf16[288,1152]{1,0:T(8,128)(2,1)S(1)}, u32[]{:S(2)}, u32[]{:S(2)}) collective-permute-start(bf16[288,1152]{1,0:T(8,128)(2,1)S(1)} %collective-permute-done.1.rest_2_), channel_id=1, source_target_pairs={{0,12},{1,13},{2,14},{3,15},{4,16},{5,17},{6,18},{7,19},{8,20},{9,... | collective-permute-start | bytes 1990664 | tf_op jit(solution)/shard_map/ppermute | solution.py:226
  74.9 1.9 %collective-permute-start.3 = (bf16[288,1152]{1,0:T(8,128)(2,1)}, bf16[288,1152]{1,0:T(8,128)(2,1)}, u32[]{:S(2)}, u32[]{:S(2)}) collective-permute-start(bf16[288,1152]{1,0:T(8,128)(2,1)} %bitcast.4.gathered.rest_0_), channel_id=1, source_target_pairs={{0,48},{48,0},{96,144},{144,96},{192,240},{240,192},{288,336},{336... | collective-permute-start | bytes 1990664 | tf_op jit(solution)/shard_map/ppermute | solution.py:229
  76.8 0.0 copy-done
  76.9 0.6 reshape.19.mask
  77.5 0.1 pad_add_fusion.where
  77.5 2.4 %collective-permute-start.4 = (bf16[288,1152]{1,0:T(8,128)(2,1)S(1)}, bf16[288,1152]{1,0:T(8,128)(2,1)}, u32[]{:S(2)}, u32[]{:S(2)}) collective-permute-start(bf16[288,1152]{1,0:T(8,128)(2,1)S(1)} %collective-permute-done.rest_1_), channel_id=1, source_target_pairs={{0,48},{48,0},{96,144},{144,96},{192,240},{240,192},{288,336},{336... | collective-permute-start | bytes 1990664 | tf_op jit(solution)/shard_map/ppermute | solution.py:229
  79.9 0.6 slice.12.piece
  80.5 1.9 %collective-permute-start.5 = (bf16[288,1152]{1,0:T(8,128)(2,1)S(1)}, bf16[288,1152]{1,0:T(8,128)(2,1)}, u32[]{:S(2)}, u32[]{:S(2)}) collective-permute-start(bf16[288,1152]{1,0:T(8,128)(2,1)S(1)} %collective-permute-done.1.rest_2_), channel_id=1, source_target_pairs={{0,48},{48,0},{96,144},{144,96},{192,240},{240,192},{288,336},{336... | collective-permute-start | bytes 1990664 | tf_op jit(solution)/shard_map/ppermute | solution.py:229
  82.4 3.9 %collective-permute-done.2.rest_3_ = bf16[288,1152]{1,0:T(8,128)(2,1)S(1)} collective-permute-done((bf16[288,1152]{1,0:T(8,128)(2,1)S(1)}, bf16[288,1152]{1,0:T(8,128)(2,1)S(1)}, u32[]{:S(2)}, u32[]{:S(2)}) %collective-permute-start.2) | collective-permute-done | bytes 663584 | tf_op jit(solution)/shard_map/ppermute | solution.py:226
  86.4 1.9 %collective-permute-start.6 = (bf16[288,1152]{1,0:T(8,128)(2,1)S(1)}, bf16[288,1152]{1,0:T(8,128)(2,1)}, u32[]{:S(2)}, u32[]{:S(2)}) collective-permute-start(bf16[288,1152]{1,0:T(8,128)(2,1)S(1)} %collective-permute-done.2.rest_3_), channel_id=1, source_target_pairs={{0,48},{48,0},{96,144},{144,96},{192,240},{240,192},{288,336},{336... | collective-permute-start | bytes 1990664 | tf_op jit(solution)/shard_map/ppermute | solution.py:229
  88.3 1.5 %spread.1.masks = bf16[12,16,1152]{2,1,0:T(8,128)(2,1)} custom-call(s32[72]{0:T(128)} %reshape.19.mask, bf16[16,128]{1,0:T(8,128)(2,1)} %slice.12.piece), custom_call_target="tpu_custom_call" | custom-call | flops 24999999488 | bytes 442368 | tf_op jit(solution)/shard_map/spread/pallas_call | solution.py:109
  89.8 0.0 collective-permute-done.3.rest_4_
  89.8 0.0 collective-permute-done.4.rest_5_
  89.8 0.0 collective-permute-done.5.rest_6_
  89.8 0.7 collective-permute-done.6.rest_7_
  90.5 11.8 %all-to-all-done.swapped = bf16[48,112,128]{2,1,0:T(8,128)(2,1)S(1)} async-done(((bf16[48,112,128]{2,1,0:T(8,128)(2,1)}), bf16[48,112,128]{2,1,0:T(8,128)(2,1)S(1)}, u32[]{:S(2)}, u32[]{:S(2)}) %all-to-all-start) | async-done | bytes 1376288 | tf_op jit(solution)/shard_map/all_to_all | solution.py:219
  102.3 6.8 %final.1 = f32[288,1152]{1,0:T(8,128)} custom-call(s32[2]{0:T(128)S(1)} %pad_add_fusion.where, bf16[576,1152]{1,0:T(8,128)(2,1)} %bitcast.8, f32[288,1152]{1,0:T(8,128)} %bitcast.9, bf16[12,16,1152]{2,1,0:T(8,128)(2,1)} %spread.1.masks, bf16[48,112,128]{2,1,0:T(8,128)(2,1)S(1)} %all-to-all-done.swapped, bf16[288,1152]{1,0:T(8,128)(2,1)} %bitcast.4.gathered.rest_0_, ...), custom_call_target="tpu_custom_call" | custom-call | tf_op jit(solution)/shard_map/final/pallas_call | solution.py:187
  (1 shorter events, 0.0 us)
Async XLA Ops:
  38.8 16.6 %collective-permute-start = (bf16[288,1152]{1,0:T(8,128)(2,1)}, bf16[288,1152]{1,0:T(8,128)(2,1)S(1)}, u32[]{:S(2)}, u32[]{:S(2)}) collective-permute-start(bf16[288,1152]{1,0:T(8,128)(2,1)} %bitcast.4.gathered.rest_0_), channel_id=1, source_target_pairs={{0,12},{1,13},{2,14},{3,15},{4,16},{5,17},{6,18},{7,19},{8,20},{9,... | collective-permute-start | bytes 1990664 | tf_op jit(solution)/shard_map/ppermute | solution.py:226
  48.3 28.6 %copy-start = (s32[2,6,6]{2,0,1:T(2,128)S(1)}, s32[2,6,6]{2,0,1:T(2,128)}, u32[]{:S(2)}) copy-start(s32[2,6,6]{2,0,1:T(2,128)} %param.6) | copy-start | bytes 868
  48.3 54.0 %all-to-all-start = ((bf16[48,112,128]{2,1,0:T(8,128)(2,1)}), bf16[48,112,128]{2,1,0:T(8,128)(2,1)S(1)}, u32[]{:S(2)}, u32[]{:S(2)}) async-start(bf16[48,112,128]{2,1,0:T(8,128)(2,1)} %pack.1), calls=%async_computation | async-start | bytes 2752512 | tf_op jit(solution)/shard_map/all_to_all | solution.py:219
  55.4 15.8 %collective-permute-start.1 = (bf16[288,1152]{1,0:T(8,128)(2,1)S(1)}, bf16[288,1152]{1,0:T(8,128)(2,1)S(1)}, u32[]{:S(2)}, u32[]{:S(2)}) collective-permute-start(bf16[288,1152]{1,0:T(8,128)(2,1)S(1)} %collective-permute-done.rest_1_), channel_id=1, source_target_pairs={{0,12},{1,13},{2,14},{3,15},{4,16},{5,17},{6,18},{7,19},{8,20},{9,... | collective-permute-start | bytes 1990664 | tf_op jit(solution)/shard_map/ppermute | solution.py:226
  71.2 15.2 %collective-permute-start.2 = (bf16[288,1152]{1,0:T(8,128)(2,1)S(1)}, bf16[288,1152]{1,0:T(8,128)(2,1)S(1)}, u32[]{:S(2)}, u32[]{:S(2)}) collective-permute-start(bf16[288,1152]{1,0:T(8,128)(2,1)S(1)} %collective-permute-done.1.rest_2_), channel_id=1, source_target_pairs={{0,12},{1,13},{2,14},{3,15},{4,16},{5,17},{6,18},{7,19},{8,20},{9,... | collective-permute-start | bytes 1990664 | tf_op jit(solution)/shard_map/ppermute | solution.py:226
  74.9 14.9 %collective-permute-start.3 = (bf16[288,1152]{1,0:T(8,128)(2,1)}, bf16[288,1152]{1,0:T(8,128)(2,1)}, u32[]{:S(2)}, u32[]{:S(2)}) collective-permute-start(bf16[288,1152]{1,0:T(8,128)(2,1)} %bitcast.4.gathered.rest_0_), channel_id=1, source_target_pairs={{0,48},{48,0},{96,144},{144,96},{192,240},{240,192},{288,336},{336... | collective-permute-start | bytes 1990664 | tf_op jit(solution)/shard_map/ppermute | solution.py:229
  77.5 12.2 %collective-permute-start.4 = (bf16[288,1152]{1,0:T(8,128)(2,1)S(1)}, bf16[288,1152]{1,0:T(8,128)(2,1)}, u32[]{:S(2)}, u32[]{:S(2)}) collective-permute-start(bf16[288,1152]{1,0:T(8,128)(2,1)S(1)} %collective-permute-done.rest_1_), channel_id=1, source_target_pairs={{0,48},{48,0},{96,144},{144,96},{192,240},{240,192},{288,336},{336... | collective-permute-start | bytes 1990664 | tf_op jit(solution)/shard_map/ppermute | solution.py:229
  80.5 9.2 %collective-permute-start.5 = (bf16[288,1152]{1,0:T(8,128)(2,1)S(1)}, bf16[288,1152]{1,0:T(8,128)(2,1)}, u32[]{:S(2)}, u32[]{:S(2)}) collective-permute-start(bf16[288,1152]{1,0:T(8,128)(2,1)S(1)} %collective-permute-done.1.rest_2_), channel_id=1, source_target_pairs={{0,48},{48,0},{96,144},{144,96},{192,240},{240,192},{288,336},{336... | collective-permute-start | bytes 1990664 | tf_op jit(solution)/shard_map/ppermute | solution.py:229
  86.4 4.1 %collective-permute-start.6 = (bf16[288,1152]{1,0:T(8,128)(2,1)S(1)}, bf16[288,1152]{1,0:T(8,128)(2,1)}, u32[]{:S(2)}, u32[]{:S(2)}) collective-permute-start(bf16[288,1152]{1,0:T(8,128)(2,1)S(1)} %collective-permute-done.2.rest_3_), channel_id=1, source_target_pairs={{0,48},{48,0},{96,144},{144,96},{192,240},{240,192},{288,336},{336... | collective-permute-start | bytes 1990664 | tf_op jit(solution)/shard_map/ppermute | solution.py:229

commit v4 on v2

v4 whole, which is shorter than its diff:
```python
import jax
import jax.numpy as jnp
from jax import lax
from jax.experimental import pallas as pl
from jax.experimental.pallas import tpu as pltpu
from jax.sharding import PartitionSpec as P

TILE = 192
LANES = 128
NX, NZ = 4, 12


def in_hbm(array):
    return pltpu.with_memory_space_constraint(array, pltpu.HBM)


def pack_body(source, gathered, packed, wide):
    pairs, rows, width = source.shape
    peers = packed.shape[0]
    step = width // peers
    full = pairs * step // LANES
    wide[...] = source[...].astype(jnp.float32)
    lane = lax.broadcasted_iota(jnp.int32, (rows, LANES), 1)
    for q in range(peers):
        tile, at = divmod(step * q, LANES)
        made = [None] * (full + 2)
        beside = None
        for g in range(pairs):
            piece = wide[g, :, tile * LANES : (tile + 1) * LANES]
            if at + step > LANES:
                piece = jnp.where(lane >= at, piece, wide[g, :, (tile + 1) * LANES : (tile + 2) * LANES])
            put, to = divmod(step * g, LANES)
            over = step * (g + 1) - full * LANES
            if over > 0:
                first = LANES // 2 + over - step
                turned = pltpu.roll(piece[8:16], (first - at) % LANES, 1)
                beside = turned if beside is None else jnp.where(lane[:8] >= first, turned, beside)
            if to != at:
                piece = pltpu.roll(piece, (to - at) % LANES, 1)
            made[put] = piece if made[put] is None else jnp.where(lane >= to, piece, made[put])
            if to + step > LANES:
                made[put + 1] = piece
        low = jnp.where(lane[:8] < LANES // 2, made[full][:8], beside)
        packed[q] = jnp.concatenate(made[:full] + [low, made[full][16:]], axis=0).astype(jnp.bfloat16)


def pack(amplitudes, gathered, peers):
    pairs, rows, width = amplitudes.shape
    full = pairs * (width // peers) // LANES
    tall = full * rows + 16
    blocks = width // 384
    return pl.pallas_call(
        pack_body,
        grid=(blocks,),
        in_specs=[pl.BlockSpec((pairs, rows, 384), lambda p: (0, 0, p)), pl.BlockSpec(memory_space=pltpu.HBM)],
        out_specs=pl.BlockSpec((peers // blocks, tall, LANES), lambda p: (p, 0, 0)),
        out_shape=jax.ShapeDtypeStruct((peers, tall, LANES), jnp.bfloat16),
        scratch_shapes=[pltpu.VMEM((pairs, rows, 384), jnp.float32)],
        compiler_params=pltpu.CompilerParams(vmem_limit_bytes=12 << 20),
        name="pack",
    )(in_hbm(amplitudes), in_hbm(gathered))


def spread_body(mask, piece, mask_rows):
    count, _, width = mask_rows.shape
    tiles = width // TILE
    lane = lax.broadcasted_iota(jnp.int32, (16, width), 1)
    for t in range(count):
        row = jnp.zeros((16, width), jnp.float32)
        for u in range(tiles):
            inside = (lane >= u * TILE) & (lane < (u + 1) * TILE)
            row = jnp.where(inside, mask[t * tiles + u].astype(jnp.float32), row)
        mask_rows[t] = row.astype(jnp.bfloat16)


def spread(block_mask, piece, width):
    tiles = width // TILE
    count = block_mask.size // tiles
    return pl.pallas_call(
        spread_body,
        in_specs=[pl.BlockSpec(memory_space=pltpu.SMEM), pl.BlockSpec(memory_space=pltpu.HBM)],
        out_specs=pl.BlockSpec(memory_space=pltpu.VMEM),
        out_shape=pltpu.VMEM((count, 16, width), jnp.bfloat16),
        cost_estimate=pl.CostEstimate(flops=25 * 10**9, transcendentals=0, bytes_accessed=count * 32 * width),
        name="spread",
    )(block_mask.reshape(-1), in_hbm(piece))


def final_body(where, own, mask_rows, swapped, residual, *rest):
    pieces, (out, weights, start, combined, made, sems) = rest[:-6], rest[-6:]
    kept, width = weights.shape[0], weights.shape[1]
    tiles = width // TILE
    core, mine = where[0], where[1]
    half = pieces[0].shape[0]
    steps = len(pieces) // kept
    copies = []
    for side in range(kept):
        k = core if side == 0 else 1 - core
        for j in range(steps):
            base = pl.multiple_of(lax.rem(mine + jnp.where(k == 0, NX - j, j), NX) * half, 16)
            target = weights.at[side, pl.ds(base, half), :]
            copies.append(pltpu.make_async_copy(pieces[len(copies)], target, sems.at[len(copies)]))
    copies.append(pltpu.make_async_copy(residual, start, sems.at[len(copies)]))
    for copy in copies:
        copy.start()

    pairs = own.shape[0]
    peers, tall = swapped.shape[0], swapped.shape[1]
    rows = width // peers
    full = tall // rows
    for d in range(full + 1):
        count = min(LANES, pairs - d * LANES)
        if d < full:
            tile = swapped[:, d * rows : (d + 1) * rows, :].astype(jnp.float32)
        else:
            ends = swapped[:, d * rows :, :].astype(jnp.float32)
            low = ends[:, :8].reshape(peers * 8, LANES)
            middle = pltpu.roll(low, LANES // 2, 1).reshape(peers, 8, LANES)
            tile = jnp.concatenate([ends[:, :8], middle, ends[:, 8:]], axis=1)
        turned = jnp.transpose(tile.reshape(width, LANES))
        own_rows = own[d * LANES : d * LANES + count, :].astype(jnp.float32)
        combined[d * LANES : d * LANES + count, :] = (2.0 * own_rows - turned[:count]).astype(jnp.bfloat16)

    half_rows = pairs // kept
    wide = 384
    stores = []
    for side in range(kept):
        k = core if side == 0 else 1 - core
        for copy in copies[side * steps : (side + 1) * steps]:
            copy.wait()
        if side == kept - 1:
            copies[-1].wait()
        left = combined[pl.ds(pl.multiple_of(k * half_rows, 16), half_rows), :]
        for n in range(width // wide):
            cols = slice(n * wide, (n + 1) * wide)
            masked = jnp.concatenate(
                [
                    weights[side, t * TILE : (t + 1) * TILE, cols].reshape(-1, 16, wide)
                    * mask_rows[k * tiles + t, :, cols][None]
                    for t in range(tiles)
                ]
            ).reshape(width, wide)
            total = jnp.dot(left, masked, preferred_element_type=jnp.float32)
            if side == 0:
                made[:, cols] = total
            else:
                made[:, cols] = made[:, cols] + total + start[:, cols]
                stores.append(pltpu.make_async_copy(made.at[:, cols], out.at[:, cols], sems.at[len(copies) + n]))
                stores[-1].start()
    for store in stores:
        store.wait()


def final(where, own, mask_rows, swapped, residual, pieces, kept):
    width = residual.shape[1]
    vmem = pl.BlockSpec(memory_space=pltpu.VMEM)
    hbm = pl.BlockSpec(memory_space=pltpu.HBM)
    return pl.pallas_call(
        final_body,
        in_specs=[pl.BlockSpec(memory_space=pltpu.SMEM)] + [vmem] * 3 + [hbm] * (1 + len(pieces)),
        out_specs=hbm,
        out_shape=jax.ShapeDtypeStruct(residual.shape, jnp.float32),
        scratch_shapes=[
            pltpu.VMEM((kept, width, width), jnp.bfloat16),
            pltpu.VMEM(residual.shape, jnp.float32),
            pltpu.VMEM(own.shape, jnp.bfloat16),
            pltpu.VMEM(residual.shape, jnp.float32),
            pltpu.SemaphoreType.DMA((len(pieces) + 1 + width // 384,)),
        ],
        compiler_params=pltpu.CompilerParams(vmem_limit_bytes=20 << 20),
        name="final",
    )(where, own, mask_rows, swapped, in_hbm(residual), *[in_hbm(piece) for piece in pieces])


def per_device(amplitudes, integrals, block_mask, residual_in):
    kept, occ, rows, width = amplitudes.shape
    core = lax.rem(lax.axis_index("occ"), 2)
    column = lax.div(lax.axis_index("vir"), NZ)
    where = jnp.stack([core, column]).astype(jnp.int32)

    along = NX * NZ
    occ_axis = lax.axis_size("occ")
    slab = jnp.where(core == 0, integrals[0], integrals[1])
    groups = [[x * NZ + z for z in range(NZ)] for x in range(NX)]
    here = lax.all_gather(slab, "vir", axis=0, tiled=True, axis_index_groups=groups)

    packed = pack(amplitudes.reshape(kept * occ, rows, width), here, width // rows)
    swapped = lax.all_to_all(packed, "vir", 0, 0, tiled=True)

    ring = [
        (o * along + v, o * along + (v + (NZ if o % 2 == 0 else -NZ)) % along) for o in range(occ_axis) for v in range(along)
    ]
    pieces = [here]
    for _ in range(NX - 1):
        pieces.append(lax.ppermute(pieces[-1], ("occ", "vir"), ring))
    mask_rows = spread(block_mask, pieces[1][:16, :LANES], width)
    swap_cores = [(j, j ^ 1) for j in range(occ_axis)]
    pieces += [lax.ppermute(piece, "occ", swap_cores) for piece in pieces]

    out = final(
        where,
        amplitudes.reshape(kept * occ * rows, width),
        mask_rows,
        swapped,
        residual_in.reshape(occ * rows, width),
        pieces,
        kept,
    )
    return out.reshape(residual_in.shape)


def solution(mesh):
    return jax.shard_map(
        per_device,
        mesh=mesh,
        in_specs=(P(None, "occ", "vir", None), P(None, "vir", None), P(), P("occ", "vir", None)),
        out_specs=P("occ", "vir", None),
        check_vma=False,
    )
```

time: 107 us -> 106 us (level)
  starting transfers between devices: 28.3 us -> 22 us
  waiting for transfers between devices: 26.6 us -> 31.7 us
  Pallas kernels: 13.4 us -> 11 us
  blocking collectives: 36.2 us -> 38 us
  local copies, waits for them, and re-layouts: 0.14 us -> 1.91 us
    all_to_all x1, waiting for transfers between devices: 0.01 us -> 9.15 us  [per_device(): swapped = lax.all_to_all(packed, 'vir', 0, 0, tiled=True)]
    ppermute x4 -> x3, starting transfers between devices: 11.7 us -> 6.48 us  [per_device(): pieces.append(lax.ppermute(pieces[-1], ('occ', 'vir'), ring))]
    ppermute x4 -> x3, waiting for transfers between devices: 24.9 us -> 20.9 us  [per_device(): pieces.append(lax.ppermute(pieces[-1], ('occ', 'vir'), ring))]
    pallas_call x1, Pallas kernels: 6.55 us -> 4.31 us  [pack(): pl.pallas_call(pack_body, grid=(blocks,), in_specs=[pl.BlockSpec((pairs,...]
    ppermute x5 -> x4, starting transfers between devices: 10.1 us -> 8.27 us  [per_device(): pieces += [lax.ppermute(piece, 'occ', swap_cores) for piece in pieces]]
    all_gather x1, blocking collectives: 36.2 us -> 38 us  [per_device(): lax.all_gather(slab, 'vir', axis=0, tiled=True, axis_index_groups=groups)]
    slice x2 -> x1, local copies, waits for them, and re-layouts: 0.05 us -> 1.28 us  [per_device(): mask_rows = spread(block_mask, pieces[1][:16, :LANES], width)]
    pallas_call x1 -> x2, Pallas kernels: 6.86 us -> 6.65 us  [the longest x1 5.95 us: final(): pl.pallas_call(final_body, in_specs=[pl.BlockSpec(memory_space=pltpu.SMEM...]
  transfers between devices with their start and end apart: 10 -> 8, of which waited for: 3 -> 5; matrix products, arithmetic and copies ran while one was open for 0% -> 2% of each run, Pallas kernels for 0% -> 5%
where the time goes in v4:
time: 106 us
  blocking collectives  38 us (36%)
  waiting for transfers between devices  31.7 us (30%)
  starting transfers between devices  22 us (21%)
  Pallas kernels  11 us (10%)
  local copies, waits for them, and re-layouts  1.91 us (2%)
    all_gather x1, blocking collectives, per_device(): lax.all_gather(slab, 'vir', axis=0, tiled=True, axis_index_groups=groups)  38 us
    ppermute x3, waiting for transfers between devices, per_device(): pieces.append(lax.ppermute(pieces[-1], ('occ', 'vir'), ring))  20.9 us
    all_to_all x1, waiting for transfers between devices, per_device(): swapped = lax.all_to_all(packed, 'vir', 0, 0, tiled=True)  9.15 us
    ppermute x4, starting transfers between devices, per_device(): pieces += [lax.ppermute(piece, 'occ', swap_cores) for piece in pieces]  8.27 us
    all_to_all x1, starting transfers between devices, per_device(): swapped = lax.all_to_all(packed, 'vir', 0, 0, tiled=True)  7.23 us
    ppermute x3, starting transfers between devices, per_device(): pieces.append(lax.ppermute(pieces[-1], ('occ', 'vir'), ring))  6.48 us
    pallas_call x1, Pallas kernels, final(): pl.pallas_call(final_body, in_specs=[pl.BlockSpec(memory_space=pltpu.SMEM...  5.95 us
    pallas_call x1, Pallas kernels, pack(): pl.pallas_call(pack_body, grid=(blocks,), in_specs=[pl.BlockSpec((pairs,...  4.31 us
  transfers between devices with their start and end apart: 8, of which 5 were waited for; matrix products, arithmetic and copies ran while one was open for 2% of the time, Pallas kernels for 5%

profile of v4, /device:TPU:6, one launch (start us, length us, event | category | flops | bytes accessed | tf_op | source)
XLA Modules:
  0.0 105.6 jit_solution(3006566263564909099)
XLA Ops:
  0.0 0.8 slice_select_fusion
  0.9 38.0 %all-gather = bf16[1,288,1152]{2,1,0:T(8,128)(2,1)} all-gather(bf16[1,24,1152]{2,1,0:T(8,128)(2,1)S(1)} %slice_select_fusion), channel_id=2, replica_groups={{0,1,2,3,4,5,6,7,8,9,10,11},{12,13,14,15,16,17,18,19,20,21,22,23},{24,2..., dimensions={1}, use_global_device_ids=true | all-gather | bytes 718848 | tf_op jit(solution)/shard_map/all_gather | solution.py:185
  38.8 2.4 %collective-permute-start = (bf16[288,1152]{1,0:T(8,128)(2,1)}, bf16[288,1152]{1,0:T(8,128)(2,1)}, u32[]{:S(2)}, u32[]{:S(2)}) collective-permute-start(bf16[288,1152]{1,0:T(8,128)(2,1)} %bitcast.3.gathered.rest_0_), channel_id=1, source_target_pairs={{0,12},{1,13},{2,14},{3,15},{4,16},{5,17},{6,18},{7,19},{8,20},{9,... | collective-permute-start | bytes 1990664 | tf_op jit(solution)/shard_map/ppermute | solution.py:195
  41.2 4.3 %pack.1 = bf16[48,112,128]{2,1,0:T(8,128)(2,1)} custom-call(bf16[24,24,1152]{2,1,0:T(8,128)(2,1)} %bitcast.7, bf16[288,1152]{1,0:T(8,128)(2,1)} %bitcast.3.gathered.rest_0_), custom_call_target="tpu_custom_call" | custom-call | tf_op jit(solution)/shard_map/pack/pallas_call | solution.py:52
  45.5 0.0 copy-start.1
  45.5 7.2 %all-to-all-start = ((bf16[48,112,128]{2,1,0:T(8,128)(2,1)}), bf16[48,112,128]{2,1,0:T(8,128)(2,1)S(1)}, u32[]{:S(2)}, u32[]{:S(2)}) async-start(bf16[48,112,128]{2,1,0:T(8,128)(2,1)} %pack.1), calls=%async_computation | async-start | bytes 2752512 | tf_op jit(solution)/shard_map/all_to_all | solution.py:188
  52.8 1.9 %collective-permute-done.rest_1_ = bf16[288,1152]{1,0:T(8,128)(2,1)} collective-permute-done((bf16[288,1152]{1,0:T(8,128)(2,1)}, bf16[288,1152]{1,0:T(8,128)(2,1)}, u32[]{:S(2)}, u32[]{:S(2)}) %collective-permute-start) | collective-permute-done | bytes 663584 | tf_op jit(solution)/shard_map/ppermute | solution.py:195
  54.7 1.9 %collective-permute-start.1 = (bf16[288,1152]{1,0:T(8,128)(2,1)}, bf16[288,1152]{1,0:T(8,128)(2,1)}, u32[]{:S(2)}, u32[]{:S(2)}) collective-permute-start(bf16[288,1152]{1,0:T(8,128)(2,1)} %collective-permute-done.rest_1_), channel_id=1, source_target_pairs={{0,12},{1,13},{2,14},{3,15},{4,16},{5,17},{6,18},{7,19},{8,20},{9,... | collective-permute-start | bytes 1990664 | tf_op jit(solution)/shard_map/ppermute | solution.py:195
  56.6 14.8 %collective-permute-done.1.rest_2_ = bf16[288,1152]{1,0:T(8,128)(2,1)} collective-permute-done((bf16[288,1152]{1,0:T(8,128)(2,1)}, bf16[288,1152]{1,0:T(8,128)(2,1)}, u32[]{:S(2)}, u32[]{:S(2)}) %collective-permute-start.1) | collective-permute-done | bytes 663584 | tf_op jit(solution)/shard_map/ppermute | solution.py:195
  71.4 2.2 %collective-permute-start.2 = (bf16[288,1152]{1,0:T(8,128)(2,1)}, bf16[288,1152]{1,0:T(8,128)(2,1)}, u32[]{:S(2)}, u32[]{:S(2)}) collective-permute-start(bf16[288,1152]{1,0:T(8,128)(2,1)} %collective-permute-done.1.rest_2_), channel_id=1, source_target_pairs={{0,12},{1,13},{2,14},{3,15},{4,16},{5,17},{6,18},{7,19},{8,20},{9,... | collective-permute-start | bytes 1990664 | tf_op jit(solution)/shard_map/ppermute | solution.py:195
  73.6 1.9 %collective-permute-start.3 = (bf16[288,1152]{1,0:T(8,128)(2,1)}, bf16[288,1152]{1,0:T(8,128)(2,1)}, u32[]{:S(2)}, u32[]{:S(2)}) collective-permute-start(bf16[288,1152]{1,0:T(8,128)(2,1)} %bitcast.3.gathered.rest_0_), channel_id=1, source_target_pairs={{0,48},{48,0},{96,144},{144,96},{192,240},{240,192},{288,336},{336... | collective-permute-start | bytes 1990664 | tf_op jit(solution)/shard_map/ppermute | solution.py:198
  75.6 0.0 copy-done.1
  75.6 0.6 reshape.18.mask
  76.2 0.1 pad_add_fusion.where
  76.3 2.4 %collective-permute-start.4 = (bf16[288,1152]{1,0:T(8,128)(2,1)}, bf16[288,1152]{1,0:T(8,128)(2,1)}, u32[]{:S(2)}, u32[]{:S(2)}) collective-permute-start(bf16[288,1152]{1,0:T(8,128)(2,1)} %collective-permute-done.rest_1_), channel_id=1, source_target_pairs={{0,48},{48,0},{96,144},{144,96},{192,240},{240,192},{288,336},{336... | collective-permute-start | bytes 1990664 | tf_op jit(solution)/shard_map/ppermute | solution.py:198
  78.7 1.3 %slice.12.piece = bf16[16,128]{1,0:T(8,128)(2,1)} slice(bf16[288,1152]{1,0:T(8,128)(2,1)} %collective-permute-done.rest_1_), slice={[0:16], [0:128]} | slice | bytes 8192 | tf_op jit(solution)/shard_map/slice | solution.py:196
  80.0 0.0 copy-start
  80.0 2.0 %collective-permute-start.5 = (bf16[288,1152]{1,0:T(8,128)(2,1)}, bf16[288,1152]{1,0:T(8,128)(2,1)}, u32[]{:S(2)}, u32[]{:S(2)}) collective-permute-start(bf16[288,1152]{1,0:T(8,128)(2,1)} %collective-permute-done.1.rest_2_), channel_id=1, source_target_pairs={{0,48},{48,0},{96,144},{144,96},{192,240},{240,192},{288,336},{336... | collective-permute-start | bytes 1990664 | tf_op jit(solution)/shard_map/ppermute | solution.py:198
  82.0 4.1 %collective-permute-done.2.rest_3_ = bf16[288,1152]{1,0:T(8,128)(2,1)} collective-permute-done((bf16[288,1152]{1,0:T(8,128)(2,1)}, bf16[288,1152]{1,0:T(8,128)(2,1)}, u32[]{:S(2)}, u32[]{:S(2)}) %collective-permute-start.2) | collective-permute-done | bytes 663584 | tf_op jit(solution)/shard_map/ppermute | solution.py:195
  86.2 1.9 %collective-permute-start.6 = (bf16[288,1152]{1,0:T(8,128)(2,1)}, bf16[288,1152]{1,0:T(8,128)(2,1)}, u32[]{:S(2)}, u32[]{:S(2)}) collective-permute-start(bf16[288,1152]{1,0:T(8,128)(2,1)} %collective-permute-done.2.rest_3_), channel_id=1, source_target_pairs={{0,48},{48,0},{96,144},{144,96},{192,240},{240,192},{288,336},{336... | collective-permute-start | bytes 1990664 | tf_op jit(solution)/shard_map/ppermute | solution.py:198
  88.1 0.7 spread.1.mask_rows
  88.8 0.0 collective-permute-done.3.rest_4_
  88.8 0.0 collective-permute-done.4.rest_5_
  88.8 0.0 collective-permute-done.5.rest_6_
  88.8 1.7 %collective-permute-done.6.rest_7_ = bf16[288,1152]{1,0:T(8,128)(2,1)} collective-permute-done((bf16[288,1152]{1,0:T(8,128)(2,1)}, bf16[288,1152]{1,0:T(8,128)(2,1)}, u32[]{:S(2)}, u32[]{:S(2)}) %collective-permute-start.6) | collective-permute-done | bytes 663584 | tf_op jit(solution)/shard_map/ppermute | solution.py:198
  90.5 9.2 %all-to-all-done.swapped = bf16[48,112,128]{2,1,0:T(8,128)(2,1)S(1)} async-done(((bf16[48,112,128]{2,1,0:T(8,128)(2,1)}), bf16[48,112,128]{2,1,0:T(8,128)(2,1)S(1)}, u32[]{:S(2)}, u32[]{:S(2)}) %all-to-all-start) | async-done | bytes 1376288 | tf_op jit(solution)/shard_map/all_to_all | solution.py:188
  99.7 0.0 copy-done
  99.7 5.9 %final.1 = f32[288,1152]{1,0:T(8,128)} custom-call(s32[2]{0:T(128)S(1)} %pad_add_fusion.where, bf16[576,1152]{1,0:T(8,128)(2,1)S(1)} %bitcast.8, bf16[12,16,1152]{2,1,0:T(8,128)(2,1)S(1)} %spread.1.mask_rows, bf16[48,112,128]{2,1,0:T(8,128)(2,1)S(1)} %all-to-all-done.swapped, f32[288,1152]{1,0:T(8,128)} %bitcast.9, ...), custom_call_target="tpu_custom_call" | custom-call | tf_op jit(solution)/shard_map/final/pallas_call | solution.py:158
  (1 shorter events, 0.0 us)
Async XLA Ops:
  38.8 15.9 %collective-permute-start = (bf16[288,1152]{1,0:T(8,128)(2,1)}, bf16[288,1152]{1,0:T(8,128)(2,1)}, u32[]{:S(2)}, u32[]{:S(2)}) collective-permute-start(bf16[288,1152]{1,0:T(8,128)(2,1)} %bitcast.3.gathered.rest_0_), channel_id=1, source_target_pairs={{0,12},{1,13},{2,14},{3,15},{4,16},{5,17},{6,18},{7,19},{8,20},{9,... | collective-permute-start | bytes 1990664 | tf_op jit(solution)/shard_map/ppermute | solution.py:195
  45.5 30.1 %copy-start.1 = (s32[2,6,6]{2,0,1:T(2,128)S(1)}, s32[2,6,6]{2,0,1:T(2,128)}, u32[]{:S(2)}) copy-start(s32[2,6,6]{2,0,1:T(2,128)} %param.6) | copy-start | bytes 868
  45.5 54.1 %all-to-all-start = ((bf16[48,112,128]{2,1,0:T(8,128)(2,1)}), bf16[48,112,128]{2,1,0:T(8,128)(2,1)S(1)}, u32[]{:S(2)}, u32[]{:S(2)}) async-start(bf16[48,112,128]{2,1,0:T(8,128)(2,1)} %pack.1), calls=%async_computation | async-start | bytes 2752512 | tf_op jit(solution)/shard_map/all_to_all | solution.py:188
  54.7 16.8 %collective-permute-start.1 = (bf16[288,1152]{1,0:T(8,128)(2,1)}, bf16[288,1152]{1,0:T(8,128)(2,1)}, u32[]{:S(2)}, u32[]{:S(2)}) collective-permute-start(bf16[288,1152]{1,0:T(8,128)(2,1)} %collective-permute-done.rest_1_), channel_id=1, source_target_pairs={{0,12},{1,13},{2,14},{3,15},{4,16},{5,17},{6,18},{7,19},{8,20},{9,... | collective-permute-start | bytes 1990664 | tf_op jit(solution)/shard_map/ppermute | solution.py:195
  71.4 14.7 %collective-permute-start.2 = (bf16[288,1152]{1,0:T(8,128)(2,1)}, bf16[288,1152]{1,0:T(8,128)(2,1)}, u32[]{:S(2)}, u32[]{:S(2)}) collective-permute-start(bf16[288,1152]{1,0:T(8,128)(2,1)} %collective-permute-done.1.rest_2_), channel_id=1, source_target_pairs={{0,12},{1,13},{2,14},{3,15},{4,16},{5,17},{6,18},{7,19},{8,20},{9,... | collective-permute-start | bytes 1990664 | tf_op jit(solution)/shard_map/ppermute | solution.py:195
  73.6 15.2 %collective-permute-start.3 = (bf16[288,1152]{1,0:T(8,128)(2,1)}, bf16[288,1152]{1,0:T(8,128)(2,1)}, u32[]{:S(2)}, u32[]{:S(2)}) collective-permute-start(bf16[288,1152]{1,0:T(8,128)(2,1)} %bitcast.3.gathered.rest_0_), channel_id=1, source_target_pairs={{0,48},{48,0},{96,144},{144,96},{192,240},{240,192},{288,336},{336... | collective-permute-start | bytes 1990664 | tf_op jit(solution)/shard_map/ppermute | solution.py:198
  76.3 12.5 %collective-permute-start.4 = (bf16[288,1152]{1,0:T(8,128)(2,1)}, bf16[288,1152]{1,0:T(8,128)(2,1)}, u32[]{:S(2)}, u32[]{:S(2)}) collective-permute-start(bf16[288,1152]{1,0:T(8,128)(2,1)} %collective-permute-done.rest_1_), channel_id=1, source_target_pairs={{0,48},{48,0},{96,144},{144,96},{192,240},{240,192},{288,336},{336... | collective-permute-start | bytes 1990664 | tf_op jit(solution)/shard_map/ppermute | solution.py:198
  80.0 19.7 %copy-start = (bf16[2,12,24,1152]{3,2,1,0:T(8,128)(2,1)S(1)}, bf16[2,12,24,1152]{3,2,1,0:T(8,128)(2,1)}, u32[]{:S(2)}) copy-start(bf16[2,12,24,1152]{3,2,1,0:T(8,128)(2,1)} %param.4) | copy-start | bytes 3981316
  80.0 8.8 %collective-permute-start.5 = (bf16[288,1152]{1,0:T(8,128)(2,1)}, bf16[288,1152]{1,0:T(8,128)(2,1)}, u32[]{:S(2)}, u32[]{:S(2)}) collective-permute-start(bf16[288,1152]{1,0:T(8,128)(2,1)} %collective-permute-done.1.rest_2_), channel_id=1, source_target_pairs={{0,48},{48,0},{96,144},{144,96},{192,240},{240,192},{288,336},{336... | collective-permute-start | bytes 1990664 | tf_op jit(solution)/shard_map/ppermute | solution.py:198
  86.2 4.3 %collective-permute-start.6 = (bf16[288,1152]{1,0:T(8,128)(2,1)}, bf16[288,1152]{1,0:T(8,128)(2,1)}, u32[]{:S(2)}, u32[]{:S(2)}) collective-permute-start(bf16[288,1152]{1,0:T(8,128)(2,1)} %collective-permute-done.2.rest_3_), channel_id=1, source_target_pairs={{0,48},{48,0},{96,144},{144,96},{192,240},{240,192},{288,336},{336... | collective-permute-start | bytes 1990664 | tf_op jit(solution)/shard_map/ppermute | solution.py:198

commit v5 on v4

--- a/solution.py
+++ b/solution.py
@@ -81,7 +81,7 @@
         in_specs=[pl.BlockSpec(memory_space=pltpu.SMEM), pl.BlockSpec(memory_space=pltpu.HBM)],
         out_specs=pl.BlockSpec(memory_space=pltpu.VMEM),
         out_shape=pltpu.VMEM((count, 16, width), jnp.bfloat16),
-        cost_estimate=pl.CostEstimate(flops=25 * 10**9, transcendentals=0, bytes_accessed=count * 32 * width),
+        cost_estimate=pl.CostEstimate(flops=0, transcendentals=0, bytes_accessed=count * 32 * width),
         name="spread",
     )(block_mask.reshape(-1), in_hbm(piece))
 
@@ -93,22 +93,36 @@
     core, mine = where[0], where[1]
     half = pieces[0].shape[0]
     steps = len(pieces) // kept
-    copies = []
-    for side in range(kept):
+    def load(side, j):
         k = core if side == 0 else 1 - core
-        for j in range(steps):
-            base = pl.multiple_of(lax.rem(mine + jnp.where(k == 0, NX - j, j), NX) * half, 16)
-            target = weights.at[side, pl.ds(base, half), :]
-            copies.append(pltpu.make_async_copy(pieces[len(copies)], target, sems.at[len(copies)]))
-    copies.append(pltpu.make_async_copy(residual, start, sems.at[len(copies)]))
-    for copy in copies:
-        copy.start()
+        base = pl.multiple_of(lax.rem(mine + jnp.where(k == 0, NX - j, j), NX) * half, 16)
+        target = weights.at[k, pl.ds(base, half), :]
+        return pltpu.make_async_copy(pieces[side * steps + j], target, sems.at[k * steps + j])
+
+    @pl.when(core == 0)
+    def _():
+        for side in range(kept):
+            for j in range(steps):
+                load(side, j).start()
+
+    @pl.when(core != 0)
+    def _():
+        for side in reversed(range(kept)):
+            for j in range(steps):
+                load(side, j).start()
+
+    rest_load = pltpu.make_async_copy(residual, start, sems.at[kept * steps])
+    rest_load.start()
 
     pairs = own.shape[0]
     peers, tall = swapped.shape[0], swapped.shape[1]
     rows = width // peers
     full = tall // rows
-    for d in range(full + 1):
+    half_rows = pairs // kept
+    wide = 384
+    stores = []
+
+    def combine(d):
         count = min(LANES, pairs - d * LANES)
         if d < full:
             tile = swapped[:, d * rows : (d + 1) * rows, :].astype(jnp.float32)
@@ -121,31 +135,34 @@
         own_rows = own[d * LANES : d * LANES + count, :].astype(jnp.float32)
         combined[d * LANES : d * LANES + count, :] = (2.0 * own_rows - turned[:count]).astype(jnp.bfloat16)
 
-    half_rows = pairs // kept
-    wide = 384
-    stores = []
-    for side in range(kept):
-        k = core if side == 0 else 1 - core
-        for copy in copies[side * steps : (side + 1) * steps]:
-            copy.wait()
-        if side == kept - 1:
-            copies[-1].wait()
-        left = combined[pl.ds(pl.multiple_of(k * half_rows, 16), half_rows), :]
+    ready = 0
+    for k in range(kept):
+        while ready * LANES < (k + 1) * half_rows:
+            combine(ready)
+            ready += 1
+        for j in range(steps):
+            pltpu.make_async_copy(
+                pieces[0], weights.at[k, pl.ds(j * half, half), :], sems.at[k * steps + j]
+            ).wait()
+        if k == kept - 1:
+            rest_load.wait()
         for n in range(width // wide):
             cols = slice(n * wide, (n + 1) * wide)
             masked = jnp.concatenate(
                 [
-                    weights[side, t * TILE : (t + 1) * TILE, cols].reshape(-1, 16, wide)
+                    weights[k, t * TILE : (t + 1) * TILE, cols].reshape(-1, 16, wide)
                     * mask_rows[k * tiles + t, :, cols][None]
                     for t in range(tiles)
                 ]
             ).reshape(width, wide)
-            total = jnp.dot(left, masked, preferred_element_type=jnp.float32)
-            if side == 0:
+            total = jnp.dot(
+                combined[k * half_rows : (k + 1) * half_rows, :], masked, preferred_element_type=jnp.float32
+            )
+            if k == 0:
                 made[:, cols] = total
             else:
                 made[:, cols] = made[:, cols] + total + start[:, cols]
-                stores.append(pltpu.make_async_copy(made.at[:, cols], out.at[:, cols], sems.at[len(copies) + n]))
+                stores.append(pltpu.make_async_copy(made.at[:, cols], out.at[:, cols], sems.at[kept * steps + 1 + n]))
                 stores[-1].start()
     for store in stores:
         store.wait()
@@ -187,12 +204,16 @@
     packed = pack(amplitudes.reshape(kept * occ, rows, width), here, width // rows)
     swapped = lax.all_to_all(packed, "vir", 0, 0, tiled=True)
 
-    ring = [
-        (o * along + v, o * along + (v + (NZ if o % 2 == 0 else -NZ)) % along) for o in range(occ_axis) for v in range(along)
-    ]
-    pieces = [here]
-    for _ in range(NX - 1):
-        pieces.append(lax.ppermute(pieces[-1], ("occ", "vir"), ring))
+    def neighbour(array, sign):
+        pairs = [
+            (o * along + v, o * along + (v + (NZ if o % 2 == 0 else -NZ) * sign) % along)
+            for o in range(occ_axis)
+            for v in range(along)
+        ]
+        return lax.ppermute(array, ("occ", "vir"), pairs)
+
+    first = neighbour(here, 1)
+    pieces = [here, first, neighbour(first, 1), neighbour(here, -1)]
     mask_rows = spread(block_mask, pieces[1][:16, :LANES], width)
     swap_cores = [(j, j ^ 1) for j in range(occ_axis)]
     pieces += [lax.ppermute(piece, "occ", swap_cores) for piece in pieces]

time: 106 us -> 103 us (0.972)
  waiting for transfers between devices: 31.7 us -> 25.1 us
  starting transfers between devices: 22 us -> 25.5 us
    all_to_all x1, waiting for transfers between devices: 9.15 us -> 4.63 us  [per_device(): swapped = lax.all_to_all(packed, 'vir', 0, 0, tiled=True)]
    ppermute x3, starting transfers between devices: 6.48 us -> 10.8 us  [neighbour(): return lax.ppermute(array, ('occ', 'vir'), pairs)]
    ppermute x4, waiting for transfers between devices: 1.68 us -> 0.01 us  [per_device(): pieces += [lax.ppermute(piece, 'occ', swap_cores) for piece in pieces]]
  transfers between devices with their start and end apart: 8 -> 8, of which waited for: 5 -> 3; matrix products, arithmetic and copies ran while one was open for 2% -> 2% of each run, Pallas kernels for 5% -> 1%
where the time goes in v5:
time: 103 us; the launch traced here: 102 us
  blocking collectives  38 us (37%)
  starting transfers between devices  25.5 us (25%)
  waiting for transfers between devices  25.1 us (24%)
  Pallas kernels  10.7 us (10%)
  local copies, waits for them, and re-layouts  1.89 us (2%)
    all_gather x1, blocking collectives, per_device(): lax.all_gather(slab, 'vir', axis=0, tiled=True, axis_index_groups=groups)  38 us
    ppermute x3, waiting for transfers between devices, neighbour(): return lax.ppermute(array, ('occ', 'vir'), pairs)  20.5 us
    ppermute x3, starting transfers between devices, neighbour(): return lax.ppermute(array, ('occ', 'vir'), pairs)  10.8 us
    ppermute x4, starting transfers between devices, per_device(): pieces += [lax.ppermute(piece, 'occ', swap_cores) for piece in pieces]  8.16 us
    all_to_all x1, starting transfers between devices, per_device(): swapped = lax.all_to_all(packed, 'vir', 0, 0, tiled=True)  6.51 us
    pallas_call x1, Pallas kernels, final(): pl.pallas_call(final_body, in_specs=[pl.BlockSpec(memory_space=pltpu.SMEM...  5.7 us
    all_to_all x1, waiting for transfers between devices, per_device(): swapped = lax.all_to_all(packed, 'vir', 0, 0, tiled=True)  4.63 us
    pallas_call x1, Pallas kernels, pack(): pl.pallas_call(pack_body, grid=(blocks,), in_specs=[pl.BlockSpec((pairs,...  4.3 us
  transfers between devices with their start and end apart: 8, of which 3 were waited for; matrix products, arithmetic and copies ran while one was open for 2% of the time, Pallas kernels for 1%

profile of v5, /device:TPU:6, one launch (start us, length us, event | category | flops | bytes accessed | tf_op | source)
XLA Modules:
  0.0 102.3 jit_solution(12581630115967234570)
XLA Ops:
  0.0 0.8 slice_select_fusion
  0.9 38.0 %all-gather = bf16[1,288,1152]{2,1,0:T(8,128)(2,1)} all-gather(bf16[1,24,1152]{2,1,0:T(8,128)(2,1)S(1)} %slice_select_fusion), channel_id=2, replica_groups={{0,1,2,3,4,5,6,7,8,9,10,11},{12,13,14,15,16,17,18,19,20,21,22,23},{24,2..., dimensions={1}, use_global_device_ids=true | all-gather | bytes 718848 | tf_op jit(solution)/shard_map/all_gather | solution.py:202
  38.8 4.3 %pack.1 = bf16[48,112,128]{2,1,0:T(8,128)(2,1)} custom-call(bf16[24,24,1152]{2,1,0:T(8,128)(2,1)} %bitcast.7, bf16[288,1152]{1,0:T(8,128)(2,1)} %bitcast.3.gathered.rest_0_), custom_call_target="tpu_custom_call" | custom-call | tf_op jit(solution)/shard_map/pack/pallas_call | solution.py:52
  43.1 0.0 copy-start.1
  43.1 0.0 copy-start
  43.1 6.5 %all-to-all-start = ((bf16[48,112,128]{2,1,0:T(8,128)(2,1)}), bf16[48,112,128]{2,1,0:T(8,128)(2,1)S(1)}, u32[]{:S(2)}, u32[]{:S(2)}) async-start(bf16[48,112,128]{2,1,0:T(8,128)(2,1)} %pack.1), calls=%async_computation | async-start | bytes 2752512 | tf_op jit(solution)/shard_map/all_to_all | solution.py:205
  49.7 2.1 %collective-permute-start = (bf16[288,1152]{1,0:T(8,128)(2,1)}, bf16[288,1152]{1,0:T(8,128)(2,1)}, u32[]{:S(2)}, u32[]{:S(2)}) collective-permute-start(bf16[288,1152]{1,0:T(8,128)(2,1)} %bitcast.3.gathered.rest_0_), channel_id=1, source_target_pairs={{0,12},{1,13},{2,14},{3,15},{4,16},{5,17},{6,18},{7,19},{8,20},{9,... | collective-permute-start | bytes 1990664 | tf_op jit(solution)/shard_map/ppermute | solution.py:213
  51.8 3.7 %collective-permute-start.2 = (bf16[288,1152]{1,0:T(8,128)(2,1)}, bf16[288,1152]{1,0:T(8,128)(2,1)}, u32[]{:S(2)}, u32[]{:S(2)}) collective-permute-start(bf16[288,1152]{1,0:T(8,128)(2,1)} %bitcast.3.gathered.rest_0_), channel_id=1, source_target_pairs={{0,36},{1,37},{2,38},{3,39},{4,40},{5,41},{6,42},{7,43},{8,44},{9,... | collective-permute-start | bytes 1990664 | tf_op jit(solution)/shard_map/ppermute | solution.py:213
  55.5 17.6 %collective-permute-done.rest_1_ = bf16[288,1152]{1,0:T(8,128)(2,1)} collective-permute-done((bf16[288,1152]{1,0:T(8,128)(2,1)}, bf16[288,1152]{1,0:T(8,128)(2,1)}, u32[]{:S(2)}, u32[]{:S(2)}) %collective-permute-start) | collective-permute-done | bytes 663584 | tf_op jit(solution)/shard_map/ppermute | solution.py:213
  73.1 5.0 %collective-permute-start.1 = (bf16[288,1152]{1,0:T(8,128)(2,1)}, bf16[288,1152]{1,0:T(8,128)(2,1)}, u32[]{:S(2)}, u32[]{:S(2)}) collective-permute-start(bf16[288,1152]{1,0:T(8,128)(2,1)} %collective-permute-done.rest_1_), channel_id=1, source_target_pairs={{0,12},{1,13},{2,14},{3,15},{4,16},{5,17},{6,18},{7,19},{8,20},{9,... | collective-permute-start | bytes 1990664 | tf_op jit(solution)/shard_map/ppermute | solution.py:213
  78.1 1.9 %collective-permute-start.3 = (bf16[288,1152]{1,0:T(8,128)(2,1)}, bf16[288,1152]{1,0:T(8,128)(2,1)}, u32[]{:S(2)}, u32[]{:S(2)}) collective-permute-start(bf16[288,1152]{1,0:T(8,128)(2,1)} %bitcast.3.gathered.rest_0_), channel_id=1, source_target_pairs={{0,48},{48,0},{96,144},{144,96},{192,240},{240,192},{288,336},{336... | collective-permute-start | bytes 1990664 | tf_op jit(solution)/shard_map/ppermute | solution.py:219
  80.0 2.4 %collective-permute-start.4 = (bf16[288,1152]{1,0:T(8,128)(2,1)}, bf16[288,1152]{1,0:T(8,128)(2,1)}, u32[]{:S(2)}, u32[]{:S(2)}) collective-permute-start(bf16[288,1152]{1,0:T(8,128)(2,1)} %collective-permute-done.rest_1_), channel_id=1, source_target_pairs={{0,48},{48,0},{96,144},{144,96},{192,240},{240,192},{288,336},{336... | collective-permute-start | bytes 1990664 | tf_op jit(solution)/shard_map/ppermute | solution.py:219
  82.4 0.0 collective-permute-done.2.rest_3_
  82.5 1.9 %collective-permute-start.6 = (bf16[288,1152]{1,0:T(8,128)(2,1)}, bf16[288,1152]{1,0:T(8,128)(2,1)}, u32[]{:S(2)}, u32[]{:S(2)}) collective-permute-start(bf16[288,1152]{1,0:T(8,128)(2,1)} %collective-permute-done.2.rest_3_), channel_id=1, source_target_pairs={{0,48},{48,0},{96,144},{144,96},{192,240},{240,192},{288,336},{336... | collective-permute-start | bytes 1990664 | tf_op jit(solution)/shard_map/ppermute | solution.py:219
  84.4 2.9 %collective-permute-done.1.rest_2_ = bf16[288,1152]{1,0:T(8,128)(2,1)} collective-permute-done((bf16[288,1152]{1,0:T(8,128)(2,1)}, bf16[288,1152]{1,0:T(8,128)(2,1)}, u32[]{:S(2)}, u32[]{:S(2)}) %collective-permute-start.1) | collective-permute-done | bytes 663584 | tf_op jit(solution)/shard_map/ppermute | solution.py:213
  87.3 1.9 %collective-permute-start.5 = (bf16[288,1152]{1,0:T(8,128)(2,1)}, bf16[288,1152]{1,0:T(8,128)(2,1)}, u32[]{:S(2)}, u32[]{:S(2)}) collective-permute-start(bf16[288,1152]{1,0:T(8,128)(2,1)} %collective-permute-done.1.rest_2_), channel_id=1, source_target_pairs={{0,48},{48,0},{96,144},{144,96},{192,240},{240,192},{288,336},{336... | collective-permute-start | bytes 1990664 | tf_op jit(solution)/shard_map/ppermute | solution.py:219
  89.2 0.0 copy-done.1
  89.2 0.6 reshape.18.mask
  89.8 0.1 pad_add_fusion.where
  89.9 1.3 %slice.12.piece = bf16[16,128]{1,0:T(8,128)(2,1)} slice(bf16[288,1152]{1,0:T(8,128)(2,1)} %collective-permute-done.rest_1_), slice={[0:16], [0:128]} | slice | bytes 8192 | tf_op jit(solution)/shard_map/slice | solution.py:217
  91.2 0.7 spread.1.mask_rows
  91.9 0.0 collective-permute-done.3.rest_4_
  91.9 0.0 collective-permute-done.4.rest_5_
  91.9 0.0 collective-permute-done.6.rest_7_
  91.9 0.0 collective-permute-done.5.rest_6_
  91.9 4.6 %all-to-all-done.swapped = bf16[48,112,128]{2,1,0:T(8,128)(2,1)S(1)} async-done(((bf16[48,112,128]{2,1,0:T(8,128)(2,1)}), bf16[48,112,128]{2,1,0:T(8,128)(2,1)S(1)}, u32[]{:S(2)}, u32[]{:S(2)}) %all-to-all-start) | async-done | bytes 1376288 | tf_op jit(solution)/shard_map/all_to_all | solution.py:205
  96.6 0.0 copy-done
  96.6 5.7 %final.1 = f32[288,1152]{1,0:T(8,128)} custom-call(s32[2]{0:T(128)S(1)} %pad_add_fusion.where, bf16[576,1152]{1,0:T(8,128)(2,1)S(1)} %bitcast.8, bf16[12,16,1152]{2,1,0:T(8,128)(2,1)S(1)} %spread.1.mask_rows, bf16[48,112,128]{2,1,0:T(8,128)(2,1)S(1)} %all-to-all-done.swapped, f32[288,1152]{1,0:T(8,128)} %bitcast.9, ...), custom_call_target="tpu_custom_call" | custom-call | tf_op jit(solution)/shard_map/final/pallas_call | solution.py:175
  (1 shorter events, 0.0 us)
Async XLA Ops:
  43.1 46.1 %copy-start.1 = (s32[2,6,6]{2,0,1:T(2,128)S(1)}, s32[2,6,6]{2,0,1:T(2,128)}, u32[]{:S(2)}) copy-start(s32[2,6,6]{2,0,1:T(2,128)} %param.6) | copy-start | bytes 868
  43.1 53.4 %copy-start = (bf16[2,12,24,1152]{3,2,1,0:T(8,128)(2,1)S(1)}, bf16[2,12,24,1152]{3,2,1,0:T(8,128)(2,1)}, u32[]{:S(2)}) copy-start(bf16[2,12,24,1152]{3,2,1,0:T(8,128)(2,1)} %param.4) | copy-start | bytes 3981316
  43.1 53.4 %all-to-all-start = ((bf16[48,112,128]{2,1,0:T(8,128)(2,1)}), bf16[48,112,128]{2,1,0:T(8,128)(2,1)S(1)}, u32[]{:S(2)}, u32[]{:S(2)}) async-start(bf16[48,112,128]{2,1,0:T(8,128)(2,1)} %pack.1), calls=%async_computation | async-start | bytes 2752512 | tf_op jit(solution)/shard_map/all_to_all | solution.py:205
  49.7 23.5 %collective-permute-start = (bf16[288,1152]{1,0:T(8,128)(2,1)}, bf16[288,1152]{1,0:T(8,128)(2,1)}, u32[]{:S(2)}, u32[]{:S(2)}) collective-permute-start(bf16[288,1152]{1,0:T(8,128)(2,1)} %bitcast.3.gathered.rest_0_), channel_id=1, source_target_pairs={{0,12},{1,13},{2,14},{3,15},{4,16},{5,17},{6,18},{7,19},{8,20},{9,... | collective-permute-start | bytes 1990664 | tf_op jit(solution)/shard_map/ppermute | solution.py:213
  51.8 30.7 %collective-permute-start.2 = (bf16[288,1152]{1,0:T(8,128)(2,1)}, bf16[288,1152]{1,0:T(8,128)(2,1)}, u32[]{:S(2)}, u32[]{:S(2)}) collective-permute-start(bf16[288,1152]{1,0:T(8,128)(2,1)} %bitcast.3.gathered.rest_0_), channel_id=1, source_target_pairs={{0,36},{1,37},{2,38},{3,39},{4,40},{5,41},{6,42},{7,43},{8,44},{9,... | collective-permute-start | bytes 1990664 | tf_op jit(solution)/shard_map/ppermute | solution.py:213
  73.1 14.1 %collective-permute-start.1 = (bf16[288,1152]{1,0:T(8,128)(2,1)}, bf16[288,1152]{1,0:T(8,128)(2,1)}, u32[]{:S(2)}, u32[]{:S(2)}) collective-permute-start(bf16[288,1152]{1,0:T(8,128)(2,1)} %collective-permute-done.rest_1_), channel_id=1, source_target_pairs={{0,12},{1,13},{2,14},{3,15},{4,16},{5,17},{6,18},{7,19},{8,20},{9,... | collective-permute-start | bytes 1990664 | tf_op jit(solution)/shard_map/ppermute | solution.py:213
  78.1 13.8 %collective-permute-start.3 = (bf16[288,1152]{1,0:T(8,128)(2,1)}, bf16[288,1152]{1,0:T(8,128)(2,1)}, u32[]{:S(2)}, u32[]{:S(2)}) collective-permute-start(bf16[288,1152]{1,0:T(8,128)(2,1)} %bitcast.3.gathered.rest_0_), channel_id=1, source_target_pairs={{0,48},{48,0},{96,144},{144,96},{192,240},{240,192},{288,336},{336... | collective-permute-start | bytes 1990664 | tf_op jit(solution)/shard_map/ppermute | solution.py:219
  80.0 11.9 %collective-permute-start.4 = (bf16[288,1152]{1,0:T(8,128)(2,1)}, bf16[288,1152]{1,0:T(8,128)(2,1)}, u32[]{:S(2)}, u32[]{:S(2)}) collective-permute-start(bf16[288,1152]{1,0:T(8,128)(2,1)} %collective-permute-done.rest_1_), channel_id=1, source_target_pairs={{0,48},{48,0},{96,144},{144,96},{192,240},{240,192},{288,336},{336... | collective-permute-start | bytes 1990664 | tf_op jit(solution)/shard_map/ppermute | solution.py:219
  82.5 9.5 %collective-permute-start.6 = (bf16[288,1152]{1,0:T(8,128)(2,1)}, bf16[288,1152]{1,0:T(8,128)(2,1)}, u32[]{:S(2)}, u32[]{:S(2)}) collective-permute-start(bf16[288,1152]{1,0:T(8,128)(2,1)} %collective-permute-done.2.rest_3_), channel_id=1, source_target_pairs={{0,48},{48,0},{96,144},{144,96},{192,240},{240,192},{288,336},{336... | collective-permute-start | bytes 1990664 | tf_op jit(solution)/shard_map/ppermute | solution.py:219
  87.3 4.7 %collective-permute-start.5 = (bf16[288,1152]{1,0:T(8,128)(2,1)}, bf16[288,1152]{1,0:T(8,128)(2,1)}, u32[]{:S(2)}, u32[]{:S(2)}) collective-permute-start(bf16[288,1152]{1,0:T(8,128)(2,1)} %collective-permute-done.1.rest_2_), channel_id=1, source_target_pairs={{0,48},{48,0},{96,144},{144,96},{192,240},{240,192},{288,336},{336... | collective-permute-start | bytes 1990664 | tf_op jit(solution)/shard_map/ppermute | solution.py:219

commit v6 on v5

--- a/solution.py
+++ b/solution.py
@@ -61,33 +61,8 @@
     )(in_hbm(amplitudes), in_hbm(gathered))
 
 
-def spread_body(mask, piece, mask_rows):
-    count, _, width = mask_rows.shape
-    tiles = width // TILE
-    lane = lax.broadcasted_iota(jnp.int32, (16, width), 1)
-    for t in range(count):
-        row = jnp.zeros((16, width), jnp.float32)
-        for u in range(tiles):
-            inside = (lane >= u * TILE) & (lane < (u + 1) * TILE)
-            row = jnp.where(inside, mask[t * tiles + u].astype(jnp.float32), row)
-        mask_rows[t] = row.astype(jnp.bfloat16)
-
-
-def spread(block_mask, piece, width):
-    tiles = width // TILE
-    count = block_mask.size // tiles
-    return pl.pallas_call(
-        spread_body,
-        in_specs=[pl.BlockSpec(memory_space=pltpu.SMEM), pl.BlockSpec(memory_space=pltpu.HBM)],
-        out_specs=pl.BlockSpec(memory_space=pltpu.VMEM),
-        out_shape=pltpu.VMEM((count, 16, width), jnp.bfloat16),
-        cost_estimate=pl.CostEstimate(flops=0, transcendentals=0, bytes_accessed=count * 32 * width),
-        name="spread",
-    )(block_mask.reshape(-1), in_hbm(piece))
-
-
-def final_body(where, own, mask_rows, swapped, residual, *rest):
-    pieces, (out, weights, start, combined, made, sems) = rest[:-6], rest[-6:]
+def final_body(where, mask, own, swapped, residual, *rest):
+    pieces, (out, weights, start, combined, made, mask_rows, sems) = rest[:-7], rest[-7:]
     kept, width = weights.shape[0], weights.shape[1]
     tiles = width // TILE
     core, mine = where[0], where[1]
@@ -113,6 +88,14 @@
 
     rest_load = pltpu.make_async_copy(residual, start, sems.at[kept * steps])
     rest_load.start()
+
+    lane = lax.broadcasted_iota(jnp.int32, (16, width), 1)
+    for t in range(kept * tiles):
+        row = jnp.zeros((16, width), jnp.float32)
+        for u in range(tiles):
+            inside = (lane >= u * TILE) & (lane < (u + 1) * TILE)
+            row = jnp.where(inside, mask[t * tiles + u].astype(jnp.float32), row)
+        mask_rows[t] = row.astype(jnp.bfloat16)
 
     pairs = own.shape[0]
     peers, tall = swapped.shape[0], swapped.shape[1]
@@ -168,13 +151,14 @@
         store.wait()
 
 
-def final(where, own, mask_rows, swapped, residual, pieces, kept):
+def final(where, mask, own, swapped, residual, pieces, kept):
     width = residual.shape[1]
+    smem = pl.BlockSpec(memory_space=pltpu.SMEM)
     vmem = pl.BlockSpec(memory_space=pltpu.VMEM)
     hbm = pl.BlockSpec(memory_space=pltpu.HBM)
     return pl.pallas_call(
         final_body,
-        in_specs=[pl.BlockSpec(memory_space=pltpu.SMEM)] + [vmem] * 3 + [hbm] * (1 + len(pieces)),
+        in_specs=[smem] * 2 + [vmem] * 2 + [hbm] * (1 + len(pieces)),
         out_specs=hbm,
         out_shape=jax.ShapeDtypeStruct(residual.shape, jnp.float32),
         scratch_shapes=[
@@ -182,11 +166,12 @@
             pltpu.VMEM(residual.shape, jnp.float32),
             pltpu.VMEM(own.shape, jnp.bfloat16),
             pltpu.VMEM(residual.shape, jnp.float32),
+            pltpu.VMEM((kept * (width // TILE), 16, width), jnp.bfloat16),
             pltpu.SemaphoreType.DMA((len(pieces) + 1 + width // 384,)),
         ],
         compiler_params=pltpu.CompilerParams(vmem_limit_bytes=20 << 20),
         name="final",
-    )(where, own, mask_rows, swapped, in_hbm(residual), *[in_hbm(piece) for piece in pieces])
+    )(where, mask, own, swapped, in_hbm(residual), *[in_hbm(piece) for piece in pieces])
 
 
 def per_device(amplitudes, integrals, block_mask, residual_in):
@@ -213,15 +198,15 @@
         return lax.ppermute(array, ("occ", "vir"), pairs)
 
     first = neighbour(here, 1)
-    pieces = [here, first, neighbour(first, 1), neighbour(here, -1)]
-    mask_rows = spread(block_mask, pieces[1][:16, :LANES], width)
+    first, later = lax.optimization_barrier((first, here))
+    pieces = [here, first, neighbour(first, 1), neighbour(later, -1)]
     swap_cores = [(j, j ^ 1) for j in range(occ_axis)]
     pieces += [lax.ppermute(piece, "occ", swap_cores) for piece in pieces]
 
     out = final(
         where,
+        block_mask.reshape(-1),
         amplitudes.reshape(kept * occ * rows, width),
-        mask_rows,
         swapped,
         residual_in.reshape(occ * rows, width),
         pieces,

time: 103 us -> 103 us (level)
  waiting for transfers between devices: 25.1 us -> 30 us
  starting transfers between devices: 25.5 us -> 23.1 us
  local copies, waits for them, and re-layouts: 1.89 us -> 0.09 us
    ppermute x3, waiting for transfers between devices: 20.5 us -> 24 us  [neighbour(): return lax.ppermute(array, ('occ', 'vir'), pairs)]
    ppermute x3, starting transfers between devices: 10.8 us -> 7.96 us  [neighbour(): return lax.ppermute(array, ('occ', 'vir'), pairs)]
    ppermute x4, waiting for transfers between devices: 0.01 us -> 1.86 us  [per_device(): pieces += [lax.ppermute(piece, 'occ', swap_cores) for piece in pieces]]
    slice x1 -> x0, local copies, waits for them, and re-layouts: 1.27 us -> none  [per_device(): mask_rows = spread(block_mask, pieces[1][:16, :LANES], width)]
    pallas_call x2 -> x1, Pallas kernels: 6.4 us -> 5.68 us  [final(): pl.pallas_call(final_body, in_specs=[smem] * 2 + [vmem] * 2 + [hbm] * (1...]
  transfers between devices with their start and end apart: 8 -> 8, of which waited for: 3 -> 4; matrix products, arithmetic and copies ran while one was open for 2% -> 0% of each run, Pallas kernels for 1% -> 0%
where the time goes in v6:
time: 103 us; the launch traced here: 102 us
  blocking collectives  38 us (37%)
  waiting for transfers between devices  30 us (29%)
  starting transfers between devices  23.1 us (22%)
  Pallas kernels  9.99 us (10%)
    all_gather x1, blocking collectives, per_device(): lax.all_gather(slab, 'vir', axis=0, tiled=True, axis_index_groups=groups)  38 us
    ppermute x3, waiting for transfers between devices, neighbour(): return lax.ppermute(array, ('occ', 'vir'), pairs)  24 us
    ppermute x4, starting transfers between devices, per_device(): pieces += [lax.ppermute(piece, 'occ', swap_cores) for piece in pieces]  8.65 us
    ppermute x3, starting transfers between devices, neighbour(): return lax.ppermute(array, ('occ', 'vir'), pairs)  7.96 us
    all_to_all x1, starting transfers between devices, per_device(): swapped = lax.all_to_all(packed, 'vir', 0, 0, tiled=True)  6.52 us
    pallas_call x1, Pallas kernels, final(): pl.pallas_call(final_body, in_specs=[smem] * 2 + [vmem] * 2 + [hbm] * (1...  5.68 us
    pallas_call x1, Pallas kernels, pack(): pl.pallas_call(pack_body, grid=(blocks,), in_specs=[pl.BlockSpec((pairs,...  4.31 us
    all_to_all x1, waiting for transfers between devices, per_device(): swapped = lax.all_to_all(packed, 'vir', 0, 0, tiled=True)  4.21 us
  transfers between devices with their start and end apart: 8, of which 4 were waited for; matrix products, arithmetic and copies ran while one was open for 0% of the time, Pallas kernels for 0%

profile of v6, /device:TPU:6, one launch (start us, length us, event | category | flops | bytes accessed | tf_op | source)
XLA Modules:
  0.0 102.3 jit_solution(924705981267559872)
XLA Ops:
  0.0 0.8 slice_select_fusion
  0.9 38.0 %all-gather = bf16[1,288,1152]{2,1,0:T(8,128)(2,1)} all-gather(bf16[1,24,1152]{2,1,0:T(8,128)(2,1)S(1)} %slice_select_fusion), channel_id=2, replica_groups={{0,1,2,3,4,5,6,7,8,9,10,11},{12,13,14,15,16,17,18,19,20,21,22,23},{24,2..., dimensions={1}, use_global_device_ids=true | all-gather | bytes 718848 | tf_op jit(solution)/shard_map/all_gather | solution.py:187
  38.8 4.3 %pack.1 = bf16[48,112,128]{2,1,0:T(8,128)(2,1)} custom-call(bf16[24,24,1152]{2,1,0:T(8,128)(2,1)} %bitcast.7, bf16[288,1152]{1,0:T(8,128)(2,1)} %bitcast.9), custom_call_target="tpu_custom_call" | custom-call | tf_op jit(solution)/shard_map/pack/pallas_call | solution.py:52
  43.1 0.0 copy-start.1
  43.1 0.0 copy-start.2
  43.1 0.0 copy-start
  43.1 6.5 %all-to-all-start = ((bf16[48,112,128]{2,1,0:T(8,128)(2,1)}), bf16[48,112,128]{2,1,0:T(8,128)(2,1)S(1)}, u32[]{:S(2)}, u32[]{:S(2)}) async-start(bf16[48,112,128]{2,1,0:T(8,128)(2,1)} %pack.1), calls=%async_computation | async-start | bytes 2752512 | tf_op jit(solution)/shard_map/all_to_all | solution.py:190
  49.7 0.0 copy-done.1
  49.7 2.1 %collective-permute-start = (bf16[288,1152]{1,0:T(8,128)(2,1)S(1)}, bf16[288,1152]{1,0:T(8,128)(2,1)}, u32[]{:S(2)}, u32[]{:S(2)}) collective-permute-start(bf16[288,1152]{1,0:T(8,128)(2,1)S(1)} %bitcast.11), channel_id=1, source_target_pairs={{0,12},{1,13},{2,14},{3,15},{4,16},{5,17},{6,18},{7,19},{8,20},{9,... | collective-permute-start | bytes 1990664 | tf_op jit(solution)/shard_map/ppermute | solution.py:198
  51.8 13.8 %collective-permute-done.rest_1_ = bf16[288,1152]{1,0:T(8,128)(2,1)} collective-permute-done((bf16[288,1152]{1,0:T(8,128)(2,1)S(1)}, bf16[288,1152]{1,0:T(8,128)(2,1)}, u32[]{:S(2)}, u32[]{:S(2)}) %collective-permute-start) | collective-permute-done | bytes 663584 | tf_op jit(solution)/shard_map/ppermute | solution.py:198
  65.6 3.7 %collective-permute-start.1 = (bf16[288,1152]{1,0:T(8,128)(2,1)}, bf16[288,1152]{1,0:T(8,128)(2,1)}, u32[]{:S(2)}, u32[]{:S(2)}) collective-permute-start(bf16[288,1152]{1,0:T(8,128)(2,1)} %collective-permute-done.rest_1_), channel_id=1, source_target_pairs={{0,12},{1,13},{2,14},{3,15},{4,16},{5,17},{6,18},{7,19},{8,20},{9,... | collective-permute-start | bytes 1990664 | tf_op jit(solution)/shard_map/ppermute | solution.py:198
  69.3 2.2 %collective-permute-start.2 = (bf16[288,1152]{1,0:T(8,128)(2,1)S(1)}, bf16[288,1152]{1,0:T(8,128)(2,1)}, u32[]{:S(2)}, u32[]{:S(2)}) collective-permute-start(bf16[288,1152]{1,0:T(8,128)(2,1)S(1)} %bitcast.12), channel_id=1, source_target_pairs={{0,36},{1,37},{2,38},{3,39},{4,40},{5,41},{6,42},{7,43},{8,44},{9,... | collective-permute-start | bytes 1990664 | tf_op jit(solution)/shard_map/ppermute | solution.py:198
  71.4 1.9 %collective-permute-start.3 = (bf16[288,1152]{1,0:T(8,128)(2,1)S(1)}, bf16[288,1152]{1,0:T(8,128)(2,1)}, u32[]{:S(2)}, u32[]{:S(2)}) collective-permute-start(bf16[288,1152]{1,0:T(8,128)(2,1)S(1)} %bitcast.13), channel_id=1, source_target_pairs={{0,48},{48,0},{96,144},{144,96},{192,240},{240,192},{288,336},{336... | collective-permute-start | bytes 1990664 | tf_op jit(solution)/shard_map/ppermute | solution.py:204
  73.4 2.4 %collective-permute-start.4 = (bf16[288,1152]{1,0:T(8,128)(2,1)}, bf16[288,1152]{1,0:T(8,128)(2,1)}, u32[]{:S(2)}, u32[]{:S(2)}) collective-permute-start(bf16[288,1152]{1,0:T(8,128)(2,1)} %collective-permute-done.rest_1_), channel_id=1, source_target_pairs={{0,48},{48,0},{96,144},{144,96},{192,240},{240,192},{288,336},{336... | collective-permute-start | bytes 1990664 | tf_op jit(solution)/shard_map/ppermute | solution.py:204
  75.8 10.2 %collective-permute-done.1.rest_2_ = bf16[288,1152]{1,0:T(8,128)(2,1)} collective-permute-done((bf16[288,1152]{1,0:T(8,128)(2,1)}, bf16[288,1152]{1,0:T(8,128)(2,1)}, u32[]{:S(2)}, u32[]{:S(2)}) %collective-permute-start.1) | collective-permute-done | bytes 663584 | tf_op jit(solution)/shard_map/ppermute | solution.py:198
  86.0 1.9 %collective-permute-start.5 = (bf16[288,1152]{1,0:T(8,128)(2,1)}, bf16[288,1152]{1,0:T(8,128)(2,1)}, u32[]{:S(2)}, u32[]{:S(2)}) collective-permute-start(bf16[288,1152]{1,0:T(8,128)(2,1)} %collective-permute-done.1.rest_2_), channel_id=1, source_target_pairs={{0,48},{48,0},{96,144},{144,96},{192,240},{240,192},{288,336},{336... | collective-permute-start | bytes 1990664 | tf_op jit(solution)/shard_map/ppermute | solution.py:204
  87.9 0.0 collective-permute-done.2.rest_3_
  87.9 2.4 %collective-permute-start.6 = (bf16[288,1152]{1,0:T(8,128)(2,1)}, bf16[288,1152]{1,0:T(8,128)(2,1)}, u32[]{:S(2)}, u32[]{:S(2)}) collective-permute-start(bf16[288,1152]{1,0:T(8,128)(2,1)} %collective-permute-done.2.rest_3_), channel_id=1, source_target_pairs={{0,48},{48,0},{96,144},{144,96},{192,240},{240,192},{288,336},{336... | collective-permute-start | bytes 1990664 | tf_op jit(solution)/shard_map/ppermute | solution.py:204
  90.3 0.0 copy-done.2
  90.3 0.1 reshape.17.mask
  90.4 0.1 pad_add_fusion.where
  90.5 0.0 collective-permute-done.3.rest_4_
  90.5 0.0 collective-permute-done.4.rest_5_
  90.5 0.0 collective-permute-done.5.rest_6_
  90.5 1.8 %collective-permute-done.6.rest_7_ = bf16[288,1152]{1,0:T(8,128)(2,1)} collective-permute-done((bf16[288,1152]{1,0:T(8,128)(2,1)}, bf16[288,1152]{1,0:T(8,128)(2,1)}, u32[]{:S(2)}, u32[]{:S(2)}) %collective-permute-start.6) | collective-permute-done | bytes 663584 | tf_op jit(solution)/shard_map/ppermute | solution.py:204
  92.4 4.2 %all-to-all-done.swapped = bf16[48,112,128]{2,1,0:T(8,128)(2,1)S(1)} async-done(((bf16[48,112,128]{2,1,0:T(8,128)(2,1)}), bf16[48,112,128]{2,1,0:T(8,128)(2,1)S(1)}, u32[]{:S(2)}, u32[]{:S(2)}) %all-to-all-start) | async-done | bytes 1376288 | tf_op jit(solution)/shard_map/all_to_all | solution.py:190
  96.6 0.0 copy-done
  96.6 5.7 %final.1 = f32[288,1152]{1,0:T(8,128)} custom-call(s32[2]{0:T(128)S(1)} %pad_add_fusion.where, s32[72]{0:T(128)S(1)} %reshape.17.mask, bf16[576,1152]{1,0:T(8,128)(2,1)S(1)} %bitcast.8, bf16[48,112,128]{2,1,0:T(8,128)(2,1)S(1)} %all-to-all-done.swapped, f32[288,1152]{1,0:T(8,128)} %bitcast.14, bf16[288,1152]{1,0:T(8,128)(2,1)} %bitcast.10, ...), custom_call_target="tpu_custom_call" | custom-call | tf_op jit(solution)/shard_map/final/pallas_call | solution.py:159
  (1 shorter events, 0.0 us)
Async XLA Ops:
  43.1 6.5 %copy-start.1 = (bf16[1,288,1152]{2,1,0:T(8,128)(2,1)S(1)}, bf16[1,288,1152]{2,1,0:T(8,128)(2,1)}, u32[]{:S(2)}) copy-start(bf16[1,288,1152]{2,1,0:T(8,128)(2,1)} %all-gather) | copy-start | bytes 1990660
  43.1 47.2 %copy-start.2 = (s32[2,6,6]{2,0,1:T(2,128)S(1)}, s32[2,6,6]{2,0,1:T(2,128)}, u32[]{:S(2)}) copy-start(s32[2,6,6]{2,0,1:T(2,128)} %param.6) | copy-start | bytes 868
  43.1 53.4 %copy-start = (bf16[2,12,24,1152]{3,2,1,0:T(8,128)(2,1)S(1)}, bf16[2,12,24,1152]{3,2,1,0:T(8,128)(2,1)}, u32[]{:S(2)}) copy-start(bf16[2,12,24,1152]{3,2,1,0:T(8,128)(2,1)} %param.4) | copy-start | bytes 3981316
  43.1 53.4 %all-to-all-start = ((bf16[48,112,128]{2,1,0:T(8,128)(2,1)}), bf16[48,112,128]{2,1,0:T(8,128)(2,1)S(1)}, u32[]{:S(2)}, u32[]{:S(2)}) async-start(bf16[48,112,128]{2,1,0:T(8,128)(2,1)} %pack.1), calls=%async_computation | async-start | bytes 2752512 | tf_op jit(solution)/shard_map/all_to_all | solution.py:190
  49.7 15.9 %collective-permute-start = (bf16[288,1152]{1,0:T(8,128)(2,1)S(1)}, bf16[288,1152]{1,0:T(8,128)(2,1)}, u32[]{:S(2)}, u32[]{:S(2)}) collective-permute-start(bf16[288,1152]{1,0:T(8,128)(2,1)S(1)} %bitcast.11), channel_id=1, source_target_pairs={{0,12},{1,13},{2,14},{3,15},{4,16},{5,17},{6,18},{7,19},{8,20},{9,... | collective-permute-start | bytes 1990664 | tf_op jit(solution)/shard_map/ppermute | solution.py:198
  65.6 20.4 %collective-permute-start.1 = (bf16[288,1152]{1,0:T(8,128)(2,1)}, bf16[288,1152]{1,0:T(8,128)(2,1)}, u32[]{:S(2)}, u32[]{:S(2)}) collective-permute-start(bf16[288,1152]{1,0:T(8,128)(2,1)} %collective-permute-done.rest_1_), channel_id=1, source_target_pairs={{0,12},{1,13},{2,14},{3,15},{4,16},{5,17},{6,18},{7,19},{8,20},{9,... | collective-permute-start | bytes 1990664 | tf_op jit(solution)/shard_map/ppermute | solution.py:198
  69.3 18.6 %collective-permute-start.2 = (bf16[288,1152]{1,0:T(8,128)(2,1)S(1)}, bf16[288,1152]{1,0:T(8,128)(2,1)}, u32[]{:S(2)}, u32[]{:S(2)}) collective-permute-start(bf16[288,1152]{1,0:T(8,128)(2,1)S(1)} %bitcast.12), channel_id=1, source_target_pairs={{0,36},{1,37},{2,38},{3,39},{4,40},{5,41},{6,42},{7,43},{8,44},{9,... | collective-permute-start | bytes 1990664 | tf_op jit(solution)/shard_map/ppermute | solution.py:198
  71.4 19.1 %collective-permute-start.3 = (bf16[288,1152]{1,0:T(8,128)(2,1)S(1)}, bf16[288,1152]{1,0:T(8,128)(2,1)}, u32[]{:S(2)}, u32[]{:S(2)}) collective-permute-start(bf16[288,1152]{1,0:T(8,128)(2,1)S(1)} %bitcast.13), channel_id=1, source_target_pairs={{0,48},{48,0},{96,144},{144,96},{192,240},{240,192},{288,336},{336... | collective-permute-start | bytes 1990664 | tf_op jit(solution)/shard_map/ppermute | solution.py:204
  73.4 17.2 %collective-permute-start.4 = (bf16[288,1152]{1,0:T(8,128)(2,1)}, bf16[288,1152]{1,0:T(8,128)(2,1)}, u32[]{:S(2)}, u32[]{:S(2)}) collective-permute-start(bf16[288,1152]{1,0:T(8,128)(2,1)} %collective-permute-done.rest_1_), channel_id=1, source_target_pairs={{0,48},{48,0},{96,144},{144,96},{192,240},{240,192},{288,336},{336... | collective-permute-start | bytes 1990664 | tf_op jit(solution)/shard_map/ppermute | solution.py:204
  86.0 4.5 %collective-permute-start.5 = (bf16[288,1152]{1,0:T(8,128)(2,1)}, bf16[288,1152]{1,0:T(8,128)(2,1)}, u32[]{:S(2)}, u32[]{:S(2)}) collective-permute-start(bf16[288,1152]{1,0:T(8,128)(2,1)} %collective-permute-done.1.rest_2_), channel_id=1, source_target_pairs={{0,48},{48,0},{96,144},{144,96},{192,240},{240,192},{288,336},{336... | collective-permute-start | bytes 1990664 | tf_op jit(solution)/shard_map/ppermute | solution.py:204
  87.9 4.5 %collective-permute-start.6 = (bf16[288,1152]{1,0:T(8,128)(2,1)}, bf16[288,1152]{1,0:T(8,128)(2,1)}, u32[]{:S(2)}, u32[]{:S(2)}) collective-permute-start(bf16[288,1152]{1,0:T(8,128)(2,1)} %collective-permute-done.2.rest_3_), channel_id=1, source_target_pairs={{0,48},{48,0},{96,144},{144,96},{192,240},{240,192},{288,336},{336... | collective-permute-start | bytes 1990664 | tf_op jit(solution)/shard_map/ppermute | solution.py:204

commit v7 on v6

--- a/solution.py
+++ b/solution.py
@@ -65,14 +65,17 @@
     pieces, (out, weights, start, combined, made, mask_rows, sems) = rest[:-7], rest[-7:]
     kept, width = weights.shape[0], weights.shape[1]
     tiles = width // TILE
-    core, mine = where[0], where[1]
+    core, mine, half_at = where[0], where[1], where[2]
     half = pieces[0].shape[0]
     steps = len(pieces) // kept
     def load(side, j):
         k = core if side == 0 else 1 - core
-        base = pl.multiple_of(lax.rem(mine + jnp.where(k == 0, NX - j, j), NX) * half, 16)
-        target = weights.at[k, pl.ds(base, half), :]
-        return pltpu.make_async_copy(pieces[side * steps + j], target, sems.at[k * steps + j])
+        shift = min(j, NX - 1)
+        first = 0 if j < NX - 1 else (half_at if j == NX - 1 else 1 - half_at) * (half // 2)
+        base = lax.rem(mine + jnp.where(k == 0, NX - shift, shift), NX) * half + first
+        piece = pieces[side * steps + j]
+        target = weights.at[k, pl.ds(pl.multiple_of(base, 16), piece.shape[0]), :]
+        return pltpu.make_async_copy(piece, target, sems.at[k])
 
     @pl.when(core == 0)
     def _():
@@ -86,7 +89,7 @@
             for j in range(steps):
                 load(side, j).start()
 
-    rest_load = pltpu.make_async_copy(residual, start, sems.at[kept * steps])
+    rest_load = pltpu.make_async_copy(residual, start, sems.at[kept])
     rest_load.start()
 
     lane = lax.broadcasted_iota(jnp.int32, (16, width), 1)
@@ -123,10 +126,7 @@
         while ready * LANES < (k + 1) * half_rows:
             combine(ready)
             ready += 1
-        for j in range(steps):
-            pltpu.make_async_copy(
-                pieces[0], weights.at[k, pl.ds(j * half, half), :], sems.at[k * steps + j]
-            ).wait()
+        pltpu.make_async_copy(weights.at[k], weights.at[k], sems.at[k]).wait()
         if k == kept - 1:
             rest_load.wait()
         for n in range(width // wide):
@@ -145,7 +145,7 @@
                 made[:, cols] = total
             else:
                 made[:, cols] = made[:, cols] + total + start[:, cols]
-                stores.append(pltpu.make_async_copy(made.at[:, cols], out.at[:, cols], sems.at[kept * steps + 1 + n]))
+                stores.append(pltpu.make_async_copy(made.at[:, cols], out.at[:, cols], sems.at[kept + 1 + n]))
                 stores[-1].start()
     for store in stores:
         store.wait()
@@ -167,7 +167,7 @@
             pltpu.VMEM(own.shape, jnp.bfloat16),
             pltpu.VMEM(residual.shape, jnp.float32),
             pltpu.VMEM((kept * (width // TILE), 16, width), jnp.bfloat16),
-            pltpu.SemaphoreType.DMA((len(pieces) + 1 + width // 384,)),
+            pltpu.SemaphoreType.DMA((kept + 1 + width // 384,)),
         ],
         compiler_params=pltpu.CompilerParams(vmem_limit_bytes=20 << 20),
         name="final",
@@ -178,7 +178,8 @@
     kept, occ, rows, width = amplitudes.shape
     core = lax.rem(lax.axis_index("occ"), 2)
     column = lax.div(lax.axis_index("vir"), NZ)
-    where = jnp.stack([core, column]).astype(jnp.int32)
+    plane = lax.rem(lax.div(lax.axis_index("occ"), 2), 2)
+    where = jnp.stack([core, column, plane]).astype(jnp.int32)
 
     along = NX * NZ
     occ_axis = lax.axis_size("occ")
@@ -198,8 +199,11 @@
         return lax.ppermute(array, ("occ", "vir"), pairs)
 
     first = neighbour(here, 1)
-    first, later = lax.optimization_barrier((first, here))
-    pieces = [here, first, neighbour(first, 1), neighbour(later, -1)]
+    half = here.shape[0] // 2
+    near = neighbour(lax.dynamic_slice_in_dim(here, plane * half, half, 0), -1)
+    first, near = lax.optimization_barrier((first, near))
+    other = lax.ppermute(near, "occ", [(j, j ^ 2) for j in range(occ_axis)])
+    pieces = [here, first, neighbour(first, 1), near, other]
     swap_cores = [(j, j ^ 1) for j in range(occ_axis)]
     pieces += [lax.ppermute(piece, "occ", swap_cores) for piece in pieces]
 

time: 103 us -> 103 us (level)
  waiting for transfers between devices: 30 us -> 22 us
  starting transfers between devices: 23.1 us -> 31 us
    ppermute x3, waiting for transfers between devices: 24 us -> 15.4 us  [neighbour(): return lax.ppermute(array, ('occ', 'vir'), pairs)]
    ppermute x0 -> x1, starting transfers between devices: none -> 3.49 us  [per_device(): other = lax.ppermute(near, 'occ', [(j, j ^ 2) for j in range(occ_axis)])]
    ppermute x3, starting transfers between devices: 7.96 us -> 10.7 us  [neighbour(): return lax.ppermute(array, ('occ', 'vir'), pairs)]
    ppermute x4 -> x5, starting transfers between devices: 8.65 us -> 10.3 us  [per_device(): pieces += [lax.ppermute(piece, 'occ', swap_cores) for piece in pieces]]
  transfers between devices with their start and end apart: 8 -> 10, of which waited for: 4 -> 5; matrix products, arithmetic and copies ran while one was open for 0% -> 0% of each run, Pallas kernels for 0% -> 0%
where the time goes in v7:
time: 103 us; the launch traced here: 102 us
  blocking collectives  38 us (37%)
  starting transfers between devices  31 us (30%)
  waiting for transfers between devices  22 us (21%)
  Pallas kernels  9.9 us (10%)
    all_gather x1, blocking collectives, per_device(): lax.all_gather(slab, 'vir', axis=0, tiled=True, axis_index_groups=groups)  38 us
    ppermute x3, waiting for transfers between devices, neighbour(): return lax.ppermute(array, ('occ', 'vir'), pairs)  15.4 us
    ppermute x3, starting transfers between devices, neighbour(): return lax.ppermute(array, ('occ', 'vir'), pairs)  10.7 us
    ppermute x5, starting transfers between devices, per_device(): pieces += [lax.ppermute(piece, 'occ', swap_cores) for piece in pieces]  10.3 us
    all_to_all x1, starting transfers between devices, per_device(): swapped = lax.all_to_all(packed, 'vir', 0, 0, tiled=True)  6.52 us
    pallas_call x1, Pallas kernels, final(): pl.pallas_call(final_body, in_specs=[smem] * 2 + [vmem] * 2 + [hbm] * (1...  5.6 us
    all_to_all x1, waiting for transfers between devices, per_device(): swapped = lax.all_to_all(packed, 'vir', 0, 0, tiled=True)  4.92 us
    pallas_call x1, Pallas kernels, pack(): pl.pallas_call(pack_body, grid=(blocks,), in_specs=[pl.BlockSpec((pairs,...  4.3 us
  transfers between devices with their start and end apart: 10, of which 5 were waited for; matrix products, arithmetic and copies ran while one was open for 0% of the time, Pallas kernels for 0%

profile of v7, /device:TPU:6, one launch (start us, length us, event | category | flops | bytes accessed | tf_op | source)
XLA Modules:
  0.0 102.2 jit_solution(13232818017535361967)
XLA Ops:
  0.0 0.8 slice_select_fusion
  0.9 38.0 %all-gather = bf16[1,288,1152]{2,1,0:T(8,128)(2,1)} all-gather(bf16[1,24,1152]{2,1,0:T(8,128)(2,1)S(1)} %slice_select_fusion), channel_id=2, replica_groups={{0,1,2,3,4,5,6,7,8,9,10,11},{12,13,14,15,16,17,18,19,20,21,22,23},{24,2..., dimensions={1}, use_global_device_ids=true | all-gather | bytes 718848 | tf_op jit(solution)/shard_map/all_gather | solution.py:188
  38.8 4.3 %pack.1 = bf16[48,112,128]{2,1,0:T(8,128)(2,1)} custom-call(bf16[24,24,1152]{2,1,0:T(8,128)(2,1)} %bitcast.10, bf16[288,1152]{1,0:T(8,128)(2,1)} %bitcast.12), custom_call_target="tpu_custom_call" | custom-call | tf_op jit(solution)/shard_map/pack/pallas_call | solution.py:52
  43.1 0.0 copy-start.1
  43.1 0.0 copy-start.2
  43.1 0.0 copy-start
  43.1 6.5 %all-to-all-start = ((bf16[48,112,128]{2,1,0:T(8,128)(2,1)}), bf16[48,112,128]{2,1,0:T(8,128)(2,1)S(1)}, u32[]{:S(2)}, u32[]{:S(2)}) async-start(bf16[48,112,128]{2,1,0:T(8,128)(2,1)} %pack.1), calls=%async_computation | async-start | bytes 2752512 | tf_op jit(solution)/shard_map/all_to_all | solution.py:191
  49.7 0.0 copy-done.1
  49.7 2.1 %collective-permute-start = (bf16[288,1152]{1,0:T(8,128)(2,1)S(1)}, bf16[288,1152]{1,0:T(8,128)(2,1)}, u32[]{:S(2)}, u32[]{:S(2)}) collective-permute-start(bf16[288,1152]{1,0:T(8,128)(2,1)S(1)} %bitcast.14), channel_id=1, source_target_pairs={{0,12},{1,13},{2,14},{3,15},{4,16},{5,17},{6,18},{7,19},{8,20},{9,... | collective-permute-start | bytes 1990664 | tf_op jit(solution)/shard_map/ppermute | solution.py:199
  51.9 3.7 %collective-permute-start.1 = (bf16[144,1152]{1,0:T(8,128)(2,1)S(1)}, bf16[144,1152]{1,0:T(8,128)(2,1)}, u32[]{:S(2)}, u32[]{:S(2)}) collective-permute-start(bf16[144,1152]{1,0:T(8,128)(2,1)S(1)} %dynamic-slice_bitcast_fusion), channel_id=1, source_target_pairs={{0,36},{1,37},{2,38},{3,39},{4,40},{5,41},{6,42},{7,43},{8,44},{9,... | collective-permute-start | bytes 995336 | tf_op jit(solution)/shard_map/ppermute | solution.py:199
  55.6 10.6 %collective-permute-done.1.rest_3_ = bf16[144,1152]{1,0:T(8,128)(2,1)} collective-permute-done((bf16[144,1152]{1,0:T(8,128)(2,1)S(1)}, bf16[144,1152]{1,0:T(8,128)(2,1)}, u32[]{:S(2)}, u32[]{:S(2)}) %collective-permute-start.1) | collective-permute-done | bytes 331808 | tf_op jit(solution)/shard_map/ppermute | solution.py:199
  66.2 1.9 %collective-permute-done.rest_1_ = bf16[288,1152]{1,0:T(8,128)(2,1)} collective-permute-done((bf16[288,1152]{1,0:T(8,128)(2,1)S(1)}, bf16[288,1152]{1,0:T(8,128)(2,1)}, u32[]{:S(2)}, u32[]{:S(2)}) %collective-permute-start) | collective-permute-done | bytes 663584 | tf_op jit(solution)/shard_map/ppermute | solution.py:199
  68.1 4.9 %collective-permute-start.2 = (bf16[288,1152]{1,0:T(8,128)(2,1)}, bf16[288,1152]{1,0:T(8,128)(2,1)}, u32[]{:S(2)}, u32[]{:S(2)}) collective-permute-start(bf16[288,1152]{1,0:T(8,128)(2,1)} %collective-permute-done.rest_1_), channel_id=1, source_target_pairs={{0,12},{1,13},{2,14},{3,15},{4,16},{5,17},{6,18},{7,19},{8,20},{9,... | collective-permute-start | bytes 1990664 | tf_op jit(solution)/shard_map/ppermute | solution.py:199
  73.0 1.9 %collective-permute-start.4 = (bf16[288,1152]{1,0:T(8,128)(2,1)S(1)}, bf16[288,1152]{1,0:T(8,128)(2,1)}, u32[]{:S(2)}, u32[]{:S(2)}) collective-permute-start(bf16[288,1152]{1,0:T(8,128)(2,1)S(1)} %bitcast.15), channel_id=1, source_target_pairs={{0,48},{48,0},{96,144},{144,96},{192,240},{240,192},{288,336},{336... | collective-permute-start | bytes 1990664 | tf_op jit(solution)/shard_map/ppermute | solution.py:208
  74.9 3.5 %collective-permute-start.3 = (bf16[144,1152]{1,0:T(8,128)(2,1)}, bf16[144,1152]{1,0:T(8,128)(2,1)}, u32[]{:S(2)}, u32[]{:S(2)}) collective-permute-start(bf16[144,1152]{1,0:T(8,128)(2,1)} %collective-permute-done.1.rest_3_), channel_id=1, source_target_pairs={{0,96},{48,144},{96,0},{144,48},{192,288},{240,336},{288,192},{336... | collective-permute-start | bytes 995336 | tf_op jit(solution)/shard_map/ppermute | solution.py:205
  78.4 2.1 %collective-permute-start.5 = (bf16[288,1152]{1,0:T(8,128)(2,1)}, bf16[288,1152]{1,0:T(8,128)(2,1)}, u32[]{:S(2)}, u32[]{:S(2)}) collective-permute-start(bf16[288,1152]{1,0:T(8,128)(2,1)} %collective-permute-done.rest_1_), channel_id=1, source_target_pairs={{0,48},{48,0},{96,144},{144,96},{192,240},{240,192},{288,336},{336... | collective-permute-start | bytes 1990664 | tf_op jit(solution)/shard_map/ppermute | solution.py:208
  80.5 2.9 %collective-permute-done.2.rest_2_ = bf16[288,1152]{1,0:T(8,128)(2,1)} collective-permute-done((bf16[288,1152]{1,0:T(8,128)(2,1)}, bf16[288,1152]{1,0:T(8,128)(2,1)}, u32[]{:S(2)}, u32[]{:S(2)}) %collective-permute-start.2) | collective-permute-done | bytes 663584 | tf_op jit(solution)/shard_map/ppermute | solution.py:199
  83.4 1.9 %collective-permute-start.6 = (bf16[288,1152]{1,0:T(8,128)(2,1)}, bf16[288,1152]{1,0:T(8,128)(2,1)}, u32[]{:S(2)}, u32[]{:S(2)}) collective-permute-start(bf16[288,1152]{1,0:T(8,128)(2,1)} %collective-permute-done.2.rest_2_), channel_id=1, source_target_pairs={{0,48},{48,0},{96,144},{144,96},{192,240},{240,192},{288,336},{336... | collective-permute-start | bytes 1990664 | tf_op jit(solution)/shard_map/ppermute | solution.py:208
  85.3 2.4 %collective-permute-start.7 = (bf16[144,1152]{1,0:T(8,128)(2,1)}, bf16[144,1152]{1,0:T(8,128)(2,1)}, u32[]{:S(2)}, u32[]{:S(2)}) collective-permute-start(bf16[144,1152]{1,0:T(8,128)(2,1)} %collective-permute-done.1.rest_3_), channel_id=1, source_target_pairs={{0,48},{48,0},{96,144},{144,96},{192,240},{240,192},{288,336},{336... | collective-permute-start | bytes 995336 | tf_op jit(solution)/shard_map/ppermute | solution.py:208
  87.8 0.0 collective-permute-done.3.rest_4_
  87.8 1.9 %collective-permute-start.8 = (bf16[144,1152]{1,0:T(8,128)(2,1)}, bf16[144,1152]{1,0:T(8,128)(2,1)}, u32[]{:S(2)}, u32[]{:S(2)}) collective-permute-start(bf16[144,1152]{1,0:T(8,128)(2,1)} %collective-permute-done.3.rest_4_), channel_id=1, source_target_pairs={{0,48},{48,0},{96,144},{144,96},{192,240},{240,192},{288,336},{336... | collective-permute-start | bytes 995336 | tf_op jit(solution)/shard_map/ppermute | solution.py:208
  89.7 0.0 copy-done.2
  89.7 0.1 reshape.17.mask
  89.8 0.1 pad_add_fusion.where
  89.9 0.0 collective-permute-done.4.rest_5_
  89.9 0.0 collective-permute-done.7.rest_8_
  89.9 1.7 %collective-permute-done.8.rest_9_ = bf16[144,1152]{1,0:T(8,128)(2,1)} collective-permute-done((bf16[144,1152]{1,0:T(8,128)(2,1)}, bf16[144,1152]{1,0:T(8,128)(2,1)}, u32[]{:S(2)}, u32[]{:S(2)}) %collective-permute-start.8) | collective-permute-done | bytes 331808 | tf_op jit(solution)/shard_map/ppermute | solution.py:208
  91.6 0.0 collective-permute-done.5.rest_6_
  91.6 0.0 collective-permute-done.6.rest_7_
  91.6 4.9 %all-to-all-done.swapped = bf16[48,112,128]{2,1,0:T(8,128)(2,1)S(1)} async-done(((bf16[48,112,128]{2,1,0:T(8,128)(2,1)}), bf16[48,112,128]{2,1,0:T(8,128)(2,1)S(1)}, u32[]{:S(2)}, u32[]{:S(2)}) %all-to-all-start) | async-done | bytes 1376288 | tf_op jit(solution)/shard_map/all_to_all | solution.py:191
  96.6 0.0 copy-done
  96.6 5.6 %final.1 = f32[288,1152]{1,0:T(8,128)} custom-call(s32[3]{0:T(128)S(1)} %pad_add_fusion.where, s32[72]{0:T(128)S(1)} %reshape.17.mask, bf16[576,1152]{1,0:T(8,128)(2,1)S(1)} %bitcast.11, bf16[48,112,128]{2,1,0:T(8,128)(2,1)S(1)} %all-to-all-done.swapped, f32[288,1152]{1,0:T(8,128)} %bitcast.16, bf16[288,1152]{1,0:T(8,128)(2,1)} %bitcast.13, ...), custom_call_target="tpu_custom_call" | custom-call | tf_op jit(solution)/shard_map/final/pallas_call | solution.py:159
  (2 shorter events, 0.0 us)
Async XLA Ops:
  43.1 6.5 %copy-start.1 = (bf16[1,288,1152]{2,1,0:T(8,128)(2,1)S(1)}, bf16[1,288,1152]{2,1,0:T(8,128)(2,1)}, u32[]{:S(2)}) copy-start(bf16[1,288,1152]{2,1,0:T(8,128)(2,1)} %all-gather) | copy-start | bytes 1990660
  43.1 46.6 %copy-start.2 = (s32[2,6,6]{2,0,1:T(2,128)S(1)}, s32[2,6,6]{2,0,1:T(2,128)}, u32[]{:S(2)}) copy-start(s32[2,6,6]{2,0,1:T(2,128)} %param.6) | copy-start | bytes 868
  43.1 53.4 %copy-start = (bf16[2,12,24,1152]{3,2,1,0:T(8,128)(2,1)S(1)}, bf16[2,12,24,1152]{3,2,1,0:T(8,128)(2,1)}, u32[]{:S(2)}) copy-start(bf16[2,12,24,1152]{3,2,1,0:T(8,128)(2,1)} %param.4) | copy-start | bytes 3981316
  43.1 53.4 %all-to-all-start = ((bf16[48,112,128]{2,1,0:T(8,128)(2,1)}), bf16[48,112,128]{2,1,0:T(8,128)(2,1)S(1)}, u32[]{:S(2)}, u32[]{:S(2)}) async-start(bf16[48,112,128]{2,1,0:T(8,128)(2,1)} %pack.1), calls=%async_computation | async-start | bytes 2752512 | tf_op jit(solution)/shard_map/all_to_all | solution.py:191
  49.7 18.4 %collective-permute-start = (bf16[288,1152]{1,0:T(8,128)(2,1)S(1)}, bf16[288,1152]{1,0:T(8,128)(2,1)}, u32[]{:S(2)}, u32[]{:S(2)}) collective-permute-start(bf16[288,1152]{1,0:T(8,128)(2,1)S(1)} %bitcast.14), channel_id=1, source_target_pairs={{0,12},{1,13},{2,14},{3,15},{4,16},{5,17},{6,18},{7,19},{8,20},{9,... | collective-permute-start | bytes 1990664 | tf_op jit(solution)/shard_map/ppermute | solution.py:199
  51.9 14.3 %collective-permute-start.1 = (bf16[144,1152]{1,0:T(8,128)(2,1)S(1)}, bf16[144,1152]{1,0:T(8,128)(2,1)}, u32[]{:S(2)}, u32[]{:S(2)}) collective-permute-start(bf16[144,1152]{1,0:T(8,128)(2,1)S(1)} %dynamic-slice_bitcast_fusion), channel_id=1, source_target_pairs={{0,36},{1,37},{2,38},{3,39},{4,40},{5,41},{6,42},{7,43},{8,44},{9,... | collective-permute-start | bytes 995336 | tf_op jit(solution)/shard_map/ppermute | solution.py:199
  68.1 15.4 %collective-permute-start.2 = (bf16[288,1152]{1,0:T(8,128)(2,1)}, bf16[288,1152]{1,0:T(8,128)(2,1)}, u32[]{:S(2)}, u32[]{:S(2)}) collective-permute-start(bf16[288,1152]{1,0:T(8,128)(2,1)} %collective-permute-done.rest_1_), channel_id=1, source_target_pairs={{0,12},{1,13},{2,14},{3,15},{4,16},{5,17},{6,18},{7,19},{8,20},{9,... | collective-permute-start | bytes 1990664 | tf_op jit(solution)/shard_map/ppermute | solution.py:199
  73.0 16.9 %collective-permute-start.4 = (bf16[288,1152]{1,0:T(8,128)(2,1)S(1)}, bf16[288,1152]{1,0:T(8,128)(2,1)}, u32[]{:S(2)}, u32[]{:S(2)}) collective-permute-start(bf16[288,1152]{1,0:T(8,128)(2,1)S(1)} %bitcast.15), channel_id=1, source_target_pairs={{0,48},{48,0},{96,144},{144,96},{192,240},{240,192},{288,336},{336... | collective-permute-start | bytes 1990664 | tf_op jit(solution)/shard_map/ppermute | solution.py:208
  74.9 12.8 %collective-permute-start.3 = (bf16[144,1152]{1,0:T(8,128)(2,1)}, bf16[144,1152]{1,0:T(8,128)(2,1)}, u32[]{:S(2)}, u32[]{:S(2)}) collective-permute-start(bf16[144,1152]{1,0:T(8,128)(2,1)} %collective-permute-done.1.rest_3_), channel_id=1, source_target_pairs={{0,96},{48,144},{96,0},{144,48},{192,288},{240,336},{288,192},{336... | collective-permute-start | bytes 995336 | tf_op jit(solution)/shard_map/ppermute | solution.py:205
  78.4 13.2 %collective-permute-start.5 = (bf16[288,1152]{1,0:T(8,128)(2,1)}, bf16[288,1152]{1,0:T(8,128)(2,1)}, u32[]{:S(2)}, u32[]{:S(2)}) collective-permute-start(bf16[288,1152]{1,0:T(8,128)(2,1)} %collective-permute-done.rest_1_), channel_id=1, source_target_pairs={{0,48},{48,0},{96,144},{144,96},{192,240},{240,192},{288,336},{336... | collective-permute-start | bytes 1990664 | tf_op jit(solution)/shard_map/ppermute | solution.py:208
  83.4 8.2 %collective-permute-start.6 = (bf16[288,1152]{1,0:T(8,128)(2,1)}, bf16[288,1152]{1,0:T(8,128)(2,1)}, u32[]{:S(2)}, u32[]{:S(2)}) collective-permute-start(bf16[288,1152]{1,0:T(8,128)(2,1)} %collective-permute-done.2.rest_2_), channel_id=1, source_target_pairs={{0,48},{48,0},{96,144},{144,96},{192,240},{240,192},{288,336},{336... | collective-permute-start | bytes 1990664 | tf_op jit(solution)/shard_map/ppermute | solution.py:208
  85.3 4.6 %collective-permute-start.7 = (bf16[144,1152]{1,0:T(8,128)(2,1)}, bf16[144,1152]{1,0:T(8,128)(2,1)}, u32[]{:S(2)}, u32[]{:S(2)}) collective-permute-start(bf16[144,1152]{1,0:T(8,128)(2,1)} %collective-permute-done.1.rest_3_), channel_id=1, source_target_pairs={{0,48},{48,0},{96,144},{144,96},{192,240},{240,192},{288,336},{336... | collective-permute-start | bytes 995336 | tf_op jit(solution)/shard_map/ppermute | solution.py:208
  87.8 3.9 %collective-permute-start.8 = (bf16[144,1152]{1,0:T(8,128)(2,1)}, bf16[144,1152]{1,0:T(8,128)(2,1)}, u32[]{:S(2)}, u32[]{:S(2)}) collective-permute-start(bf16[144,1152]{1,0:T(8,128)(2,1)} %collective-permute-done.3.rest_4_), channel_id=1, source_target_pairs={{0,48},{48,0},{96,144},{144,96},{192,240},{240,192},{288,336},{336... | collective-permute-start | bytes 995336 | tf_op jit(solution)/shard_map/ppermute | solution.py:208

commit v8 on v7

--- a/solution.py
+++ b/solution.py
@@ -201,11 +201,12 @@
     first = neighbour(here, 1)
     half = here.shape[0] // 2
     near = neighbour(lax.dynamic_slice_in_dim(here, plane * half, half, 0), -1)
-    first, near = lax.optimization_barrier((first, near))
+    swap_cores = [(j, j ^ 1) for j in range(occ_axis)]
+    across = lax.ppermute(here, "occ", swap_cores)
+    first, near, across = lax.optimization_barrier((first, near, across))
     other = lax.ppermute(near, "occ", [(j, j ^ 2) for j in range(occ_axis)])
     pieces = [here, first, neighbour(first, 1), near, other]
-    swap_cores = [(j, j ^ 1) for j in range(occ_axis)]
-    pieces += [lax.ppermute(piece, "occ", swap_cores) for piece in pieces]
+    pieces += [across] + [lax.ppermute(piece, "occ", swap_cores) for piece in pieces[1:]]
 
     out = final(
         where,

time: 103 us -> 103 us (level)
  waiting for transfers between devices: 22 us -> 23.4 us
  starting transfers between devices: 31 us -> 29.7 us
    ppermute x3, waiting for transfers between devices: 15.4 us -> 18.8 us  [neighbour(): return lax.ppermute(array, ('occ', 'vir'), pairs)]
    all_to_all x1, waiting for transfers between devices: 4.92 us -> 2.84 us  [per_device(): swapped = lax.all_to_all(packed, 'vir', 0, 0, tiled=True)]
    ppermute x3, starting transfers between devices: 10.7 us -> 9.61 us  [neighbour(): return lax.ppermute(array, ('occ', 'vir'), pairs)]
where the time goes in v8:
time: 103 us; the launch traced here: 102 us
  blocking collectives  38 us (37%)
  starting transfers between devices  29.7 us (29%)
  waiting for transfers between devices  23.4 us (23%)
  Pallas kernels  9.91 us (10%)
    all_gather x1, blocking collectives, per_device(): lax.all_gather(slab, 'vir', axis=0, tiled=True, axis_index_groups=groups)  38 us
    ppermute x3, waiting for transfers between devices, neighbour(): return lax.ppermute(array, ('occ', 'vir'), pairs)  18.8 us
    ppermute x3, starting transfers between devices, neighbour(): return lax.ppermute(array, ('occ', 'vir'), pairs)  9.61 us
    ppermute x4, starting transfers between devices, per_device(): lax.ppermute(piece, 'occ', swap_cores)  8.16 us
    all_to_all x1, starting transfers between devices, per_device(): swapped = lax.all_to_all(packed, 'vir', 0, 0, tiled=True)  6.52 us
    pallas_call x1, Pallas kernels, final(): pl.pallas_call(final_body, in_specs=[smem] * 2 + [vmem] * 2 + [hbm] * (1...  5.61 us
    pallas_call x1, Pallas kernels, pack(): pl.pallas_call(pack_body, grid=(blocks,), in_specs=[pl.BlockSpec((pairs,...  4.3 us
    ppermute x1, starting transfers between devices, per_device(): other = lax.ppermute(near, 'occ', [(j, j ^ 2) for j in range(occ_axis)])  3.49 us
  transfers between devices with their start and end apart: 10, of which 5 were waited for; matrix products, arithmetic and copies ran while one was open for 0% of the time, Pallas kernels for 0%

profile of v8, /device:TPU:6, one launch (start us, length us, event | category | flops | bytes accessed | tf_op | source)
XLA Modules:
  0.0 102.2 jit_solution(10742308494910205477)
XLA Ops:
  0.0 0.8 slice_select_fusion
  0.9 38.0 %all-gather = bf16[1,288,1152]{2,1,0:T(8,128)(2,1)} all-gather(bf16[1,24,1152]{2,1,0:T(8,128)(2,1)S(1)} %slice_select_fusion), channel_id=2, replica_groups={{0,1,2,3,4,5,6,7,8,9,10,11},{12,13,14,15,16,17,18,19,20,21,22,23},{24,2..., dimensions={1}, use_global_device_ids=true | all-gather | bytes 718848 | tf_op jit(solution)/shard_map/all_gather | solution.py:188
  38.8 4.3 %pack.1 = bf16[48,112,128]{2,1,0:T(8,128)(2,1)} custom-call(bf16[24,24,1152]{2,1,0:T(8,128)(2,1)} %bitcast.10, bf16[288,1152]{1,0:T(8,128)(2,1)} %bitcast.12), custom_call_target="tpu_custom_call" | custom-call | tf_op jit(solution)/shard_map/pack/pallas_call | solution.py:52
  43.1 0.0 copy-start.1
  43.1 0.0 copy-start.3
  43.1 0.0 copy-start
  43.1 6.5 %all-to-all-start = ((bf16[48,112,128]{2,1,0:T(8,128)(2,1)}), bf16[48,112,128]{2,1,0:T(8,128)(2,1)S(1)}, u32[]{:S(2)}, u32[]{:S(2)}) async-start(bf16[48,112,128]{2,1,0:T(8,128)(2,1)} %pack.1), calls=%async_computation | async-start | bytes 2752512 | tf_op jit(solution)/shard_map/all_to_all | solution.py:191
  49.7 0.0 copy-done.1
  49.7 2.1 %collective-permute-start = (bf16[288,1152]{1,0:T(8,128)(2,1)S(1)}, bf16[288,1152]{1,0:T(8,128)(2,1)}, u32[]{:S(2)}, u32[]{:S(2)}) collective-permute-start(bf16[288,1152]{1,0:T(8,128)(2,1)S(1)} %bitcast.14), channel_id=1, source_target_pairs={{0,12},{1,13},{2,14},{3,15},{4,16},{5,17},{6,18},{7,19},{8,20},{9,... | collective-permute-start | bytes 1990664 | tf_op jit(solution)/shard_map/ppermute | solution.py:199
  51.8 1.9 %collective-permute-start.2 = (bf16[288,1152]{1,0:T(8,128)(2,1)S(1)}, bf16[288,1152]{1,0:T(8,128)(2,1)}, u32[]{:S(2)}, u32[]{:S(2)}) collective-permute-start(bf16[288,1152]{1,0:T(8,128)(2,1)S(1)} %bitcast.15), channel_id=1, source_target_pairs={{0,48},{48,0},{96,144},{144,96},{192,240},{240,192},{288,336},{336... | collective-permute-start | bytes 1990664 | tf_op jit(solution)/shard_map/ppermute | solution.py:205
  53.8 3.7 %collective-permute-start.1 = (bf16[144,1152]{1,0:T(8,128)(2,1)S(1)}, bf16[144,1152]{1,0:T(8,128)(2,1)}, u32[]{:S(2)}, u32[]{:S(2)}) collective-permute-start(bf16[144,1152]{1,0:T(8,128)(2,1)S(1)} %dynamic-slice_bitcast_fusion), channel_id=1, source_target_pairs={{0,36},{1,37},{2,38},{3,39},{4,40},{5,41},{6,42},{7,43},{8,44},{9,... | collective-permute-start | bytes 995336 | tf_op jit(solution)/shard_map/ppermute | solution.py:199
  57.5 8.7 %collective-permute-done.1.rest_3_ = bf16[144,1152]{1,0:T(8,128)(2,1)} collective-permute-done((bf16[144,1152]{1,0:T(8,128)(2,1)S(1)}, bf16[144,1152]{1,0:T(8,128)(2,1)}, u32[]{:S(2)}, u32[]{:S(2)}) %collective-permute-start.1) | collective-permute-done | bytes 331808 | tf_op jit(solution)/shard_map/ppermute | solution.py:199
  66.2 5.1 %collective-permute-done.rest_1_ = bf16[288,1152]{1,0:T(8,128)(2,1)} collective-permute-done((bf16[288,1152]{1,0:T(8,128)(2,1)S(1)}, bf16[288,1152]{1,0:T(8,128)(2,1)}, u32[]{:S(2)}, u32[]{:S(2)}) %collective-permute-start) | collective-permute-done | bytes 663584 | tf_op jit(solution)/shard_map/ppermute | solution.py:199
  71.3 0.0 collective-permute-done.2.rest_5_
  71.3 3.8 %collective-permute-start.3 = (bf16[288,1152]{1,0:T(8,128)(2,1)}, bf16[288,1152]{1,0:T(8,128)(2,1)S(1)}, u32[]{:S(2)}, u32[]{:S(2)}) collective-permute-start(bf16[288,1152]{1,0:T(8,128)(2,1)} %collective-permute-done.rest_1_), channel_id=1, source_target_pairs={{0,12},{1,13},{2,14},{3,15},{4,16},{5,17},{6,18},{7,19},{8,20},{9,... | collective-permute-start | bytes 1990664 | tf_op jit(solution)/shard_map/ppermute | solution.py:199
  75.0 1.9 %collective-permute-start.5 = (bf16[288,1152]{1,0:T(8,128)(2,1)}, bf16[288,1152]{1,0:T(8,128)(2,1)}, u32[]{:S(2)}, u32[]{:S(2)}) collective-permute-start(bf16[288,1152]{1,0:T(8,128)(2,1)} %collective-permute-done.rest_1_), channel_id=1, source_target_pairs={{0,48},{48,0},{96,144},{144,96},{192,240},{240,192},{288,336},{336... | collective-permute-start | bytes 1990664 | tf_op jit(solution)/shard_map/ppermute | solution.py:209
  77.0 3.5 %collective-permute-start.4 = (bf16[144,1152]{1,0:T(8,128)(2,1)}, bf16[144,1152]{1,0:T(8,128)(2,1)}, u32[]{:S(2)}, u32[]{:S(2)}) collective-permute-start(bf16[144,1152]{1,0:T(8,128)(2,1)} %collective-permute-done.1.rest_3_), channel_id=1, source_target_pairs={{0,96},{48,144},{96,0},{144,48},{192,288},{240,336},{288,192},{336... | collective-permute-start | bytes 995336 | tf_op jit(solution)/shard_map/ppermute | solution.py:207
  80.5 5.0 %collective-permute-done.3.rest_2_ = bf16[288,1152]{1,0:T(8,128)(2,1)S(1)} collective-permute-done((bf16[288,1152]{1,0:T(8,128)(2,1)}, bf16[288,1152]{1,0:T(8,128)(2,1)S(1)}, u32[]{:S(2)}, u32[]{:S(2)}) %collective-permute-start.3) | collective-permute-done | bytes 663584 | tf_op jit(solution)/shard_map/ppermute | solution.py:199
  85.5 0.0 copy-start.2
  85.5 1.9 %collective-permute-start.6 = (bf16[288,1152]{1,0:T(8,128)(2,1)S(1)}, bf16[288,1152]{1,0:T(8,128)(2,1)}, u32[]{:S(2)}, u32[]{:S(2)}) collective-permute-start(bf16[288,1152]{1,0:T(8,128)(2,1)S(1)} %collective-permute-done.3.rest_2_), channel_id=1, source_target_pairs={{0,48},{48,0},{96,144},{144,96},{192,240},{240,192},{288,336},{336... | collective-permute-start | bytes 1990664 | tf_op jit(solution)/shard_map/ppermute | solution.py:209
  87.4 2.4 %collective-permute-start.7 = (bf16[144,1152]{1,0:T(8,128)(2,1)}, bf16[144,1152]{1,0:T(8,128)(2,1)}, u32[]{:S(2)}, u32[]{:S(2)}) collective-permute-start(bf16[144,1152]{1,0:T(8,128)(2,1)} %collective-permute-done.1.rest_3_), channel_id=1, source_target_pairs={{0,48},{48,0},{96,144},{144,96},{192,240},{240,192},{288,336},{336... | collective-permute-start | bytes 995336 | tf_op jit(solution)/shard_map/ppermute | solution.py:209
  89.8 0.0 collective-permute-done.4.rest_4_
  89.8 1.9 %collective-permute-start.8 = (bf16[144,1152]{1,0:T(8,128)(2,1)}, bf16[144,1152]{1,0:T(8,128)(2,1)}, u32[]{:S(2)}, u32[]{:S(2)}) collective-permute-start(bf16[144,1152]{1,0:T(8,128)(2,1)} %collective-permute-done.4.rest_4_), channel_id=1, source_target_pairs={{0,48},{48,0},{96,144},{144,96},{192,240},{240,192},{288,336},{336... | collective-permute-start | bytes 995336 | tf_op jit(solution)/shard_map/ppermute | solution.py:209
  91.8 0.0 copy-done.3
  91.8 0.1 reshape.17.mask
  91.9 0.1 pad_add_fusion.where
  92.0 0.0 collective-permute-done.7.rest_8_
  92.0 0.0 collective-permute-done.5.rest_6_
  92.0 1.7 %collective-permute-done.8.rest_9_ = bf16[144,1152]{1,0:T(8,128)(2,1)} collective-permute-done((bf16[144,1152]{1,0:T(8,128)(2,1)}, bf16[144,1152]{1,0:T(8,128)(2,1)}, u32[]{:S(2)}, u32[]{:S(2)}) %collective-permute-start.8) | collective-permute-done | bytes 331808 | tf_op jit(solution)/shard_map/ppermute | solution.py:209
  93.7 0.0 collective-permute-done.6.rest_7_
  93.7 2.8 %all-to-all-done.swapped = bf16[48,112,128]{2,1,0:T(8,128)(2,1)S(1)} async-done(((bf16[48,112,128]{2,1,0:T(8,128)(2,1)}), bf16[48,112,128]{2,1,0:T(8,128)(2,1)S(1)}, u32[]{:S(2)}, u32[]{:S(2)}) %all-to-all-start) | async-done | bytes 1376288 | tf_op jit(solution)/shard_map/all_to_all | solution.py:191
  96.6 0.0 copy-done.2
  96.6 0.0 copy-done
  96.6 5.6 %final.1 = f32[288,1152]{1,0:T(8,128)} custom-call(s32[3]{0:T(128)S(1)} %pad_add_fusion.where, s32[72]{0:T(128)S(1)} %reshape.17.mask, bf16[576,1152]{1,0:T(8,128)(2,1)S(1)} %bitcast.11, bf16[48,112,128]{2,1,0:T(8,128)(2,1)S(1)} %all-to-all-done.swapped, f32[288,1152]{1,0:T(8,128)} %bitcast.16, bf16[288,1152]{1,0:T(8,128)(2,1)} %bitcast.13, ...), custom_call_target="tpu_custom_call" | custom-call | tf_op jit(solution)/shard_map/final/pallas_call | solution.py:159
  (2 shorter events, 0.0 us)
Async XLA Ops:
  43.1 6.5 %copy-start.1 = (bf16[1,288,1152]{2,1,0:T(8,128)(2,1)S(1)}, bf16[1,288,1152]{2,1,0:T(8,128)(2,1)}, u32[]{:S(2)}) copy-start(bf16[1,288,1152]{2,1,0:T(8,128)(2,1)} %all-gather) | copy-start | bytes 1990660
  43.1 48.7 %copy-start.3 = (s32[2,6,6]{2,0,1:T(2,128)S(1)}, s32[2,6,6]{2,0,1:T(2,128)}, u32[]{:S(2)}) copy-start(s32[2,6,6]{2,0,1:T(2,128)} %param.6) | copy-start | bytes 868
  43.1 53.4 %copy-start = (bf16[2,12,24,1152]{3,2,1,0:T(8,128)(2,1)S(1)}, bf16[2,12,24,1152]{3,2,1,0:T(8,128)(2,1)}, u32[]{:S(2)}) copy-start(bf16[2,12,24,1152]{3,2,1,0:T(8,128)(2,1)} %param.4) | copy-start | bytes 3981316
  43.1 53.4 %all-to-all-start = ((bf16[48,112,128]{2,1,0:T(8,128)(2,1)}), bf16[48,112,128]{2,1,0:T(8,128)(2,1)S(1)}, u32[]{:S(2)}, u32[]{:S(2)}) async-start(bf16[48,112,128]{2,1,0:T(8,128)(2,1)} %pack.1), calls=%async_computation | async-start | bytes 2752512 | tf_op jit(solution)/shard_map/all_to_all | solution.py:191
  49.7 21.6 %collective-permute-start = (bf16[288,1152]{1,0:T(8,128)(2,1)S(1)}, bf16[288,1152]{1,0:T(8,128)(2,1)}, u32[]{:S(2)}, u32[]{:S(2)}) collective-permute-start(bf16[288,1152]{1,0:T(8,128)(2,1)S(1)} %bitcast.14), channel_id=1, source_target_pairs={{0,12},{1,13},{2,14},{3,15},{4,16},{5,17},{6,18},{7,19},{8,20},{9,... | collective-permute-start | bytes 1990664 | tf_op jit(solution)/shard_map/ppermute | solution.py:199
  51.8 19.5 %collective-permute-start.2 = (bf16[288,1152]{1,0:T(8,128)(2,1)S(1)}, bf16[288,1152]{1,0:T(8,128)(2,1)}, u32[]{:S(2)}, u32[]{:S(2)}) collective-permute-start(bf16[288,1152]{1,0:T(8,128)(2,1)S(1)} %bitcast.15), channel_id=1, source_target_pairs={{0,48},{48,0},{96,144},{144,96},{192,240},{240,192},{288,336},{336... | collective-permute-start | bytes 1990664 | tf_op jit(solution)/shard_map/ppermute | solution.py:205
  53.8 12.4 %collective-permute-start.1 = (bf16[144,1152]{1,0:T(8,128)(2,1)S(1)}, bf16[144,1152]{1,0:T(8,128)(2,1)}, u32[]{:S(2)}, u32[]{:S(2)}) collective-permute-start(bf16[144,1152]{1,0:T(8,128)(2,1)S(1)} %dynamic-slice_bitcast_fusion), channel_id=1, source_target_pairs={{0,36},{1,37},{2,38},{3,39},{4,40},{5,41},{6,42},{7,43},{8,44},{9,... | collective-permute-start | bytes 995336 | tf_op jit(solution)/shard_map/ppermute | solution.py:199
  71.3 14.2 %collective-permute-start.3 = (bf16[288,1152]{1,0:T(8,128)(2,1)}, bf16[288,1152]{1,0:T(8,128)(2,1)S(1)}, u32[]{:S(2)}, u32[]{:S(2)}) collective-permute-start(bf16[288,1152]{1,0:T(8,128)(2,1)} %collective-permute-done.rest_1_), channel_id=1, source_target_pairs={{0,12},{1,13},{2,14},{3,15},{4,16},{5,17},{6,18},{7,19},{8,20},{9,... | collective-permute-start | bytes 1990664 | tf_op jit(solution)/shard_map/ppermute | solution.py:199
  75.0 17.0 %collective-permute-start.5 = (bf16[288,1152]{1,0:T(8,128)(2,1)}, bf16[288,1152]{1,0:T(8,128)(2,1)}, u32[]{:S(2)}, u32[]{:S(2)}) collective-permute-start(bf16[288,1152]{1,0:T(8,128)(2,1)} %collective-permute-done.rest_1_), channel_id=1, source_target_pairs={{0,48},{48,0},{96,144},{144,96},{192,240},{240,192},{288,336},{336... | collective-permute-start | bytes 1990664 | tf_op jit(solution)/shard_map/ppermute | solution.py:209
  77.0 12.9 %collective-permute-start.4 = (bf16[144,1152]{1,0:T(8,128)(2,1)}, bf16[144,1152]{1,0:T(8,128)(2,1)}, u32[]{:S(2)}, u32[]{:S(2)}) collective-permute-start(bf16[144,1152]{1,0:T(8,128)(2,1)} %collective-permute-done.1.rest_3_), channel_id=1, source_target_pairs={{0,96},{48,144},{96,0},{144,48},{192,288},{240,336},{288,192},{336... | collective-permute-start | bytes 995336 | tf_op jit(solution)/shard_map/ppermute | solution.py:207
  85.5 11.1 %copy-start.2 = (bf16[288,1152]{1,0:T(8,128)(2,1)}, bf16[288,1152]{1,0:T(8,128)(2,1)S(1)}, u32[]{:S(2)}) copy-start(bf16[288,1152]{1,0:T(8,128)(2,1)S(1)} %collective-permute-done.3.rest_2_) | copy-start | bytes 1990660
  85.5 8.2 %collective-permute-start.6 = (bf16[288,1152]{1,0:T(8,128)(2,1)S(1)}, bf16[288,1152]{1,0:T(8,128)(2,1)}, u32[]{:S(2)}, u32[]{:S(2)}) collective-permute-start(bf16[288,1152]{1,0:T(8,128)(2,1)S(1)} %collective-permute-done.3.rest_2_), channel_id=1, source_target_pairs={{0,48},{48,0},{96,144},{144,96},{192,240},{240,192},{288,336},{336... | collective-permute-start | bytes 1990664 | tf_op jit(solution)/shard_map/ppermute | solution.py:209
  87.4 4.6 %collective-permute-start.7 = (bf16[144,1152]{1,0:T(8,128)(2,1)}, bf16[144,1152]{1,0:T(8,128)(2,1)}, u32[]{:S(2)}, u32[]{:S(2)}) collective-permute-start(bf16[144,1152]{1,0:T(8,128)(2,1)} %collective-permute-done.1.rest_3_), channel_id=1, source_target_pairs={{0,48},{48,0},{96,144},{144,96},{192,240},{240,192},{288,336},{336... | collective-permute-start | bytes 995336 | tf_op jit(solution)/shard_map/ppermute | solution.py:209
  89.8 3.9 %collective-permute-start.8 = (bf16[144,1152]{1,0:T(8,128)(2,1)}, bf16[144,1152]{1,0:T(8,128)(2,1)}, u32[]{:S(2)}, u32[]{:S(2)}) collective-permute-start(bf16[144,1152]{1,0:T(8,128)(2,1)} %collective-permute-done.4.rest_4_), channel_id=1, source_target_pairs={{0,48},{48,0},{96,144},{144,96},{192,240},{240,192},{288,336},{336... | collective-permute-start | bytes 995336 | tf_op jit(solution)/shard_map/ppermute | solution.py:209
